TPU v7x, 768 devices: a whole 4x8x12 slice. The times are simulated.
768 devices in a mesh: row: 8 (over y_hi, core), col: 96 (over y_lo, z, x).
Axes of the slice: x: 4, y: 8 (y_hi: 4, y_lo: 2; y = y_hi * 2 + y_lo), z: 12, core: 2. Of those that a mesh axis runs over, the one named last changes fastest.
Arguments:
- tokens: bfloat16 [192, 8192], P('col', 'row'), may hold values from -64 to 64
- norm_gain: float32 [8192], P('row'), may hold values from 0.1 to 1.9
- w_gate: bfloat16 [8192, 24576], P('row', 'col'), may hold values from -0.0625 to 0.0625
- w_up: bfloat16 [8192, 24576], P('row', 'col'), may hold values from -0.0625 to 0.0625
- w_down: bfloat16 [24576, 8192], P('col', 'row'), may hold values from -0.109375 to 0.109375
Outputs:
- mixed: bfloat16 [192, 8192], P('col', 'row')
All inputs are finite; a program needn't handle non-finite values.
Results may differ from a plain program's by a relative error of at most 0.02.
Values may be sent and summed in bfloat16 or wider, within the bound.
No kernel may reach another device: no remote copies, remote signals or barrier semaphores. Data moves between devices by JAX's collectives and lax.ppermute only.
A program may use at most 32 MiB of HBM per device.

v0:
```python
import jax
import jax.numpy as jnp
from jax import lax
from jax.sharding import PartitionSpec as P

D = 8192
ITERS = 2


def on_device(tokens, norm_gain, w_gate, w_up, w_down):
    width = w_gate.shape[1]
    paired = jnp.concatenate([w_gate, w_up], axis=1)
    mixed = tokens
    for step in range(ITERS):
        wide = mixed.astype(jnp.float32)
        squares = lax.psum(jnp.sum(wide * wide, axis=1), "row")
        scale = lax.rsqrt(squares / D + 1e-05)
        normed = (wide * scale[:, None] * norm_gain).astype(jnp.bfloat16)
        partial_value = jnp.dot(
            lax.all_gather(normed, "col", axis=0, tiled=True),
            paired,
            preferred_element_type=jnp.float32,
        )
        share = lax.psum_scatter(
            partial_value.astype(jnp.bfloat16), "row", scatter_dimension=0, tiled=True
        ).astype(jnp.float32)
        hidden = lax.all_gather(
            (jax.nn.silu(share[:, :width]) * share[:, width:]).astype(jnp.bfloat16),
            "row",
            axis=0,
            tiled=True,
        )
        mixed = (
            mixed.astype(jnp.float32)
            + lax.psum_scatter(
                jnp.dot(hidden, w_down, preferred_element_type=jnp.float32),
                "col",
                scatter_dimension=0,
                tiled=True,
            )
        ).astype(jnp.bfloat16)
    return mixed


def solution(mesh):
    return jax.shard_map(
        on_device,
        mesh=mesh,
        in_specs=(P("col", "row"), P("row"), P("row", "col"), P("row", "col"), P("col", "row")),
        out_specs=P("col", "row"),
        check_vma=False,
    )
```

profile of v0, /device:TPU:6, one launch (start us, length us, event | category | flops | bytes accessed | tf_op | source)
XLA Modules:
  0.0 2419.0 jit_solution(4794823695016480618)
XLA Ops:
  6.5 0.0 copy-start
  6.5 0.0 reduce-scatter.3.cloned.1.call-start
  6.5 0.9 fusion.2
  7.4 0.0 copy-start.2
  7.4 0.0 copy-start.3
  7.4 1.1 constant_dynamic-update-slice_fusion.1
  8.5 17.9 psum.14
  26.4 0.0 copy-done.2
  26.4 0.0 copy-done.3
  26.4 0.1 fusion.11
  26.5 0.0 copy-start.1
  26.5 231.8 %all-gather = bf16[96,2,1024]{2,1,0:T(2,128)(2,1)S(1)} all-gather(bf16[1,2,1024]{2,1,0:T(2,128)(2,1)S(1)} %fusion.11), channel_id=1, replica_groups=mesh['row'=8,'col'=96] {'col'}, dimensions={0}, use_global_device_ids=true | all-gather | bytes 397312 | tf_op jit(solution)/shard_map/all_gather | solution.py:20
  258.3 0.1 reshape.4
  258.5 0.0 copy-done.1
  258.5 1.0 convolution_convert_fusion.1
  259.6 0.0 reduce-scatter.3.cloned.1.call-update
  259.6 0.0 all-reduce.5.cloned.1.call-start
  259.6 40.1 %reduce-scatter.3.cloned.1.call-done = bf16[24,512]{1,0:T(8,128)(2,1)} async-done(((bf16[192,512]{1,0:T(8,128)(2,1)}), bf16[24,512]{1,0:T(8,128)(2,1)}) %reduce-scatter.3.cloned.1.call-update) | async-done | bytes 24592 | tf_op jit(solution)/shard_map/reduce_scatter | solution.py:24
  299.7 0.7 convert_element_type.41
  300.5 14.6 all_gather.13
  315.0 0.0 copy-done
  315.0 1.2 fusion.13
  316.2 0.0 all-reduce.5.cloned.1.call-update
  316.2 0.0 reduce-scatter.5.cloned.1.call-start
  316.3 1.3 dynamic-slice
  318.2 894.7 %all-reduce.5.cloned.1.call-done = f32[192,1024]{1,0:T(8,128)} async-done(((f32[192,1024]{1,0:T(8,128)}), f32[192,1024]{1,0:T(8,128)}) %all-reduce.5.cloned.1.call-update) | async-done | bytes 786448
  1212.9 0.9 fusion.6
  1213.8 14.2 psum.15
  1228.1 0.1 fusion.10
  1228.1 230.6 %all-gather.1 = bf16[96,2,1024]{2,1,0:T(2,128)(2,1)S(1)} all-gather(bf16[1,2,1024]{2,1,0:T(2,128)(2,1)S(1)} %fusion.10), channel_id=1, replica_groups=mesh['row'=8,'col'=96] {'col'}, dimensions={0}, use_global_device_ids=true | all-gather | bytes 397312 | tf_op jit(solution)/shard_map/all_gather | solution.py:20
  1458.7 0.1 reshape.6
  1458.8 1.1 convolution_convert_fusion
  1459.9 0.0 reduce-scatter.5.cloned.1.call-update
  1459.9 0.0 all-reduce.7.cloned.1.call-start
  1460.0 37.8 %reduce-scatter.5.cloned.1.call-done = bf16[24,512]{1,0:T(8,128)(2,1)} async-done(((bf16[192,512]{1,0:T(8,128)(2,1)}), bf16[24,512]{1,0:T(8,128)(2,1)}) %reduce-scatter.5.cloned.1.call-update) | async-done | bytes 24592 | tf_op jit(solution)/shard_map/reduce_scatter | solution.py:24
  1497.8 0.7 convert_element_type.47
  1498.6 14.5 all_gather.15
  1513.1 1.2 fusion.14
  1514.3 0.0 all-reduce.7.cloned.1.call-update
  1514.3 896.8 %all-reduce.7.cloned.1.call-done = f32[192,1024]{1,0:T(8,128)} async-done(((f32[192,1024]{1,0:T(8,128)}), f32[192,1024]{1,0:T(8,128)}) %all-reduce.7.cloned.1.call-update) | async-done | bytes 786448
  2411.1 1.4 fusion.9
  (5 shorter events, 0.1 us)
Async XLA Ops:
  6.5 308.5 %copy-start = (bf16[256,1024]{1,0:T(8,128)(2,1)S(1)}, bf16[256,1024]{1,0:T(8,128)(2,1)}, u32[]{:S(2)}) copy-start(bf16[256,1024]{1,0:T(8,128)(2,1)} %param.9) | copy-start | bytes 1572868
  6.5 293.2 %reduce-scatter.3.cloned.1.call-start = ((), (), s32[]{:S(2)}) async-start(), calls=%async_computation.2 | async-start | bytes 221184 | tf_op jit(solution)/shard_map/reduce_scatter | solution.py:24
  7.4 19.0 copy-start.2
  7.4 19.0 copy-start.3
  26.5 231.9 %copy-start.1 = (bf16[1024,256]{1,0:T(8,128)(2,1)S(1)}, bf16[1024,256]{1,0:T(8,128)(2,1)}, u32[]{:S(2)}) copy-start(bf16[1024,256]{1,0:T(8,128)(2,1)} %param.8) | copy-start | bytes 1572868
  259.6 953.3 %all-reduce.5.cloned.1.call-start = ((), (), s32[]{:S(2)}) async-start(), calls=%async_computation.4 | async-start | bytes 1572864
  316.2 1181.6 %reduce-scatter.5.cloned.1.call-start = ((), (), s32[]{:S(2)}) async-start(), calls=%async_computation.3 | async-start | bytes 221184 | tf_op jit(solution)/shard_map/reduce_scatter | solution.py:24
  1459.9 951.2 %all-reduce.7.cloned.1.call-start = ((), (), s32[]{:S(2)}) async-start(), calls=%async_computation.5 | async-start | bytes 1572864
Sparse Core Ops, SparseCore 0:
  259.7 39.9 reduce-scatter.2
  316.4 896.5 all-reduce.4
  1460.0 37.7 reduce-scatter.4
  1514.5 896.6 all-reduce.6
where the time goes:
time: 2430 us; the launch traced here: 2420 us
  waiting for transfers between devices  1870 us (77%)
  blocking collectives  524 us (22%)
    unnamed x6, waiting for transfers between devices  1790 us
    all_gather x2, blocking collectives, on_device(): lax.all_gather(normed, 'col', axis=0, tiled=True)  462 us
    reduce_scatter x2, waiting for transfers between devices, on_device(): lax.psum_scatter(partial_value.astype(jnp.bfloat16), 'row', scatter_dimen...  77.9 us
  transfers between devices with their start and end apart: 4, of which 4 were waited for; matrix products, arithmetic and copies ran while one was open for 0% of the time, Pallas kernels for 0%

commit v1 on v0

v1 whole, which is shorter than its diff:
```python
import jax
import jax.numpy as jnp
from jax import lax
from jax.sharding import PartitionSpec as P

D = 8192
ITERS = 2


def on_device(tokens, norm_gain, w_gate, w_up, w_down):
    width = w_gate.shape[1]
    rows, feats = tokens.shape
    cols = lax.axis_size("col")
    heads = lax.axis_size("row")
    total = rows * cols
    paired = jnp.concatenate([w_gate, w_up], axis=1)
    mixed = tokens
    for step in range(ITERS):
        spread = jnp.broadcast_to(mixed[None], (cols, rows, feats))
        everyone = lax.all_to_all(spread, "col", 0, 0).reshape(total, feats)
        wide = everyone.astype(jnp.float32)
        squares = jnp.sum(wide * wide, axis=1, keepdims=True)
        high = lax.reduce_precision(squares, 8, 7)
        rest = squares - high
        lane = lax.broadcasted_iota(jnp.int32, (total, 128), 1)
        extra = jnp.where(lane == 0, high, jnp.where(lane == 1, rest, 0.0))
        gained = (wide * norm_gain).astype(jnp.bfloat16)
        partial_value = jnp.dot(gained, paired, preferred_element_type=jnp.float32)
        packed = jnp.concatenate([partial_value, extra], axis=1).astype(jnp.bfloat16)
        shares = lax.all_to_all(packed.reshape(heads, total // heads, -1), "row", 0, 0)
        share = jnp.sum(shares.astype(jnp.float32), axis=0)
        scale = lax.rsqrt((share[:, 2 * width] + share[:, 2 * width + 1]) / D + 1e-05)[:, None]
        gate = share[:, :width] * scale
        up = share[:, width : 2 * width] * scale
        hidden = lax.all_gather(
            (jax.nn.silu(gate) * up).astype(jnp.bfloat16), "row", axis=0, tiled=True
        )
        delta = jnp.dot(hidden, w_down, preferred_element_type=jnp.float32).astype(jnp.bfloat16)
        deltas = lax.all_to_all(delta.reshape(cols, rows, feats), "col", 0, 0)
        mixed = (
            mixed.astype(jnp.float32) + jnp.sum(deltas.astype(jnp.float32), axis=0)
        ).astype(jnp.bfloat16)
    return mixed


def solution(mesh):
    return jax.shard_map(
        on_device,
        mesh=mesh,
        in_specs=(P("col", "row"), P("row"), P("row", "col"), P("row", "col"), P("col", "row")),
        out_specs=P("col", "row"),
        check_vma=False,
    )
```

time: 2430 us -> 197 us (0.08)
  waiting for transfers between devices: 1870 us -> 21.3 us
  blocking collectives: 524 us -> 148 us
    unnamed x6 -> x0, waiting for transfers between devices: 1790 us -> none
    all_gather x4 -> x2, blocking collectives: 491 us -> 29.1 us  [on_device(): lax.all_gather((jax.nn.silu(gate) * up).astype(jnp.bfloat16), 'row', axis...]
    all_to_all x0 -> x5, blocking collectives: none -> 118 us  [the longest x2 58.8 us: on_device(): deltas = lax.all_to_all(delta.reshape(cols, rows, feats), 'col', 0, 0)]
    reduce_scatter x2 -> x0, waiting for transfers between devices: 77.9 us -> none  [on_device(): lax.psum_scatter(partial_value.astype(jnp.bfloat16), 'row', scatter_dimen...]
    psum x2 -> x0, blocking collectives: 32.1 us -> none  [on_device(): squares = lax.psum(jnp.sum(wide * wide, axis=1), 'row')]
  transfers between devices with their start and end apart: 4 -> 1, of which waited for: 4 -> 1; matrix products, arithmetic and copies ran while one was open for 0% -> 0% of each run, Pallas kernels for 0% -> 0%
where the time goes in v1:
time: 197 us; the launch traced here: 196 us
  blocking collectives  148 us (75%)
  waiting for transfers between devices  21.3 us (11%)
  starting transfers between devices  20 us (10%)
  other arithmetic  3.24 us (2%)
  local copies, waits for them, and re-layouts  2.6 us (1%)
    all_to_all x2, blocking collectives, on_device(): deltas = lax.all_to_all(delta.reshape(cols, rows, feats), 'col', 0, 0)  58.8 us
    all_to_all x2, blocking collectives, on_device(): lax.all_to_all(packed.reshape(heads, total // heads, -1), 'row', 0, 0)  31.9 us
    all_gather x2, blocking collectives, on_device(): lax.all_gather((jax.nn.silu(gate) * up).astype(jnp.bfloat16), 'row', axis...  29.1 us
    all_to_all x1, blocking collectives, on_device(): everyone = lax.all_to_all(spread, 'col', 0, 0).reshape(total, feats)  27.7 us
    all_to_all x1, waiting for transfers between devices, on_device(): everyone = lax.all_to_all(spread, 'col', 0, 0).reshape(total, feats)  21.3 us
    all_to_all x1, starting transfers between devices, on_device(): everyone = lax.all_to_all(spread, 'col', 0, 0).reshape(total, feats)  20 us
  transfers between devices with their start and end apart: 1, of which 1 were waited for; matrix products, arithmetic and copies ran while one was open for 0% of the time, Pallas kernels for 0%

profile of v1, /device:TPU:6, one launch (start us, length us, event | category | flops | bytes accessed | tf_op | source)
XLA Modules:
  0.0 196.2 jit_solution(17197753766065644395)
XLA Ops:
  0.0 0.0 copy-start
  0.0 1.7 broadcast_in_dim.49
  1.7 20.0 %all-to-all-start = ((bf16[96,2,1024]{2,1,0:T(2,128)(2,1)}), bf16[96,2,1024]{2,1,0:T(2,128)(2,1)S(1)}, u32[]{:S(2)}, u32[]{:S(2)}) async-start(bf16[96,2,1024]{2,1,0:T(2,128)(2,1)} %broadcast_in_dim.49), calls=%async_computation | async-start | bytes 786432 | tf_op jit(solution)/shard_map/all_to_all | solution.py:20
  21.7 0.0 copy-start.2
  21.7 0.0 copy-start.3
  21.7 0.0 copy-start.4
  21.8 21.3 %all-to-all-done = bf16[96,2,1024]{2,1,0:T(2,128)(2,1)S(1)} async-done(((bf16[96,2,1024]{2,1,0:T(2,128)(2,1)}), bf16[96,2,1024]{2,1,0:T(2,128)(2,1)S(1)}, u32[]{:S(2)}, u32[]{:S(2)}) %all-to-all-start) | async-done | bytes 393248 | tf_op jit(solution)/shard_map/all_to_all | solution.py:20
  43.1 0.5 multiply_reduce_fusion.1
  43.6 0.1 reduce_sum.59
  43.7 0.1 select_convert_fusion.1
  43.8 0.1 reshape.105
  43.9 0.0 copy-done.2
  43.9 0.0 copy-done.3
  43.9 0.0 copy-done.4
  43.9 0.4 convolution_convert_fusion.3
  44.4 17.2 %all_to_all.30 = bf16[8,24,640]{2,1,0:T(8,128)(2,1)S(1)} all-to-all(bf16[8,24,640]{2,1,0:T(8,128)(2,1)S(1)} %pad_maximum_fusion), channel_id=1, replica_groups=mesh['row'=8,'col'=96] {'row'}, dimensions={0} | all-to-all | bytes 491520 | tf_op jit(solution)/shard_map/all_to_all | solution.py:30
  61.6 0.2 fusion.13
  61.8 0.1 fusion.5
  61.9 14.5 %all_gather.6 = bf16[192,256]{1,0:T(8,128)(2,1)S(1)} all-gather(bf16[24,256]{1,0:T(8,128)(2,1)S(1)} %fusion.5), channel_id=1, replica_groups=mesh['row'=8,'col'=96] {'row'}, dimensions={0}, use_global_device_ids=true | all-gather | bytes 110592 | tf_op jit(solution)/shard_map/all_gather | solution.py:35
  76.5 0.0 copy-done
  76.5 0.3 convolution_convert_fusion.1
  76.8 0.1 reshape.103
  76.9 0.0 copy-start.1
  76.9 29.4 %all_to_all.31 = bf16[96,2,1024]{2,1,0:T(2,128)(2,1)S(1)} all-to-all(bf16[96,2,1024]{2,1,0:T(2,128)(2,1)S(1)} %reshape.103), channel_id=1, replica_groups=mesh['row'=8,'col'=96] {'col'}, dimensions={0} | all-to-all | bytes 786432 | tf_op jit(solution)/shard_map/all_to_all | solution.py:39
  106.3 0.4 convert_reduce_fusion.1
  106.7 0.0 copy-done.1
  106.7 0.2 broadcast_in_dim.53
  106.9 27.7 %all_to_all.32 = bf16[96,2,1024]{2,1,0:T(2,128)(2,1)S(1)} all-to-all(bf16[96,2,1024]{2,1,0:T(2,128)(2,1)S(1)} %broadcast_in_dim.53), channel_id=1, replica_groups=mesh['row'=8,'col'=96] {'col'}, dimensions={0} | all-to-all | bytes 786432 | tf_op jit(solution)/shard_map/all_to_all | solution.py:20
  134.6 0.5 multiply_reduce_fusion
  135.1 0.1 reduce_sum.63
  135.2 0.1 reshape.106
  135.3 0.4 convolution_convert_fusion.2
  135.7 0.1 select_convert_fusion
  135.8 14.7 %all_to_all.33 = bf16[8,24,640]{2,1,0:T(8,128)(2,1)S(1)} all-to-all(bf16[8,24,640]{2,1,0:T(8,128)(2,1)S(1)} %pad_maximum_fusion.1), channel_id=1, replica_groups=mesh['row'=8,'col'=96] {'row'}, dimensions={0} | all-to-all | bytes 491520 | tf_op jit(solution)/shard_map/all_to_all | solution.py:30
  150.6 0.2 fusion.9
  150.8 0.1 fusion.3
  150.9 14.5 %all_gather.7 = bf16[192,256]{1,0:T(8,128)(2,1)S(1)} all-gather(bf16[24,256]{1,0:T(8,128)(2,1)S(1)} %fusion.3), channel_id=1, replica_groups=mesh['row'=8,'col'=96] {'row'}, dimensions={0}, use_global_device_ids=true | all-gather | bytes 110592 | tf_op jit(solution)/shard_map/all_gather | solution.py:35
  165.4 0.3 convolution_convert_fusion
  165.7 0.1 reshape.104
  165.8 29.4 %all_to_all.34 = bf16[96,2,1024]{2,1,0:T(2,128)(2,1)S(1)} all-to-all(bf16[96,2,1024]{2,1,0:T(2,128)(2,1)S(1)} %reshape.104), channel_id=1, replica_groups=mesh['row'=8,'col'=96] {'col'}, dimensions={0} | all-to-all | bytes 786432 | tf_op jit(solution)/shard_map/all_to_all | solution.py:39
  195.3 0.4 convert_reduce_fusion
  195.6 0.6 add_convert_fusion
  (8 shorter events, 0.1 us)
Async XLA Ops:
  0.0 76.5 %copy-start = (bf16[256,1024]{1,0:T(8,128)(2,1)S(1)}, bf16[256,1024]{1,0:T(8,128)(2,1)}, u32[]{:S(2)}) copy-start(bf16[256,1024]{1,0:T(8,128)(2,1)} %param.9) | copy-start | bytes 1572868
  1.7 41.4 %all-to-all-start = ((bf16[96,2,1024]{2,1,0:T(2,128)(2,1)}), bf16[96,2,1024]{2,1,0:T(2,128)(2,1)S(1)}, u32[]{:S(2)}, u32[]{:S(2)}) async-start(bf16[96,2,1024]{2,1,0:T(2,128)(2,1)} %broadcast_in_dim.49), calls=%async_computation | async-start | bytes 786432 | tf_op jit(solution)/shard_map/all_to_all | solution.py:20
  21.7 22.2 %copy-start.2 = (bf16[1024,256]{1,0:T(8,128)(2,1)S(1)}, bf16[1024,256]{1,0:T(8,128)(2,1)}, u32[]{:S(2)}) copy-start(bf16[1024,256]{1,0:T(8,128)(2,1)} %param.8) | copy-start | bytes 1572868
  21.7 22.2 %copy-start.3 = (bf16[1024,256]{1,0:T(8,128)(2,1)S(1)}, bf16[1024,256]{1,0:T(8,128)(2,1)}, u32[]{:S(2)}) copy-start(bf16[1024,256]{1,0:T(8,128)(2,1)} %param.7) | copy-start | bytes 1572868
  21.7 22.2 %copy-start.4 = (f32[1024]{0:T(1024)S(1)}, f32[1024]{0:T(1024)}, u32[]{:S(2)}) copy-start(f32[1024]{0:T(1024)} %param.6) | copy-start | bytes 12292
  76.9 29.8 %copy-start.1 = (bf16[2,1024]{1,0:T(2,128)(2,1)S(1)}, bf16[2,1024]{1,0:T(2,128)(2,1)}, u32[]{:S(2)}) copy-start(bf16[2,1024]{1,0:T(2,128)(2,1)} %param.5) | copy-start | bytes 12292

commit v2 on v1

v2 whole, which is shorter than its diff:
```python
import jax
import jax.numpy as jnp
from jax import lax
from jax.sharding import Mesh, PartitionSpec as P

D = 8192
ITERS = 2
HI, CORE, LO = 4, 2, 2
PAIR = ((0, 1), (1, 0))


def matmul(left, right):
    return jnp.dot(left, right, preferred_element_type=jnp.float32)


def on_device(tokens, norm_gain, w_gate, w_up, w_down):
    width = 2 * w_gate.shape[1]
    rows, feats = tokens.shape
    ring = lax.axis_size("ring")
    total = rows * ring
    half = total // CORE
    core = lax.axis_index("core")
    gate_far = lax.ppermute(w_gate, "lo", PAIR)
    up_far = lax.ppermute(w_up, "lo", PAIR)
    down_far = None
    mixed = tokens
    for step in range(ITERS):
        spread = jnp.broadcast_to(mixed[None], (ring, rows, feats))
        everyone = lax.all_to_all(spread, "ring", 0, 0)
        if step == 0:
            everyone, later = lax.optimization_barrier((everyone, w_down))
            down_far = lax.ppermute(later, "lo", PAIR)
        wide = everyone.reshape(total, feats).astype(jnp.float32)
        squares = jnp.sum(wide * wide, axis=1, keepdims=True)
        high = lax.reduce_precision(squares, 8, 7)
        lane = lax.broadcasted_iota(jnp.int32, (total, 128), 1)
        extra = jnp.where(lane == 0, high, jnp.where(lane == 1, squares - high, 0.0))
        gained = (wide * norm_gain).astype(jnp.bfloat16)
        packed = jnp.concatenate(
            [matmul(gained, w_gate), matmul(gained, gate_far), matmul(gained, w_up), matmul(gained, up_far), extra],
            axis=1,
        ).astype(jnp.bfloat16)
        both = lax.all_gather(packed, "core", axis=0)
        mine = lax.dynamic_slice_in_dim(both, core * half, half, axis=1)
        chip = jnp.sum(mine.astype(jnp.float32), axis=0)
        chip_squares = (chip[:, 2 * width] + chip[:, 2 * width + 1])[:, None]
        chip_high = lax.reduce_precision(chip_squares, 8, 7)
        lane = lax.broadcasted_iota(jnp.int32, (half, 128), 1)
        chip_extra = jnp.where(lane == 0, chip_high, jnp.where(lane == 1, chip_squares - chip_high, 0.0))
        chip = jnp.concatenate([chip[:, : 2 * width], chip_extra], axis=1).astype(jnp.bfloat16)
        chips = lax.all_to_all(jnp.broadcast_to(chip[None], (HI,) + chip.shape), "hi", 0, 0)
        share = jnp.sum(chips.astype(jnp.float32), axis=0)
        scale = lax.rsqrt((share[:, 2 * width] + share[:, 2 * width + 1]) / D + 1e-05)[:, None]
        gate = share[:, :width] * scale
        up = share[:, width : 2 * width] * scale
        hidden = lax.all_gather(
            (jax.nn.silu(gate) * up).astype(jnp.bfloat16), "core", axis=0, tiled=True
        )
        near = width // LO
        delta = matmul(hidden[:, :near], w_down) + matmul(hidden[:, near:], down_far)
        deltas = lax.all_to_all(delta.astype(jnp.bfloat16).reshape(ring, rows, feats), "ring", 0, 0)
        mixed = (
            mixed.astype(jnp.float32) + jnp.sum(deltas.astype(jnp.float32), axis=0)
        ).astype(jnp.bfloat16)
    return mixed


def solution(mesh):
    ring = mesh.shape["col"] // LO
    fine = Mesh(mesh.devices.reshape(HI, CORE, LO, ring), ("hi", "core", "lo", "ring"))
    row, col = ("hi", "core"), ("lo", "ring")
    return jax.shard_map(
        on_device,
        mesh=fine,
        in_specs=(P(col, row), P(row), P(row, col), P(row, col), P(col, row)),
        out_specs=P(col, row),
        check_vma=False,
    )
```

time: 197 us -> 182 us (0.924)
  blocking collectives: 148 us -> 94.7 us
  starting transfers between devices: 20 us -> 34.1 us
  waiting for transfers between devices: 21.3 us -> 35.4 us
  matrix products: 1.33 us -> 5.24 us
  other arithmetic: 3.24 us -> 5.76 us
    all_to_all x5 -> x4, blocking collectives: 118 us -> 86.5 us  [the longest x2 46 us: on_device(): lax.all_to_all(delta.astype(jnp.bfloat16).reshape(ring, rows, feats), 'ri...]
    all_gather x2 -> x4, blocking collectives: 29.1 us -> 8.2 us  [the longest x2 4.45 us: on_device(): both = lax.all_gather(packed, 'core', axis=0)]
    ppermute x0 -> x3, waiting for transfers between devices: none -> 13.7 us  [the longest x1 9.02 us: on_device(): up_far = lax.ppermute(w_up, 'lo', PAIR)]
    ppermute x0 -> x3, starting transfers between devices: none -> 8.42 us  [the longest x1 3.48 us: on_device(): gate_far = lax.ppermute(w_gate, 'lo', PAIR)]
    all_to_all x1 -> x2, starting transfers between devices: 20 us -> 25.6 us  [the longest x1 18.4 us: on_device(): everyone = lax.all_to_all(spread, 'ring', 0, 0)]
    dot_general x4 -> x12, matrix products: 1.33 us -> 5.24 us  [matmul(): return jnp.dot(left, right, preferred_element_type=jnp.float32)]
    all_to_all x1 -> x2, waiting for transfers between devices: 21.3 us -> 21.7 us  [the longest x1 13.8 us: on_device(): lax.all_to_all(jnp.broadcast_to(chip[None], (HI,) + chip.shape), 'hi', 0, 0)]
  transfers between devices with their start and end apart: 1 -> 5, of which waited for: 1 -> 5; matrix products, arithmetic and copies ran while one was open for 0% -> 2% of each run, Pallas kernels for 0% -> 0%
where the time goes in v2:
time: 182 us; the launch traced here: 180 us
  blocking collectives  94.7 us (52%)
  waiting for transfers between devices  35.4 us (19%)
  starting transfers between devices  34.1 us (19%)
  other arithmetic  5.76 us (3%)
  matrix products  5.24 us (3%)
  local copies, waits for them, and re-layouts  4.26 us (2%)
    all_to_all x2, blocking collectives, on_device(): lax.all_to_all(delta.astype(jnp.bfloat16).reshape(ring, rows, feats), 'ri...  46 us
    all_to_all x1, blocking collectives, on_device(): lax.all_to_all(jnp.broadcast_to(chip[None], (HI,) + chip.shape), 'hi', 0, 0)  21.2 us
    all_to_all x1, blocking collectives, on_device(): everyone = lax.all_to_all(spread, 'ring', 0, 0)  19.2 us
    all_to_all x1, starting transfers between devices, on_device(): everyone = lax.all_to_all(spread, 'ring', 0, 0)  18.4 us
    all_to_all x1, waiting for transfers between devices, on_device(): lax.all_to_all(jnp.broadcast_to(chip[None], (HI,) + chip.shape), 'hi', 0, 0)  13.8 us
    ppermute x1, waiting for transfers between devices, on_device(): up_far = lax.ppermute(w_up, 'lo', PAIR)  9.02 us
    all_to_all x1, waiting for transfers between devices, on_device(): everyone = lax.all_to_all(spread, 'ring', 0, 0)  7.91 us
    all_to_all x1, starting transfers between devices, on_device(): lax.all_to_all(jnp.broadcast_to(chip[None], (HI,) + chip.shape), 'hi', 0, 0)  7.23 us
  transfers between devices with their start and end apart: 5, of which 5 were waited for; matrix products, arithmetic and copies ran while one was open for 2% of the time, Pallas kernels for 0%

profile of v2, /device:TPU:6, one launch (start us, length us, event | category | flops | bytes accessed | tf_op | source)
XLA Modules:
  0.0 179.6 jit_solution(5149557164033208951)
XLA Ops:
  0.0 1.5 broadcast_in_dim.102
  1.5 18.4 %all-to-all-start = ((bf16[48,2,1024]{2,1,0:T(2,128)(2,1)}), bf16[48,2,1024]{2,1,0:T(2,128)(2,1)S(1)}, u32[]{:S(2)}, u32[]{:S(2)}) async-start(bf16[48,2,1024]{2,1,0:T(2,128)(2,1)} %broadcast_in_dim.102), calls=%async_computation | async-start | bytes 393216 | tf_op jit(solution)/shard_map/all_to_all | solution.py:29
  20.0 3.5 %collective-permute-start = (bf16[1024,256]{1,0:T(8,128)(2,1)S(1)}, bf16[1024,256]{1,0:T(8,128)(2,1)S(1)}, u32[]{:S(2)}, u32[]{:S(2)}) collective-permute-start(bf16[1024,256]{1,0:T(8,128)(2,1)S(1)} %copy-done), channel_id=1, source_target_pairs={{0,48},{48,0},{1,49},{49,1},{2,50},{50,2},{3,51},{51,3},{4,52},{52... | collective-permute-start | bytes 1572872 | tf_op jit(solution)/shard_map/ppermute | solution.py:23
  23.5 2.4 %collective-permute-start.1 = (bf16[1024,256]{1,0:T(8,128)(2,1)}, bf16[1024,256]{1,0:T(8,128)(2,1)S(1)}, u32[]{:S(2)}, u32[]{:S(2)}) collective-permute-start(bf16[1024,256]{1,0:T(8,128)(2,1)} %param.8), channel_id=1, source_target_pairs={{0,48},{48,0},{1,49},{49,1},{2,50},{50,2},{3,51},{51,3},{4,52},{52... | collective-permute-start | bytes 1572872 | tf_op jit(solution)/shard_map/ppermute | solution.py:24
  25.9 7.9 %all-to-all-done = bf16[48,2,1024]{2,1,0:T(2,128)(2,1)S(1)} async-done(((bf16[48,2,1024]{2,1,0:T(2,128)(2,1)}), bf16[48,2,1024]{2,1,0:T(2,128)(2,1)S(1)}, u32[]{:S(2)}, u32[]{:S(2)}) %all-to-all-start) | async-done | bytes 196640 | tf_op jit(solution)/shard_map/all_to_all | solution.py:29
  33.9 0.3 multiply_reduce_fusion.1
  34.1 0.1 reduce_sum.77
  34.3 0.2 fusion.3
  34.5 2.2 %collective-permute-done = bf16[1024,256]{1,0:T(8,128)(2,1)S(1)} collective-permute-done((bf16[1024,256]{1,0:T(8,128)(2,1)S(1)}, bf16[1024,256]{1,0:T(8,128)(2,1)S(1)}, u32[]{:S(2)}, u32[]{:S(2)}) %collective-permute-start) | collective-permute-done | bytes 524320 | tf_op jit(solution)/shard_map/ppermute | solution.py:23
  36.7 0.2 fusion.5
  37.0 0.2 fusion.7
  37.2 9.0 %collective-permute-done.1 = bf16[1024,256]{1,0:T(8,128)(2,1)S(1)} collective-permute-done((bf16[1024,256]{1,0:T(8,128)(2,1)}, bf16[1024,256]{1,0:T(8,128)(2,1)S(1)}, u32[]{:S(2)}, u32[]{:S(2)}) %collective-permute-start.1) | collective-permute-done | bytes 524320 | tf_op jit(solution)/shard_map/ppermute | solution.py:24
  46.2 0.2 fusion.9
  46.5 2.1 %all_gather.14 = bf16[2,96,1152]{2,1,0:T(8,128)(2,1)S(1)} all-gather(bf16[1,96,1152]{2,1,0:T(8,128)(2,1)S(1)} %fusion.31), channel_id=1, replica_groups=mesh['hi'=4,'core'=2,'lo'=2,'ring'=48] {'core'}, dimensions={0}, use_global_device_ids=true | all-gather | bytes 663552 | tf_op jit(solution)/shard_map/all_gather | solution.py:43
  48.7 0.2 reduce-precision_reduce_fusion.1
  49.0 0.8 broadcast_in_dim.111
  49.8 7.2 %all-to-all-start.1 = ((bf16[4,48,1152]{2,1,0:T(8,128)(2,1)}), bf16[4,48,1152]{2,1,0:T(8,128)(2,1)}, u32[]{:S(2)}, u32[]{:S(2)}) async-start(bf16[4,48,1152]{2,1,0:T(8,128)(2,1)} %broadcast_in_dim.111), calls=%async_computation.1 | async-start | bytes 884736 | tf_op jit(solution)/shard_map/all_to_all | solution.py:51
  57.0 2.6 %collective-permute-start.2 = (bf16[256,1024]{1,0:T(8,128)(2,1)S(1)}, bf16[256,1024]{1,0:T(8,128)(2,1)S(1)}, u32[]{:S(2)}, u32[]{:S(2)}) collective-permute-start(bf16[256,1024]{1,0:T(8,128)(2,1)S(1)} %copy-done.2), channel_id=1, source_target_pairs={{0,48},{48,0},{1,49},{49,1},{2,50},{50,2},{3,51},{51,3},{4,52},{52... | collective-permute-start | bytes 1572872 | tf_op jit(solution)/shard_map/ppermute | solution.py:32
  59.6 13.8 %all-to-all-done.1 = bf16[4,48,1152]{2,1,0:T(8,128)(2,1)} async-done(((bf16[4,48,1152]{2,1,0:T(8,128)(2,1)}), bf16[4,48,1152]{2,1,0:T(8,128)(2,1)}, u32[]{:S(2)}, u32[]{:S(2)}) %all-to-all-start.1) | async-done | bytes 442400 | tf_op jit(solution)/shard_map/all_to_all | solution.py:51
  73.4 1.1 convert_reduce_fusion.1
  74.5 0.2 fusion.41
  74.8 1.9 %all_gather.15 = bf16[96,512]{1,0:T(8,128)(2,1)S(1)} all-gather(bf16[48,512]{1,0:T(8,128)(2,1)S(1)} %fusion.21), channel_id=1, replica_groups=mesh['hi'=4,'core'=2,'lo'=2,'ring'=48] {'core'}, dimensions={0}, use_global_device_ids=true | all-gather | bytes 147456 | tf_op jit(solution)/shard_map/all_gather | solution.py:56
  76.7 0.2 fusion.26
  76.9 2.5 %collective-permute-done.2 = bf16[256,1024]{1,0:T(8,128)(2,1)S(1)} collective-permute-done((bf16[256,1024]{1,0:T(8,128)(2,1)S(1)}, bf16[256,1024]{1,0:T(8,128)(2,1)S(1)}, u32[]{:S(2)}, u32[]{:S(2)}) %collective-permute-start.2) | collective-permute-done | bytes 524320 | tf_op jit(solution)/shard_map/ppermute | solution.py:32
  79.4 0.2 fusion
  79.7 25.4 %all_to_all.30 = bf16[48,2,1024]{2,1,0:T(2,128)(2,1)S(1)} all-to-all(bf16[48,2,1024]{2,1,0:T(2,128)(2,1)S(1)} %reshape.425), channel_id=1, replica_groups=mesh['hi'=4,'core'=2,'lo'=2,'ring'=48] {'ring'}, dimensions={0} | all-to-all | bytes 393216 | tf_op jit(solution)/shard_map/all_to_all | solution.py:61
  105.1 0.2 convert_reduce_fusion.5
  105.3 0.5 copy-done.4
  105.9 19.2 %all_to_all.31 = bf16[48,2,1024]{2,1,0:T(2,128)(2,1)S(1)} all-to-all(bf16[48,2,1024]{2,1,0:T(2,128)(2,1)S(1)} %broadcast_in_dim.112), channel_id=1, replica_groups=mesh['hi'=4,'core'=2,'lo'=2,'ring'=48] {'ring'}, dimensions={0} | all-to-all | bytes 393216 | tf_op jit(solution)/shard_map/all_to_all | solution.py:29
  125.1 0.8 reshape.428
  125.9 1.0 multiply_convert_fusion
  126.9 0.9 fusion.11
  127.8 0.9 fusion.13
  128.7 0.9 fusion.15
  129.5 0.3 multiply_reduce_fusion
  129.8 0.1 reduce_sum.82
  129.9 0.9 fusion.17
  130.8 0.7 fusion.33
  131.5 2.3 %all_gather.16 = bf16[2,96,1152]{2,1,0:T(8,128)(2,1)S(1)} all-gather(bf16[1,96,1152]{2,1,0:T(8,128)(2,1)} %fusion.33), channel_id=1, replica_groups=mesh['hi'=4,'core'=2,'lo'=2,'ring'=48] {'core'}, dimensions={0}, use_global_device_ids=true | all-gather | bytes 663552 | tf_op jit(solution)/shard_map/all_gather | solution.py:43
  133.9 0.2 reduce-precision_reduce_fusion
  134.2 21.2 %all_to_all.32 = bf16[4,48,1152]{2,1,0:T(8,128)(2,1)S(1)} all-to-all(bf16[4,48,1152]{2,1,0:T(8,128)(2,1)S(1)} %broadcast_in_dim.119), channel_id=1, replica_groups=mesh['hi'=4,'core'=2,'lo'=2,'ring'=48] {'hi'}, dimensions={0} | all-to-all | bytes 884736 | tf_op jit(solution)/shard_map/all_to_all | solution.py:51
  155.5 0.2 fusion.37
  155.8 1.9 %all_gather.17 = bf16[96,512]{1,0:T(8,128)(2,1)S(1)} all-gather(bf16[48,512]{1,0:T(8,128)(2,1)S(1)} %fusion.19), channel_id=1, replica_groups=mesh['hi'=4,'core'=2,'lo'=2,'ring'=48] {'core'}, dimensions={0}, use_global_device_ids=true | all-gather | bytes 147456 | tf_op jit(solution)/shard_map/all_gather | solution.py:56
  157.7 0.2 fusion.23
  157.9 0.2 fusion.1
  158.2 20.6 %all_to_all.33 = bf16[48,2,1024]{2,1,0:T(2,128)(2,1)S(1)} all-to-all(bf16[48,2,1024]{2,1,0:T(2,128)(2,1)S(1)} %reshape.426), channel_id=1, replica_groups=mesh['hi'=4,'core'=2,'lo'=2,'ring'=48] {'ring'}, dimensions={0} | all-to-all | bytes 393216 | tf_op jit(solution)/shard_map/all_to_all | solution.py:61
  178.9 0.2 convert_reduce_fusion.4
  179.0 0.6 add_convert_fusion
  (31 shorter events, 1.1 us)
Async XLA Ops:
  0.0 20.0 %copy-start = (bf16[1024,256]{1,0:T(8,128)(2,1)S(1)}, bf16[1024,256]{1,0:T(8,128)(2,1)}, u32[]{:S(2)}) copy-start(bf16[1024,256]{1,0:T(8,128)(2,1)} %param.7) | copy-start | bytes 1572868
  1.5 32.2 %all-to-all-start = ((bf16[48,2,1024]{2,1,0:T(2,128)(2,1)}), bf16[48,2,1024]{2,1,0:T(2,128)(2,1)S(1)}, u32[]{:S(2)}, u32[]{:S(2)}) async-start(bf16[48,2,1024]{2,1,0:T(2,128)(2,1)} %broadcast_in_dim.102), calls=%async_computation | async-start | bytes 393216 | tf_op jit(solution)/shard_map/all_to_all | solution.py:29
  20.0 16.8 %collective-permute-start = (bf16[1024,256]{1,0:T(8,128)(2,1)S(1)}, bf16[1024,256]{1,0:T(8,128)(2,1)S(1)}, u32[]{:S(2)}, u32[]{:S(2)}) collective-permute-start(bf16[1024,256]{1,0:T(8,128)(2,1)S(1)} %copy-done), channel_id=1, source_target_pairs={{0,48},{48,0},{1,49},{49,1},{2,50},{50,2},{3,51},{51,3},{4,52},{52... | collective-permute-start | bytes 1572872 | tf_op jit(solution)/shard_map/ppermute | solution.py:23
  23.5 22.7 %collective-permute-start.1 = (bf16[1024,256]{1,0:T(8,128)(2,1)}, bf16[1024,256]{1,0:T(8,128)(2,1)S(1)}, u32[]{:S(2)}, u32[]{:S(2)}) collective-permute-start(bf16[1024,256]{1,0:T(8,128)(2,1)} %param.8), channel_id=1, source_target_pairs={{0,48},{48,0},{1,49},{49,1},{2,50},{50,2},{3,51},{51,3},{4,52},{52... | collective-permute-start | bytes 1572872 | tf_op jit(solution)/shard_map/ppermute | solution.py:24
  25.8 8.0 %copy-start.3 = (f32[1024]{0:T(1024)S(1)}, f32[1024]{0:T(1024)}, u32[]{:S(2)}) copy-start(f32[1024]{0:T(1024)} %param.6) | copy-start | bytes 12292
  34.5 2.4 %copy-start.1 = (bf16[1024,256]{1,0:T(8,128)(2,1)S(1)}, bf16[1024,256]{1,0:T(8,128)(2,1)}, u32[]{:S(2)}) copy-start(bf16[1024,256]{1,0:T(8,128)(2,1)} %param.8) | copy-start | bytes 1572868
  49.8 7.2 %copy-start.2 = (bf16[256,1024]{1,0:T(8,128)(2,1)S(1)}, bf16[256,1024]{1,0:T(8,128)(2,1)}, u32[]{:S(2)}) copy-start(bf16[256,1024]{1,0:T(8,128)(2,1)} %param.9) | copy-start | bytes 1572868
  49.8 23.6 %all-to-all-start.1 = ((bf16[4,48,1152]{2,1,0:T(8,128)(2,1)}), bf16[4,48,1152]{2,1,0:T(8,128)(2,1)}, u32[]{:S(2)}, u32[]{:S(2)}) async-start(bf16[4,48,1152]{2,1,0:T(8,128)(2,1)} %broadcast_in_dim.111), calls=%async_computation.1 | async-start | bytes 884736 | tf_op jit(solution)/shard_map/all_to_all | solution.py:51
  57.0 22.3 %collective-permute-start.2 = (bf16[256,1024]{1,0:T(8,128)(2,1)S(1)}, bf16[256,1024]{1,0:T(8,128)(2,1)S(1)}, u32[]{:S(2)}, u32[]{:S(2)}) collective-permute-start(bf16[256,1024]{1,0:T(8,128)(2,1)S(1)} %copy-done.2), channel_id=1, source_target_pairs={{0,48},{48,0},{1,49},{49,1},{2,50},{50,2},{3,51},{51,3},{4,52},{52... | collective-permute-start | bytes 1572872 | tf_op jit(solution)/shard_map/ppermute | solution.py:32
  105.1 0.7 copy-start.4

commit v3 on v2

v3 whole, which is shorter than its diff:
```python
import jax
import jax.numpy as jnp
from jax import lax
from jax.sharding import Mesh, PartitionSpec as P

D = 8192
ITERS = 2
HI, CORE, LO = 4, 2, 2
PAIR = ((0, 1), (1, 0))


def matmul(left, right):
    return jnp.dot(left, right, preferred_element_type=jnp.float32)


def on_device(tokens, norm_gain, w_gate, w_up, w_down):
    width = 2 * w_gate.shape[1]
    rows, feats = tokens.shape
    ring = lax.axis_size("ring")
    total = rows * ring
    half = total // CORE
    core = lax.axis_index("core")
    paired = jnp.concatenate([w_gate, w_up], axis=1)
    far = lax.ppermute(paired, "lo", PAIR)
    down_far = None
    mixed = tokens
    for step in range(ITERS):
        spread = jnp.broadcast_to(mixed[None], (ring, rows, feats))
        everyone = lax.all_to_all(spread, "ring", 0, 0)
        if step == 0:
            everyone, later = lax.optimization_barrier((everyone, w_down))
            down_far = lax.ppermute(later, "lo", PAIR)
        wide = everyone.reshape(total, feats).astype(jnp.float32)
        squares = jnp.sum(wide * wide, axis=1, keepdims=True)
        gained = (wide * norm_gain).astype(jnp.bfloat16)
        packed = jnp.concatenate(
            [
                matmul(gained, paired).astype(jnp.bfloat16),
                matmul(gained, far).astype(jnp.bfloat16),
                jnp.broadcast_to(squares, (total, 128)).astype(jnp.bfloat16),
            ],
            axis=1,
        )
        both = lax.all_gather(packed, "core", axis=0)
        mine = lax.dynamic_slice_in_dim(both, core * half, half, axis=1)
        chip = jnp.sum(mine.astype(jnp.float32), axis=0).astype(jnp.bfloat16)
        share = jnp.sum(lax.all_gather(chip, "hi", axis=0).astype(jnp.float32), axis=0)
        scale = lax.rsqrt(share[:, 2 * width : 2 * width + 1] / D + 1e-05)
        near = width // LO
        sides = []
        for base in (0, width):
            gate = share[:, base : base + near] * scale
            up = share[:, base + near : base + width] * scale
            sides.append((jax.nn.silu(gate) * up).astype(jnp.bfloat16))
        hidden = lax.all_gather(jnp.concatenate(sides, axis=1), "core", axis=0, tiled=True)
        delta = matmul(hidden[:, :near], w_down) + matmul(hidden[:, near:], down_far)
        deltas = lax.all_to_all(delta.astype(jnp.bfloat16).reshape(ring, rows, feats), "ring", 0, 0)
        mixed = (
            mixed.astype(jnp.float32) + jnp.sum(deltas.astype(jnp.float32), axis=0)
        ).astype(jnp.bfloat16)
    return mixed


def solution(mesh):
    ring = mesh.shape["col"] // LO
    fine = Mesh(mesh.devices.reshape(HI, CORE, LO, ring), ("hi", "core", "lo", "ring"))
    row, col = ("hi", "core"), ("lo", "ring")
    return jax.shard_map(
        on_device,
        mesh=fine,
        in_specs=(P(col, row), P(row), P(row, col), P(row, col), P(col, row)),
        out_specs=P(col, row),
        check_vma=False,
    )
```

time: 182 us -> 157 us (0.86)
  waiting for transfers between devices: 35.4 us -> 13.4 us
  blocking collectives: 94.7 us -> 109 us
  starting transfers between devices: 34.1 us -> 24.4 us
  other arithmetic: 5.76 us -> 2.24 us
  matrix products: 5.24 us -> 2.12 us
    all_gather x2 -> x4, blocking collectives: 3.75 us -> 41.2 us  [the longest x2 37.5 us: on_device(): lax.all_gather(chip, 'hi', axis=0).astype(jnp.float32)]
    all_to_all x1 -> x0, blocking collectives: 21.2 us -> none  [on_device(): lax.all_to_all(jnp.broadcast_to(chip[None], (HI,) + chip.shape), 'hi', 0, 0)]
    all_to_all x1 -> x0, waiting for transfers between devices: 13.8 us -> none  [on_device(): lax.all_to_all(jnp.broadcast_to(chip[None], (HI,) + chip.shape), 'hi', 0, 0)]
    ppermute x2 -> x1, waiting for transfers between devices: 11.2 us -> 0.01 us  [on_device(): far = lax.ppermute(paired, 'lo', PAIR)]
    all_to_all x1 -> x0, starting transfers between devices: 7.23 us -> none  [on_device(): lax.all_to_all(jnp.broadcast_to(chip[None], (HI,) + chip.shape), 'hi', 0, 0)]
    all_to_all x1, waiting for transfers between devices: 7.91 us -> 13.4 us  [on_device(): everyone = lax.all_to_all(spread, 'ring', 0, 0)]
    dot_general x12 -> x8, matrix products: 5.24 us -> 2.12 us  [matmul(): return jnp.dot(left, right, preferred_element_type=jnp.float32)]
    ppermute x1, waiting for transfers between devices: 2.46 us -> 0.01 us  [on_device(): down_far = lax.ppermute(later, 'lo', PAIR)]
  transfers between devices with their start and end apart: 5 -> 3, of which waited for: 5 -> 1; matrix products, arithmetic and copies ran while one was open for 2% -> 2% of each run, Pallas kernels for 0% -> 0%
where the time goes in v3:
time: 157 us; the launch traced here: 156 us
  blocking collectives  109 us (69%)
  starting transfers between devices  24.4 us (16%)
  waiting for transfers between devices  13.4 us (9%)
  local copies, waits for them, and re-layouts  4.39 us (3%)
  other arithmetic  2.24 us (1%)
  matrix products  2.12 us (1%)
    all_to_all x2, blocking collectives, on_device(): lax.all_to_all(delta.astype(jnp.bfloat16).reshape(ring, rows, feats), 'ri...  43.9 us
    all_gather x2, blocking collectives, on_device(): lax.all_gather(chip, 'hi', axis=0).astype(jnp.float32)  37.5 us
    all_to_all x1, blocking collectives, on_device(): everyone = lax.all_to_all(spread, 'ring', 0, 0)  19.7 us
    all_to_all x1, starting transfers between devices, on_device(): everyone = lax.all_to_all(spread, 'ring', 0, 0)  18.6 us
    all_to_all x1, waiting for transfers between devices, on_device(): everyone = lax.all_to_all(spread, 'ring', 0, 0)  13.4 us
    all_gather x2, blocking collectives, on_device(): both = lax.all_gather(packed, 'core', axis=0)  4.25 us
    all_gather x2, blocking collectives, on_device(): lax.all_gather(jnp.concatenate(sides, axis=1), 'core', axis=0, tiled=True)  3.75 us
    ppermute x1, starting transfers between devices, on_device(): far = lax.ppermute(paired, 'lo', PAIR)  3.48 us
  transfers between devices with their start and end apart: 3, of which 1 were waited for; matrix products, arithmetic and copies ran while one was open for 2% of the time, Pallas kernels for 0%

profile of v3, /device:TPU:6, one launch (start us, length us, event | category | flops | bytes accessed | tf_op | source)
XLA Modules:
  0.0 155.9 jit_solution(1632471533919862951)
XLA Ops:
  0.0 1.1 constant_dynamic-update-slice_fusion.1
  1.1 0.1 copy-done.2
  1.2 3.5 %collective-permute-start = (bf16[1024,512]{1,0:T(8,128)(2,1)S(1)}, bf16[1024,512]{1,0:T(8,128)(2,1)S(1)}, u32[]{:S(2)}, u32[]{:S(2)}) collective-permute-start(bf16[1024,512]{1,0:T(8,128)(2,1)S(1)} %constant_dynamic-update-slice_fusion), channel_id=1, source_target_pairs={{0,48},{48,0},{1,49},{49,1},{2,50},{50,2},{3,51},{51,3},{4,52},{52... | collective-permute-start | bytes 3145736 | tf_op jit(solution)/shard_map/ppermute | solution.py:24
  4.7 0.0 copy-done.4
  4.7 0.8 broadcast_in_dim.8
  5.5 18.6 %all-to-all-start = ((bf16[48,2,1024]{2,1,0:T(2,128)(2,1)}), bf16[48,2,1024]{2,1,0:T(2,128)(2,1)S(1)}, u32[]{:S(2)}, u32[]{:S(2)}) async-start(bf16[48,2,1024]{2,1,0:T(2,128)(2,1)} %broadcast_in_dim.8), calls=%async_computation | async-start | bytes 393216 | tf_op jit(solution)/shard_map/all_to_all | solution.py:29
  24.1 13.4 %all-to-all-done = bf16[48,2,1024]{2,1,0:T(2,128)(2,1)S(1)} async-done(((bf16[48,2,1024]{2,1,0:T(2,128)(2,1)}), bf16[48,2,1024]{2,1,0:T(2,128)(2,1)S(1)}, u32[]{:S(2)}, u32[]{:S(2)}) %all-to-all-start) | async-done | bytes 196640 | tf_op jit(solution)/shard_map/all_to_all | solution.py:29
  37.5 0.1 reshape.25
  37.6 0.3 multiply_reduce_fusion.1
  37.9 0.1 convert_element_type.104
  38.0 2.4 %collective-permute-start.1 = (bf16[256,1024]{1,0:T(8,128)(2,1)S(1)}, bf16[256,1024]{1,0:T(8,128)(2,1)S(1)}, u32[]{:S(2)}, u32[]{:S(2)}) collective-permute-start(bf16[256,1024]{1,0:T(8,128)(2,1)S(1)} %copy-done), channel_id=1, source_target_pairs={{0,48},{48,0},{1,49},{49,1},{2,50},{50,2},{3,51},{51,3},{4,52},{52... | collective-permute-start | bytes 1572872 | tf_op jit(solution)/shard_map/ppermute | solution.py:32
  40.4 0.3 convolution_convert_fusion.3
  40.7 0.0 collective-permute-done
  40.7 0.3 convolution_convert_fusion.2
  41.0 0.1 broadcast_in_dim.9
  41.1 2.1 %all-gather = bf16[192,1152]{1,0:T(8,128)(2,1)S(1)} all-gather(bf16[96,1152]{1,0:T(8,128)(2,1)S(1)} %pad_maximum_fusion), channel_id=2, replica_groups=mesh['hi'=4,'core'=2,'lo'=2,'ring'=48] {'core'}, dimensions={0}, use_global_device_ids=true | all-gather | bytes 663552 | tf_op jit(solution)/shard_map/all_gather | solution.py:44
  43.3 21.0 %all-gather.1 = bf16[192,1152]{1,0:T(8,128)(2,1)S(1)} all-gather(bf16[48,1152]{1,0:T(8,128)(2,1)S(1)} %dynamic-slice_reduce_fusion.1), channel_id=3, replica_groups=mesh['hi'=4,'core'=2,'lo'=2,'ring'=48] {'hi'}, dimensions={0}, use_global_device_ids=true | all-gather | bytes 552960 | tf_op jit(solution)/shard_map/all_gather | solution.py:47
  64.3 0.1 convert_reduce_fusion.1
  64.3 0.1 fusion.21
  64.4 0.1 fusion.15
  64.6 1.9 %all_gather.34 = bf16[96,512]{1,0:T(8,128)(2,1)S(1)} all-gather(bf16[48,512]{1,0:T(8,128)(2,1)S(1)} %pad_maximum_fusion.2), channel_id=1, replica_groups=mesh['hi'=4,'core'=2,'lo'=2,'ring'=48] {'core'}, dimensions={0}, use_global_device_ids=true | all-gather | bytes 147456 | tf_op jit(solution)/shard_map/all_gather | solution.py:55
  66.5 0.2 fusion.10
  66.7 0.0 collective-permute-done.1
  66.7 0.2 fusion
  66.9 0.1 reshape.23
  67.0 23.1 %all_to_all.20 = bf16[48,2,1024]{2,1,0:T(2,128)(2,1)S(1)} all-to-all(bf16[48,2,1024]{2,1,0:T(2,128)(2,1)S(1)} %reshape.23), channel_id=1, replica_groups=mesh['hi'=4,'core'=2,'lo'=2,'ring'=48] {'ring'}, dimensions={0} | all-to-all | bytes 393216 | tf_op jit(solution)/shard_map/all_to_all | solution.py:57
  90.1 0.2 convert_reduce_fusion.3
  90.3 0.1 broadcast_in_dim.10
  90.4 19.7 %all_to_all.21 = bf16[48,2,1024]{2,1,0:T(2,128)(2,1)S(1)} all-to-all(bf16[48,2,1024]{2,1,0:T(2,128)(2,1)S(1)} %broadcast_in_dim.10), channel_id=1, replica_groups=mesh['hi'=4,'core'=2,'lo'=2,'ring'=48] {'ring'}, dimensions={0} | all-to-all | bytes 393216 | tf_op jit(solution)/shard_map/all_to_all | solution.py:29
  110.1 0.7 copy-done.1
  110.8 0.3 multiply_reduce_fusion
  111.1 0.1 convert_element_type.119
  111.2 1.0 reshape.26
  112.2 0.3 convolution_convert_fusion.1
  112.5 0.3 convolution_convert_fusion
  112.8 0.1 broadcast_in_dim.11
  112.9 2.1 %all-gather.2 = bf16[192,1152]{1,0:T(8,128)(2,1)S(1)} all-gather(bf16[96,1152]{1,0:T(8,128)(2,1)S(1)} %pad_maximum_fusion.1), channel_id=4, replica_groups=mesh['hi'=4,'core'=2,'lo'=2,'ring'=48] {'core'}, dimensions={0}, use_global_device_ids=true | all-gather | bytes 663552 | tf_op jit(solution)/shard_map/all_gather | solution.py:44
  115.1 16.5 %all-gather.3 = bf16[192,1152]{1,0:T(8,128)(2,1)S(1)} all-gather(bf16[48,1152]{1,0:T(8,128)(2,1)S(1)} %dynamic-slice_reduce_fusion), channel_id=5, replica_groups=mesh['hi'=4,'core'=2,'lo'=2,'ring'=48] {'hi'}, dimensions={0}, use_global_device_ids=true | all-gather | bytes 552960 | tf_op jit(solution)/shard_map/all_gather | solution.py:47
  131.6 0.1 convert_reduce_fusion
  131.6 0.1 fusion.18
  131.8 0.1 fusion.8
  131.9 1.9 %all_gather.39 = bf16[96,512]{1,0:T(8,128)(2,1)S(1)} all-gather(bf16[48,512]{1,0:T(8,128)(2,1)S(1)} %pad_maximum_fusion.3), channel_id=1, replica_groups=mesh['hi'=4,'core'=2,'lo'=2,'ring'=48] {'core'}, dimensions={0}, use_global_device_ids=true | all-gather | bytes 147456 | tf_op jit(solution)/shard_map/all_gather | solution.py:55
  133.8 0.2 fusion.3
  134.0 0.2 fusion.1
  134.2 0.1 reshape.24
  134.3 20.8 %all_to_all.22 = bf16[48,2,1024]{2,1,0:T(2,128)(2,1)S(1)} all-to-all(bf16[48,2,1024]{2,1,0:T(2,128)(2,1)S(1)} %reshape.24), channel_id=1, replica_groups=mesh['hi'=4,'core'=2,'lo'=2,'ring'=48] {'ring'}, dimensions={0} | all-to-all | bytes 393216 | tf_op jit(solution)/shard_map/all_to_all | solution.py:57
  155.2 0.2 convert_reduce_fusion.2
  155.3 0.6 add_convert_fusion
  (15 shorter events, 0.2 us)
Async XLA Ops:
  0.0 1.2 copy-start.2
  1.2 3.5 %copy-start.4 = (bf16[2,1024]{1,0:T(2,128)(2,1)S(1)}, bf16[2,1024]{1,0:T(2,128)(2,1)}, u32[]{:S(2)}) copy-start(bf16[2,1024]{1,0:T(2,128)(2,1)} %param.5) | copy-start | bytes 12292
  1.2 39.5 %collective-permute-start = (bf16[1024,512]{1,0:T(8,128)(2,1)S(1)}, bf16[1024,512]{1,0:T(8,128)(2,1)S(1)}, u32[]{:S(2)}, u32[]{:S(2)}) collective-permute-start(bf16[1024,512]{1,0:T(8,128)(2,1)S(1)} %constant_dynamic-update-slice_fusion), channel_id=1, source_target_pairs={{0,48},{48,0},{1,49},{49,1},{2,50},{50,2},{3,51},{51,3},{4,52},{52... | collective-permute-start | bytes 3145736 | tf_op jit(solution)/shard_map/ppermute | solution.py:24
  5.5 32.5 %copy-start = (bf16[256,1024]{1,0:T(8,128)(2,1)S(1)}, bf16[256,1024]{1,0:T(8,128)(2,1)}, u32[]{:S(2)}) copy-start(bf16[256,1024]{1,0:T(8,128)(2,1)} %param.9) | copy-start | bytes 1572868
  5.5 32.0 %all-to-all-start = ((bf16[48,2,1024]{2,1,0:T(2,128)(2,1)}), bf16[48,2,1024]{2,1,0:T(2,128)(2,1)S(1)}, u32[]{:S(2)}, u32[]{:S(2)}) async-start(bf16[48,2,1024]{2,1,0:T(2,128)(2,1)} %broadcast_in_dim.8), calls=%async_computation | async-start | bytes 393216 | tf_op jit(solution)/shard_map/all_to_all | solution.py:29
  37.9 2.5 %copy-start.3 = (f32[1024]{0:T(1024)S(1)}, f32[1024]{0:T(1024)}, u32[]{:S(2)}) copy-start(f32[1024]{0:T(1024)} %param.6) | copy-start | bytes 12292
  38.0 28.7 %collective-permute-start.1 = (bf16[256,1024]{1,0:T(8,128)(2,1)S(1)}, bf16[256,1024]{1,0:T(8,128)(2,1)S(1)}, u32[]{:S(2)}, u32[]{:S(2)}) collective-permute-start(bf16[256,1024]{1,0:T(8,128)(2,1)S(1)} %copy-done), channel_id=1, source_target_pairs={{0,48},{48,0},{1,49},{49,1},{2,50},{50,2},{3,51},{51,3},{4,52},{52... | collective-permute-start | bytes 1572872 | tf_op jit(solution)/shard_map/ppermute | solution.py:32
  110.1 0.7 copy-start.1

commit v4 on v3

--- a/solution.py
+++ b/solution.py
@@ -22,15 +22,13 @@
     core = lax.axis_index("core")
     paired = jnp.concatenate([w_gate, w_up], axis=1)
     far = lax.ppermute(paired, "lo", PAIR)
-    down_far = None
+    down_far = lax.ppermute(w_down, "lo", PAIR)
     mixed = tokens
     for step in range(ITERS):
         spread = jnp.broadcast_to(mixed[None], (ring, rows, feats))
         everyone = lax.all_to_all(spread, "ring", 0, 0)
-        if step == 0:
-            everyone, later = lax.optimization_barrier((everyone, w_down))
-            down_far = lax.ppermute(later, "lo", PAIR)
-        wide = everyone.reshape(total, feats).astype(jnp.float32)
+        everyone = lax.optimization_barrier(everyone.reshape(total, feats))
+        wide = everyone.astype(jnp.float32)
         squares = jnp.sum(wide * wide, axis=1, keepdims=True)
         gained = (wide * norm_gain).astype(jnp.bfloat16)
         packed = jnp.concatenate(

time: 157 us -> 154 us (0.981)
  waiting for transfers between devices: 13.4 us -> 11.1 us
    all_gather x2, blocking collectives: 37.5 us -> 33.3 us  [on_device(): lax.all_gather(chip, 'hi', axis=0).astype(jnp.float32)]
    all_to_all x2, blocking collectives: 43.9 us -> 48 us  [on_device(): lax.all_to_all(delta.astype(jnp.bfloat16).reshape(ring, rows, feats), 'ri...]
    all_to_all x1, waiting for transfers between devices: 13.4 us -> 11.1 us  [on_device(): everyone = lax.all_to_all(spread, 'ring', 0, 0)]
  transfers between devices with their start and end apart: 3 -> 3, of which waited for: 1 -> 1; matrix products, arithmetic and copies ran while one was open for 2% -> 1% of each run, Pallas kernels for 0% -> 0%
where the time goes in v4:
time: 154 us; the launch traced here: 152 us
  blocking collectives  109 us (71%)
  starting transfers between devices  24.4 us (16%)
  waiting for transfers between devices  11.1 us (7%)
  local copies, waits for them, and re-layouts  3.12 us (2%)
  matrix products  2.12 us (1%)
  other arithmetic  1.94 us (1%)
    all_to_all x2, blocking collectives, on_device(): lax.all_to_all(delta.astype(jnp.bfloat16).reshape(ring, rows, feats), 'ri...  48 us
    all_gather x2, blocking collectives, on_device(): lax.all_gather(chip, 'hi', axis=0).astype(jnp.float32)  33.3 us
    all_to_all x1, blocking collectives, on_device(): everyone = lax.all_to_all(spread, 'ring', 0, 0)  19.7 us
    all_to_all x1, starting transfers between devices, on_device(): everyone = lax.all_to_all(spread, 'ring', 0, 0)  18.4 us
    all_to_all x1, waiting for transfers between devices, on_device(): everyone = lax.all_to_all(spread, 'ring', 0, 0)  11.1 us
    all_gather x2, blocking collectives, on_device(): both = lax.all_gather(packed, 'core', axis=0)  4.25 us
    all_gather x2, blocking collectives, on_device(): lax.all_gather(jnp.concatenate(sides, axis=1), 'core', axis=0, tiled=True)  3.75 us
    ppermute x1, starting transfers between devices, on_device(): far = lax.ppermute(paired, 'lo', PAIR)  3.62 us
  transfers between devices with their start and end apart: 3, of which 1 were waited for; matrix products, arithmetic and copies ran while one was open for 1% of the time, Pallas kernels for 0%

profile of v4, /device:TPU:6, one launch (start us, length us, event | category | flops | bytes accessed | tf_op | source)
XLA Modules:
  0.0 151.9 jit_solution(8440724521360232422)
XLA Ops:
  0.0 1.1 constant_dynamic-update-slice_fusion.1
  1.1 0.1 copy-done.1
  1.2 0.0 copy-start
  1.3 3.6 %collective-permute-start = (bf16[1024,512]{1,0:T(8,128)(2,1)S(1)}, bf16[1024,512]{1,0:T(8,128)(2,1)S(1)}, u32[]{:S(2)}, u32[]{:S(2)}) collective-permute-start(bf16[1024,512]{1,0:T(8,128)(2,1)S(1)} %constant_dynamic-update-slice_fusion), channel_id=1, source_target_pairs={{0,48},{48,0},{1,49},{49,1},{2,50},{50,2},{3,51},{51,3},{4,52},{52... | collective-permute-start | bytes 3145736 | tf_op jit(solution)/shard_map/ppermute | solution.py:24
  4.9 0.0 copy-done.3
  4.9 0.8 broadcast_in_dim.8
  5.7 18.4 %all-to-all-start = ((bf16[48,2,1024]{2,1,0:T(2,128)(2,1)}), bf16[48,2,1024]{2,1,0:T(2,128)(2,1)S(1)}, u32[]{:S(2)}, u32[]{:S(2)}) async-start(bf16[48,2,1024]{2,1,0:T(2,128)(2,1)} %broadcast_in_dim.8), calls=%async_computation | async-start | bytes 393216 | tf_op jit(solution)/shard_map/all_to_all | solution.py:29
  24.1 2.4 %collective-permute-start.1 = (bf16[256,1024]{1,0:T(8,128)(2,1)S(1)}, bf16[256,1024]{1,0:T(8,128)(2,1)S(1)}, u32[]{:S(2)}, u32[]{:S(2)}) collective-permute-start(bf16[256,1024]{1,0:T(8,128)(2,1)S(1)} %copy-done), channel_id=1, source_target_pairs={{0,48},{48,0},{1,49},{49,1},{2,50},{50,2},{3,51},{51,3},{4,52},{52... | collective-permute-start | bytes 1572872 | tf_op jit(solution)/shard_map/ppermute | solution.py:25
  26.5 11.1 %all-to-all-done = bf16[48,2,1024]{2,1,0:T(2,128)(2,1)S(1)} async-done(((bf16[48,2,1024]{2,1,0:T(2,128)(2,1)}), bf16[48,2,1024]{2,1,0:T(2,128)(2,1)S(1)}, u32[]{:S(2)}, u32[]{:S(2)}) %all-to-all-start) | async-done | bytes 196640 | tf_op jit(solution)/shard_map/all_to_all | solution.py:29
  37.5 0.1 reshape.17
  37.6 0.0 copy-start.2
  37.6 0.1 fusion.3
  37.8 0.5 copy-done.2
  38.3 0.3 convolution_convert_fusion.3
  38.6 0.0 collective-permute-done
  38.6 0.3 convolution_convert_fusion.2
  38.9 0.1 broadcast_in_dim.9
  39.0 2.1 %all-gather = bf16[192,1152]{1,0:T(8,128)(2,1)S(1)} all-gather(bf16[96,1152]{1,0:T(8,128)(2,1)S(1)} %pad_maximum_fusion), channel_id=2, replica_groups=mesh['hi'=4,'core'=2,'lo'=2,'ring'=48] {'core'}, dimensions={0}, use_global_device_ids=true | all-gather | bytes 663552 | tf_op jit(solution)/shard_map/all_gather | solution.py:42
  41.2 17.2 %all-gather.1 = bf16[192,1152]{1,0:T(8,128)(2,1)S(1)} all-gather(bf16[48,1152]{1,0:T(8,128)(2,1)S(1)} %dynamic-slice_reduce_fusion.1), channel_id=3, replica_groups=mesh['hi'=4,'core'=2,'lo'=2,'ring'=48] {'hi'}, dimensions={0}, use_global_device_ids=true | all-gather | bytes 552960 | tf_op jit(solution)/shard_map/all_gather | solution.py:45
  58.4 0.1 convert_reduce_fusion.1
  58.4 0.1 fusion.29
  58.5 0.1 fusion.23
  58.7 1.9 %all_gather.34 = bf16[96,512]{1,0:T(8,128)(2,1)S(1)} all-gather(bf16[48,512]{1,0:T(8,128)(2,1)S(1)} %pad_maximum_fusion.2), channel_id=1, replica_groups=mesh['hi'=4,'core'=2,'lo'=2,'ring'=48] {'core'}, dimensions={0}, use_global_device_ids=true | all-gather | bytes 147456 | tf_op jit(solution)/shard_map/all_gather | solution.py:53
  60.6 0.2 fusion.18
  60.8 0.0 collective-permute-done.1
  60.8 0.2 fusion
  61.0 0.1 reshape.18
  61.1 27.1 %all_to_all.20 = bf16[48,2,1024]{2,1,0:T(2,128)(2,1)S(1)} all-to-all(bf16[48,2,1024]{2,1,0:T(2,128)(2,1)S(1)} %reshape.18), channel_id=1, replica_groups=mesh['hi'=4,'core'=2,'lo'=2,'ring'=48] {'ring'}, dimensions={0} | all-to-all | bytes 393216 | tf_op jit(solution)/shard_map/all_to_all | solution.py:55
  88.3 0.2 convert_reduce_fusion.3
  88.4 0.1 broadcast_in_dim.10
  88.6 19.7 %all_to_all.21 = bf16[48,2,1024]{2,1,0:T(2,128)(2,1)S(1)} all-to-all(bf16[48,2,1024]{2,1,0:T(2,128)(2,1)S(1)} %broadcast_in_dim.10), channel_id=1, replica_groups=mesh['hi'=4,'core'=2,'lo'=2,'ring'=48] {'ring'}, dimensions={0} | all-to-all | bytes 393216 | tf_op jit(solution)/shard_map/all_to_all | solution.py:29
  108.3 0.1 reshape.19
  108.4 0.3 convolution_convert_fusion.1
  108.7 0.1 fusion.5
  108.8 0.3 convolution_convert_fusion
  109.1 0.1 broadcast_in_dim.11
  109.2 2.1 %all-gather.2 = bf16[192,1152]{1,0:T(8,128)(2,1)S(1)} all-gather(bf16[96,1152]{1,0:T(8,128)(2,1)S(1)} %pad_maximum_fusion.1), channel_id=4, replica_groups=mesh['hi'=4,'core'=2,'lo'=2,'ring'=48] {'core'}, dimensions={0}, use_global_device_ids=true | all-gather | bytes 663552 | tf_op jit(solution)/shard_map/all_gather | solution.py:42
  111.4 16.2 %all-gather.3 = bf16[192,1152]{1,0:T(8,128)(2,1)S(1)} all-gather(bf16[48,1152]{1,0:T(8,128)(2,1)S(1)} %dynamic-slice_reduce_fusion), channel_id=5, replica_groups=mesh['hi'=4,'core'=2,'lo'=2,'ring'=48] {'hi'}, dimensions={0}, use_global_device_ids=true | all-gather | bytes 552960 | tf_op jit(solution)/shard_map/all_gather | solution.py:45
  127.5 0.1 convert_reduce_fusion
  127.6 0.1 fusion.26
  127.7 0.1 fusion.16
  127.8 1.9 %all_gather.39 = bf16[96,512]{1,0:T(8,128)(2,1)S(1)} all-gather(bf16[48,512]{1,0:T(8,128)(2,1)S(1)} %pad_maximum_fusion.3), channel_id=1, replica_groups=mesh['hi'=4,'core'=2,'lo'=2,'ring'=48] {'core'}, dimensions={0}, use_global_device_ids=true | all-gather | bytes 147456 | tf_op jit(solution)/shard_map/all_gather | solution.py:53
  129.7 0.2 fusion.11
  129.9 0.2 fusion.1
  130.2 0.1 reshape.20
  130.3 20.8 %all_to_all.22 = bf16[48,2,1024]{2,1,0:T(2,128)(2,1)S(1)} all-to-all(bf16[48,2,1024]{2,1,0:T(2,128)(2,1)S(1)} %reshape.20), channel_id=1, replica_groups=mesh['hi'=4,'core'=2,'lo'=2,'ring'=48] {'ring'}, dimensions={0} | all-to-all | bytes 393216 | tf_op jit(solution)/shard_map/all_to_all | solution.py:55
  151.1 0.2 convert_reduce_fusion.2
  151.3 0.6 add_convert_fusion
  (11 shorter events, 0.2 us)
Async XLA Ops:
  0.0 1.2 copy-start.1
  1.2 3.7 %copy-start.3 = (bf16[2,1024]{1,0:T(2,128)(2,1)S(1)}, bf16[2,1024]{1,0:T(2,128)(2,1)}, u32[]{:S(2)}) copy-start(bf16[2,1024]{1,0:T(2,128)(2,1)} %param.5) | copy-start | bytes 12292
  1.2 22.9 %copy-start = (bf16[256,1024]{1,0:T(8,128)(2,1)S(1)}, bf16[256,1024]{1,0:T(8,128)(2,1)}, u32[]{:S(2)}) copy-start(bf16[256,1024]{1,0:T(8,128)(2,1)} %param.9) | copy-start | bytes 1572868
  1.3 37.4 %collective-permute-start = (bf16[1024,512]{1,0:T(8,128)(2,1)S(1)}, bf16[1024,512]{1,0:T(8,128)(2,1)S(1)}, u32[]{:S(2)}, u32[]{:S(2)}) collective-permute-start(bf16[1024,512]{1,0:T(8,128)(2,1)S(1)} %constant_dynamic-update-slice_fusion), channel_id=1, source_target_pairs={{0,48},{48,0},{1,49},{49,1},{2,50},{50,2},{3,51},{51,3},{4,52},{52... | collective-permute-start | bytes 3145736 | tf_op jit(solution)/shard_map/ppermute | solution.py:24
  5.7 31.9 %all-to-all-start = ((bf16[48,2,1024]{2,1,0:T(2,128)(2,1)}), bf16[48,2,1024]{2,1,0:T(2,128)(2,1)S(1)}, u32[]{:S(2)}, u32[]{:S(2)}) async-start(bf16[48,2,1024]{2,1,0:T(2,128)(2,1)} %broadcast_in_dim.8), calls=%async_computation | async-start | bytes 393216 | tf_op jit(solution)/shard_map/all_to_all | solution.py:29
  24.1 36.7 %collective-permute-start.1 = (bf16[256,1024]{1,0:T(8,128)(2,1)S(1)}, bf16[256,1024]{1,0:T(8,128)(2,1)S(1)}, u32[]{:S(2)}, u32[]{:S(2)}) collective-permute-start(bf16[256,1024]{1,0:T(8,128)(2,1)S(1)} %copy-done), channel_id=1, source_target_pairs={{0,48},{48,0},{1,49},{49,1},{2,50},{50,2},{3,51},{51,3},{4,52},{52... | collective-permute-start | bytes 1572872 | tf_op jit(solution)/shard_map/ppermute | solution.py:25
  37.6 0.7 copy-start.2

commit v5 on v4

--- a/solution.py
+++ b/solution.py
@@ -21,8 +21,11 @@
     half = total // CORE
     core = lax.axis_index("core")
     paired = jnp.concatenate([w_gate, w_up], axis=1)
-    far = lax.ppermute(paired, "lo", PAIR)
-    down_far = lax.ppermute(w_down, "lo", PAIR)
+    deep = w_down.shape[0]
+    stripes = jnp.concatenate(jnp.split(w_down, feats // deep, axis=1), axis=0)
+    swapped = lax.ppermute(jnp.concatenate([paired, stripes], axis=1), "lo", PAIR)
+    far = swapped[:, :width]
+    down_far = jnp.concatenate(jnp.split(swapped[:, width:], feats // deep, axis=0), axis=1)
     mixed = tokens
     for step in range(ITERS):
         spread = jnp.broadcast_to(mixed[None], (ring, rows, feats))

time: 154 us -> 169 us (1.097)
  blocking collectives: 109 us -> 115 us
  waiting for transfers between devices: 11.1 us -> 14.9 us
  other arithmetic: 1.94 us -> 4.45 us
  matrix products: 2.12 us -> 4.57 us
  starting transfers between devices: 24.4 us -> 22.2 us
    all_to_all x2, blocking collectives: 48 us -> 53.2 us  [on_device(): lax.all_to_all(delta.astype(jnp.bfloat16).reshape(ring, rows, feats), 'ri...]
    concatenate x0 -> x1, other arithmetic: none -> 2.51 us  [on_device(): jnp.concatenate([paired, stripes], axis=1)]
    dot_general x8, matrix products: 2.12 us -> 4.57 us  [matmul(): return jnp.dot(left, right, preferred_element_type=jnp.float32)]
    ppermute x2 -> x1, starting transfers between devices: 5.97 us -> 3.61 us  [on_device(): lax.ppermute(jnp.concatenate([paired, stripes], axis=1), 'lo', PAIR)]
    split x0 -> x2, local copies, waits for them, and re-layouts: none -> 2.28 us  [the longest x1 1.14 us: on_device(): jnp.split(swapped[:, width:], feats // deep, axis=0)]
    all_to_all x1, waiting for transfers between devices: 11.1 us -> 13.3 us  [on_device(): everyone = lax.all_to_all(spread, 'ring', 0, 0)]
  transfers between devices with their start and end apart: 3 -> 2, of which waited for: 1 -> 2; matrix products, arithmetic and copies ran while one was open for 1% -> 1% of each run, Pallas kernels for 0% -> 0%
where the time goes in v5:
time: 169 us; the launch traced here: 165 us
  blocking collectives  115 us (68%)
  starting transfers between devices  22.2 us (13%)
  waiting for transfers between devices  14.9 us (9%)
  matrix products  4.57 us (3%)
  other arithmetic  4.45 us (3%)
  local copies, waits for them, and re-layouts  3.72 us (2%)
    all_to_all x2, blocking collectives, on_device(): lax.all_to_all(delta.astype(jnp.bfloat16).reshape(ring, rows, feats), 'ri...  53.2 us
    all_gather x2, blocking collectives, on_device(): lax.all_gather(chip, 'hi', axis=0).astype(jnp.float32)  34.3 us
    all_to_all x1, blocking collectives, on_device(): everyone = lax.all_to_all(spread, 'ring', 0, 0)  19.7 us
    all_to_all x1, starting transfers between devices, on_device(): everyone = lax.all_to_all(spread, 'ring', 0, 0)  18.6 us
    all_to_all x1, waiting for transfers between devices, on_device(): everyone = lax.all_to_all(spread, 'ring', 0, 0)  13.3 us
    dot_general x8, matrix products, matmul(): return jnp.dot(left, right, preferred_element_type=jnp.float32)  4.57 us
    all_gather x2, blocking collectives, on_device(): both = lax.all_gather(packed, 'core', axis=0)  4.38 us
    all_gather x2, blocking collectives, on_device(): lax.all_gather(jnp.concatenate(sides, axis=1), 'core', axis=0, tiled=True)  3.75 us
  transfers between devices with their start and end apart: 2, of which 2 were waited for; matrix products, arithmetic and copies ran while one was open for 1% of the time, Pallas kernels for 0%

profile of v5, /device:TPU:6, one launch (start us, length us, event | category | flops | bytes accessed | tf_op | source)
XLA Modules:
  0.0 165.3 jit_solution(10426333889857862583)
XLA Ops:
  0.0 1.1 fusion.35
  1.1 0.0 copy-start.4
  1.1 0.0 copy-start.1
  1.2 2.5 %maximum_maximum_fusion = bf16[1024,768]{1,0:T(8,128)(2,1)} fusion(bf16[256,256]{1,0:T(8,128)(2,1)S(1)} %get-tuple-element.10, bf16[256,256]{1,0:T(8,128)(2,1)S(1)} %get-tuple-element.11, bf16[256,256]{1,0:T(8,128)(2,1)S(1)} %get-tuple-element.12, bf16[256,256]{1,0:T(8,128)(2,1)S(1)} %get-tuple-element.9, bf16[1024,256]{1,0:T(8,128)(2,1)} %param.8, ...), kind=kLoop, calls=%fused_computation | loop fusion | flops 9437184 | bytes 3145728 | tf_op jit(solution)/shard_map/concatenate | solution.py:26
  3.7 3.6 %collective-permute-start = (bf16[1024,768]{1,0:T(8,128)(2,1)}, bf16[1024,768]{1,0:T(8,128)(2,1)}, u32[]{:S(2)}, u32[]{:S(2)}) collective-permute-start(bf16[1024,768]{1,0:T(8,128)(2,1)} %maximum_maximum_fusion), channel_id=1, source_target_pairs={{0,48},{48,0},{1,49},{49,1},{2,50},{50,2},{3,51},{51,3},{4,52},{52... | collective-permute-start | bytes 4718600 | tf_op jit(solution)/shard_map/ppermute | solution.py:26
  7.3 0.0 copy-done.4
  7.3 0.8 broadcast_in_dim.8
  8.1 18.6 %all-to-all-start = ((bf16[48,2,1024]{2,1,0:T(2,128)(2,1)}), bf16[48,2,1024]{2,1,0:T(2,128)(2,1)S(1)}, u32[]{:S(2)}, u32[]{:S(2)}) async-start(bf16[48,2,1024]{2,1,0:T(2,128)(2,1)} %broadcast_in_dim.8), calls=%async_computation | async-start | bytes 393216 | tf_op jit(solution)/shard_map/all_to_all | solution.py:32
  26.7 0.0 copy-done.1
  26.8 13.3 %all-to-all-done = bf16[48,2,1024]{2,1,0:T(2,128)(2,1)S(1)} async-done(((bf16[48,2,1024]{2,1,0:T(2,128)(2,1)}), bf16[48,2,1024]{2,1,0:T(2,128)(2,1)S(1)}, u32[]{:S(2)}, u32[]{:S(2)}) %all-to-all-start) | async-done | bytes 196640 | tf_op jit(solution)/shard_map/all_to_all | solution.py:32
  40.1 0.1 reshape.17
  40.2 0.1 fusion.5
  40.3 0.3 convolution_convert_fusion.3
  40.6 1.5 collective-permute-done
  42.1 1.5 convolution_convert_fusion.2
  43.7 0.1 broadcast_in_dim.9
  43.8 0.0 copy-start
  43.8 2.3 %all-gather = bf16[192,1152]{1,0:T(8,128)(2,1)S(1)} all-gather(bf16[96,1152]{1,0:T(8,128)(2,1)S(1)} %pad_maximum_fusion.1), channel_id=2, replica_groups=mesh['hi'=4,'core'=2,'lo'=2,'ring'=48] {'core'}, dimensions={0}, use_global_device_ids=true | all-gather | bytes 663552 | tf_op jit(solution)/shard_map/all_gather | solution.py:45
  46.1 18.9 %all-gather.1 = bf16[192,1152]{1,0:T(8,128)(2,1)S(1)} all-gather(bf16[48,1152]{1,0:T(8,128)(2,1)S(1)} %dynamic-slice_reduce_fusion.1), channel_id=3, replica_groups=mesh['hi'=4,'core'=2,'lo'=2,'ring'=48] {'hi'}, dimensions={0}, use_global_device_ids=true | all-gather | bytes 552960 | tf_op jit(solution)/shard_map/all_gather | solution.py:48
  65.0 0.1 convert_reduce_fusion.1
  65.1 0.1 fusion.31
  65.2 0.1 fusion.25
  65.3 1.9 %all_gather.34 = bf16[96,512]{1,0:T(8,128)(2,1)S(1)} all-gather(bf16[48,512]{1,0:T(8,128)(2,1)S(1)} %pad_maximum_fusion.5), channel_id=1, replica_groups=mesh['hi'=4,'core'=2,'lo'=2,'ring'=48] {'core'}, dimensions={0}, use_global_device_ids=true | all-gather | bytes 147456 | tf_op jit(solution)/shard_map/all_gather | solution.py:56
  67.2 0.2 fusion.20
  67.5 1.1 fusion.34
  68.6 0.2 fusion
  68.8 0.1 reshape.18
  68.9 32.4 %all_to_all.20 = bf16[48,2,1024]{2,1,0:T(2,128)(2,1)S(1)} all-to-all(bf16[48,2,1024]{2,1,0:T(2,128)(2,1)S(1)} %reshape.18), channel_id=1, replica_groups=mesh['hi'=4,'core'=2,'lo'=2,'ring'=48] {'ring'}, dimensions={0} | all-to-all | bytes 393216 | tf_op jit(solution)/shard_map/all_to_all | solution.py:58
  101.3 0.2 convert_reduce_fusion.3
  101.5 0.1 broadcast_in_dim.10
  101.6 19.7 %all_to_all.21 = bf16[48,2,1024]{2,1,0:T(2,128)(2,1)S(1)} all-to-all(bf16[48,2,1024]{2,1,0:T(2,128)(2,1)S(1)} %broadcast_in_dim.10), channel_id=1, replica_groups=mesh['hi'=4,'core'=2,'lo'=2,'ring'=48] {'ring'}, dimensions={0} | all-to-all | bytes 393216 | tf_op jit(solution)/shard_map/all_to_all | solution.py:32
  121.3 0.1 reshape.19
  121.4 0.3 convolution_convert_fusion.1
  121.7 0.1 fusion.7
  121.9 1.5 convolution_convert_fusion
  123.4 0.1 broadcast_in_dim.11
  123.5 2.1 %all-gather.2 = bf16[192,1152]{1,0:T(8,128)(2,1)S(1)} all-gather(bf16[96,1152]{1,0:T(8,128)(2,1)S(1)} %pad_maximum_fusion.2), channel_id=4, replica_groups=mesh['hi'=4,'core'=2,'lo'=2,'ring'=48] {'core'}, dimensions={0}, use_global_device_ids=true | all-gather | bytes 663552 | tf_op jit(solution)/shard_map/all_gather | solution.py:45
  125.7 15.3 %all-gather.3 = bf16[192,1152]{1,0:T(8,128)(2,1)S(1)} all-gather(bf16[48,1152]{1,0:T(8,128)(2,1)S(1)} %dynamic-slice_reduce_fusion), channel_id=5, replica_groups=mesh['hi'=4,'core'=2,'lo'=2,'ring'=48] {'hi'}, dimensions={0}, use_global_device_ids=true | all-gather | bytes 552960 | tf_op jit(solution)/shard_map/all_gather | solution.py:48
  141.0 0.1 convert_reduce_fusion
  141.1 0.1 fusion.28
  141.2 0.1 fusion.18
  141.3 1.9 %all_gather.39 = bf16[96,512]{1,0:T(8,128)(2,1)S(1)} all-gather(bf16[48,512]{1,0:T(8,128)(2,1)S(1)} %pad_maximum_fusion.6), channel_id=1, replica_groups=mesh['hi'=4,'core'=2,'lo'=2,'ring'=48] {'core'}, dimensions={0}, use_global_device_ids=true | all-gather | bytes 147456 | tf_op jit(solution)/shard_map/all_gather | solution.py:56
  143.2 0.2 fusion.13
  143.4 0.2 fusion.1
  143.6 0.1 reshape.20
  143.7 20.8 %all_to_all.22 = bf16[48,2,1024]{2,1,0:T(2,128)(2,1)S(1)} all-to-all(bf16[48,2,1024]{2,1,0:T(2,128)(2,1)S(1)} %reshape.20), channel_id=1, replica_groups=mesh['hi'=4,'core'=2,'lo'=2,'ring'=48] {'ring'}, dimensions={0} | all-to-all | bytes 393216 | tf_op jit(solution)/shard_map/all_to_all | solution.py:58
  164.5 0.2 convert_reduce_fusion.2
  164.7 0.6 add_convert_fusion
  (14 shorter events, 0.2 us)
Async XLA Ops:
  1.1 6.2 %copy-start.4 = (bf16[2,1024]{1,0:T(2,128)(2,1)S(1)}, bf16[2,1024]{1,0:T(2,128)(2,1)}, u32[]{:S(2)}) copy-start(bf16[2,1024]{1,0:T(2,128)(2,1)} %param.5) | copy-start | bytes 12292
  1.1 25.5 %copy-start.1 = (bf16[1024,256]{1,0:T(8,128)(2,1)S(1)}, bf16[1024,256]{1,0:T(8,128)(2,1)}, u32[]{:S(2)}) copy-start(bf16[1024,256]{1,0:T(8,128)(2,1)} %param.7) | copy-start | bytes 1572868
  3.7 23.0 %copy-start.2 = (bf16[1024,256]{1,0:T(8,128)(2,1)S(1)}, bf16[1024,256]{1,0:T(8,128)(2,1)}, u32[]{:S(2)}) copy-start(bf16[1024,256]{1,0:T(8,128)(2,1)} %param.8) | copy-start | bytes 1572868
  3.7 38.5 %collective-permute-start = (bf16[1024,768]{1,0:T(8,128)(2,1)}, bf16[1024,768]{1,0:T(8,128)(2,1)}, u32[]{:S(2)}, u32[]{:S(2)}) collective-permute-start(bf16[1024,768]{1,0:T(8,128)(2,1)} %maximum_maximum_fusion), channel_id=1, source_target_pairs={{0,48},{48,0},{1,49},{49,1},{2,50},{50,2},{3,51},{51,3},{4,52},{52... | collective-permute-start | bytes 4718600 | tf_op jit(solution)/shard_map/ppermute | solution.py:26
  8.1 32.2 %copy-start.3 = (f32[1024]{0:T(1024)S(1)}, f32[1024]{0:T(1024)}, u32[]{:S(2)}) copy-start(f32[1024]{0:T(1024)} %param.6) | copy-start | bytes 12292
  8.1 32.0 %all-to-all-start = ((bf16[48,2,1024]{2,1,0:T(2,128)(2,1)}), bf16[48,2,1024]{2,1,0:T(2,128)(2,1)S(1)}, u32[]{:S(2)}, u32[]{:S(2)}) async-start(bf16[48,2,1024]{2,1,0:T(2,128)(2,1)} %broadcast_in_dim.8), calls=%async_computation | async-start | bytes 393216 | tf_op jit(solution)/shard_map/all_to_all | solution.py:32
  43.8 23.5 %copy-start = (bf16[256,1024]{1,0:T(8,128)(2,1)S(1)}, bf16[256,1024]{1,0:T(8,128)(2,1)}, u32[]{:S(2)}) copy-start(bf16[256,1024]{1,0:T(8,128)(2,1)} %param.9) | copy-start | bytes 1572868

commit v6 on v4

v6 whole, which is shorter than its diff:
```python
import jax
import jax.numpy as jnp
from jax import lax
from jax.sharding import Mesh, PartitionSpec as P

D = 8192
ITERS = 2
HI, CORE, FAR, NEAR = 4, 2, 2, 2
RING = ("yz", "near")
PAIR = ((0, 1), (1, 0))


def matmul(left, right):
    return jnp.dot(left, right, preferred_element_type=jnp.float32)


def on_device(tokens, norm_gain, w_gate, w_up, w_down):
    width = 2 * w_gate.shape[1]
    rows, feats = tokens.shape
    ring = lax.axis_size(RING)
    total = rows * ring
    half = total // CORE
    core = lax.axis_index("core")
    paired = jnp.concatenate([w_gate, w_up], axis=1)
    far = lax.ppermute(paired, "far", PAIR)
    down_far = lax.ppermute(w_down, "far", PAIR)
    mixed = tokens
    for step in range(ITERS):
        spread = jnp.broadcast_to(mixed[None], (ring, rows, feats))
        everyone = lax.all_to_all(spread, RING, 0, 0)
        everyone = lax.optimization_barrier(everyone.reshape(total, feats))
        wide = everyone.astype(jnp.float32)
        squares = jnp.sum(wide * wide, axis=1, keepdims=True)
        gained = (wide * norm_gain).astype(jnp.bfloat16)
        packed = jnp.concatenate(
            [
                matmul(gained, paired).astype(jnp.bfloat16),
                matmul(gained, far).astype(jnp.bfloat16),
                jnp.broadcast_to(squares, (total, 128)).astype(jnp.bfloat16),
            ],
            axis=1,
        )
        both = lax.all_gather(packed, "core", axis=0)
        mine = lax.dynamic_slice_in_dim(both, core * half, half, axis=1)
        chip = jnp.sum(mine.astype(jnp.float32), axis=0).astype(jnp.bfloat16)
        share = jnp.sum(lax.all_gather(chip, "hi", axis=0).astype(jnp.float32), axis=0)
        scale = lax.rsqrt(share[:, 2 * width : 2 * width + 1] / D + 1e-05)
        side = width // FAR
        sides = []
        for base in (0, width):
            gate = share[:, base : base + side] * scale
            up = share[:, base + side : base + width] * scale
            sides.append((jax.nn.silu(gate) * up).astype(jnp.bfloat16))
        hidden = lax.all_gather(jnp.concatenate(sides, axis=1), "core", axis=0, tiled=True)
        delta = matmul(hidden[:, :side], w_down) + matmul(hidden[:, side:], down_far)
        deltas = lax.all_to_all(delta.astype(jnp.bfloat16).reshape(ring, rows, feats), RING, 0, 0)
        mixed = (
            mixed.astype(jnp.float32) + jnp.sum(deltas.astype(jnp.float32), axis=0)
        ).astype(jnp.bfloat16)
    return mixed


def solution(mesh):
    planes = mesh.shape["col"] // (FAR * NEAR)
    fine = Mesh(mesh.devices.reshape(HI, CORE, planes, FAR, NEAR), ("hi", "core", "yz", "far", "near"))
    row, col = ("hi", "core"), ("yz", "far", "near")
    return jax.shard_map(
        on_device,
        mesh=fine,
        in_specs=(P(col, row), P(row), P(row, col), P(row, col), P(col, row)),
        out_specs=P(col, row),
        check_vma=False,
    )
```

time: 154 us -> 151 us (0.981)
  blocking collectives: 109 us -> 107 us
  waiting for transfers between devices: 11.1 us -> 9.3 us
    all_to_all x3, blocking collectives: 67.7 us -> 65.7 us  [the longest x2 47.3 us: on_device(): lax.all_to_all(delta.astype(jnp.bfloat16).reshape(ring, rows, feats), RIN...]
    all_to_all x1, waiting for transfers between devices: 11.1 us -> 9.3 us  [on_device(): everyone = lax.all_to_all(spread, RING, 0, 0)]
where the time goes in v6:
time: 151 us; the launch traced here: 149 us
  blocking collectives  107 us (71%)
  starting transfers between devices  25.4 us (17%)
  waiting for transfers between devices  9.3 us (6%)
  local copies, waits for them, and re-layouts  3.12 us (2%)
  matrix products  2.12 us (1%)
  other arithmetic  1.93 us (1%)
    all_to_all x2, blocking collectives, on_device(): lax.all_to_all(delta.astype(jnp.bfloat16).reshape(ring, rows, feats), RIN...  47.3 us
    all_gather x2, blocking collectives, on_device(): lax.all_gather(chip, 'hi', axis=0).astype(jnp.float32)  33.6 us
    all_to_all x1, blocking collectives, on_device(): everyone = lax.all_to_all(spread, RING, 0, 0)  18.4 us
    all_to_all x1, starting transfers between devices, on_device(): everyone = lax.all_to_all(spread, RING, 0, 0)  18 us
    all_to_all x1, waiting for transfers between devices, on_device(): everyone = lax.all_to_all(spread, RING, 0, 0)  9.3 us
    all_gather x2, blocking collectives, on_device(): both = lax.all_gather(packed, 'core', axis=0)  4.25 us
    ppermute x1, starting transfers between devices, on_device(): down_far = lax.ppermute(w_down, 'far', PAIR)  4.03 us
    all_gather x2, blocking collectives, on_device(): lax.all_gather(jnp.concatenate(sides, axis=1), 'core', axis=0, tiled=True)  3.75 us
  transfers between devices with their start and end apart: 3, of which 1 were waited for; matrix products, arithmetic and copies ran while one was open for 1% of the time, Pallas kernels for 0%

profile of v6, /device:TPU:6, one launch (start us, length us, event | category | flops | bytes accessed | tf_op | source)
XLA Modules:
  0.0 149.5 jit_solution(4029646813205051763)
XLA Ops:
  0.0 1.1 constant_dynamic-update-slice_fusion.1
  1.1 0.1 copy-done.1
  1.2 0.0 copy-start
  1.3 3.4 %collective-permute-start = (bf16[1024,512]{1,0:T(8,128)(2,1)S(1)}, bf16[1024,512]{1,0:T(8,128)(2,1)S(1)}, u32[]{:S(2)}, u32[]{:S(2)}) collective-permute-start(bf16[1024,512]{1,0:T(8,128)(2,1)S(1)} %constant_dynamic-update-slice_fusion), channel_id=1, source_target_pairs={{0,2},{2,0},{1,3},{3,1},{4,6},{6,4},{5,7},{7,5},{8,10},{10,8},{9,1... | collective-permute-start | bytes 3145736 | tf_op jit(solution)/shard_map/ppermute | solution.py:25
  4.7 0.0 copy-done.3
  4.7 0.8 broadcast_in_dim.8
  5.5 18.0 %all-to-all-start = ((bf16[48,2,1024]{2,1,0:T(2,128)(2,1)}), bf16[48,2,1024]{2,1,0:T(2,128)(2,1)S(1)}, u32[]{:S(2)}, u32[]{:S(2)}) async-start(bf16[48,2,1024]{2,1,0:T(2,128)(2,1)} %broadcast_in_dim.8), calls=%async_computation | async-start | bytes 393216 | tf_op jit(solution)/shard_map/all_to_all | solution.py:30
  23.5 4.0 %collective-permute-start.1 = (bf16[256,1024]{1,0:T(8,128)(2,1)S(1)}, bf16[256,1024]{1,0:T(8,128)(2,1)S(1)}, u32[]{:S(2)}, u32[]{:S(2)}) collective-permute-start(bf16[256,1024]{1,0:T(8,128)(2,1)S(1)} %copy-done), channel_id=1, source_target_pairs={{0,2},{2,0},{1,3},{3,1},{4,6},{6,4},{5,7},{7,5},{8,10},{10,8},{9,1... | collective-permute-start | bytes 1572872 | tf_op jit(solution)/shard_map/ppermute | solution.py:26
  27.5 9.3 %all-to-all-done = bf16[48,2,1024]{2,1,0:T(2,128)(2,1)S(1)} async-done(((bf16[48,2,1024]{2,1,0:T(2,128)(2,1)}), bf16[48,2,1024]{2,1,0:T(2,128)(2,1)S(1)}, u32[]{:S(2)}, u32[]{:S(2)}) %all-to-all-start) | async-done | bytes 196640 | tf_op jit(solution)/shard_map/all_to_all | solution.py:30
  36.8 0.1 reshape.17
  36.9 0.0 copy-start.2
  36.9 0.1 fusion.3
  37.0 0.5 copy-done.2
  37.6 0.3 convolution_convert_fusion.3
  37.9 0.0 collective-permute-done
  37.9 0.3 convolution_convert_fusion.2
  38.2 0.1 broadcast_in_dim.9
  38.3 2.1 %all-gather = bf16[192,1152]{1,0:T(8,128)(2,1)S(1)} all-gather(bf16[96,1152]{1,0:T(8,128)(2,1)S(1)} %pad_maximum_fusion), channel_id=2, replica_groups=mesh['hi'=4,'core'=2,'yz'=24,'far'=2,'near'=2] {'core'}, dimensions={0}, use_global_device_ids=true | all-gather | bytes 663552 | tf_op jit(solution)/shard_map/all_gather | solution.py:43
  40.5 17.4 %all-gather.1 = bf16[192,1152]{1,0:T(8,128)(2,1)S(1)} all-gather(bf16[48,1152]{1,0:T(8,128)(2,1)S(1)} %dynamic-slice_reduce_fusion.1), channel_id=3, replica_groups=mesh['hi'=4,'core'=2,'yz'=24,'far'=2,'near'=2] {'hi'}, dimensions={0}, use_global_device_ids=true | all-gather | bytes 552960 | tf_op jit(solution)/shard_map/all_gather | solution.py:46
  57.9 0.1 convert_reduce_fusion.1
  58.0 0.1 fusion.29
  58.1 0.1 fusion.23
  58.2 1.9 %all_gather.34 = bf16[96,512]{1,0:T(8,128)(2,1)S(1)} all-gather(bf16[48,512]{1,0:T(8,128)(2,1)S(1)} %pad_maximum_fusion.2), channel_id=1, replica_groups=mesh['hi'=4,'core'=2,'yz'=24,'far'=2,'near'=2] {'core'}, dimensions={0}, use_global_device_ids=true | all-gather | bytes 147456 | tf_op jit(solution)/shard_map/all_gather | solution.py:54
  60.1 0.2 fusion.18
  60.3 0.0 collective-permute-done.1
  60.3 0.2 fusion
  60.6 0.1 reshape.18
  60.7 27.5 %all_to_all.20 = bf16[48,2,1024]{2,1,0:T(2,128)(2,1)S(1)} all-to-all(bf16[48,2,1024]{2,1,0:T(2,128)(2,1)S(1)} %reshape.18), channel_id=1, replica_groups=mesh['hi'=4,'core'=2,'yz'=24,'far'=2,'near'=2] {'yz','near'}, dimensions={0} | all-to-all | bytes 393216 | tf_op jit(solution)/shard_map/all_to_all | solution.py:56
  88.1 0.2 convert_reduce_fusion.3
  88.3 0.1 broadcast_in_dim.10
  88.4 18.4 %all_to_all.21 = bf16[48,2,1024]{2,1,0:T(2,128)(2,1)S(1)} all-to-all(bf16[48,2,1024]{2,1,0:T(2,128)(2,1)S(1)} %broadcast_in_dim.10), channel_id=1, replica_groups=mesh['hi'=4,'core'=2,'yz'=24,'far'=2,'near'=2] {'yz','near'}, dimensions={0} | all-to-all | bytes 393216 | tf_op jit(solution)/shard_map/all_to_all | solution.py:30
  106.9 0.1 reshape.19
  106.9 0.3 convolution_convert_fusion.1
  107.2 0.1 fusion.5
  107.4 0.3 convolution_convert_fusion
  107.7 0.1 broadcast_in_dim.11
  107.8 2.1 %all-gather.2 = bf16[192,1152]{1,0:T(8,128)(2,1)S(1)} all-gather(bf16[96,1152]{1,0:T(8,128)(2,1)S(1)} %pad_maximum_fusion.1), channel_id=4, replica_groups=mesh['hi'=4,'core'=2,'yz'=24,'far'=2,'near'=2] {'core'}, dimensions={0}, use_global_device_ids=true | all-gather | bytes 663552 | tf_op jit(solution)/shard_map/all_gather | solution.py:43
  109.9 16.2 %all-gather.3 = bf16[192,1152]{1,0:T(8,128)(2,1)S(1)} all-gather(bf16[48,1152]{1,0:T(8,128)(2,1)S(1)} %dynamic-slice_reduce_fusion), channel_id=5, replica_groups=mesh['hi'=4,'core'=2,'yz'=24,'far'=2,'near'=2] {'hi'}, dimensions={0}, use_global_device_ids=true | all-gather | bytes 552960 | tf_op jit(solution)/shard_map/all_gather | solution.py:46
  126.1 0.1 convert_reduce_fusion
  126.2 0.1 fusion.26
  126.3 0.1 fusion.16
  126.4 1.9 %all_gather.39 = bf16[96,512]{1,0:T(8,128)(2,1)S(1)} all-gather(bf16[48,512]{1,0:T(8,128)(2,1)S(1)} %pad_maximum_fusion.3), channel_id=1, replica_groups=mesh['hi'=4,'core'=2,'yz'=24,'far'=2,'near'=2] {'core'}, dimensions={0}, use_global_device_ids=true | all-gather | bytes 147456 | tf_op jit(solution)/shard_map/all_gather | solution.py:54
  128.3 0.2 fusion.11
  128.5 0.2 fusion.1
  128.8 0.1 reshape.20
  128.9 19.8 %all_to_all.22 = bf16[48,2,1024]{2,1,0:T(2,128)(2,1)S(1)} all-to-all(bf16[48,2,1024]{2,1,0:T(2,128)(2,1)S(1)} %reshape.20), channel_id=1, replica_groups=mesh['hi'=4,'core'=2,'yz'=24,'far'=2,'near'=2] {'yz','near'}, dimensions={0} | all-to-all | bytes 393216 | tf_op jit(solution)/shard_map/all_to_all | solution.py:56
  148.7 0.2 convert_reduce_fusion.2
  148.9 0.6 add_convert_fusion
  (11 shorter events, 0.2 us)
Async XLA Ops:
  0.0 1.2 copy-start.1
  1.2 3.5 %copy-start.3 = (bf16[2,1024]{1,0:T(2,128)(2,1)S(1)}, bf16[2,1024]{1,0:T(2,128)(2,1)}, u32[]{:S(2)}) copy-start(bf16[2,1024]{1,0:T(2,128)(2,1)} %param.5) | copy-start | bytes 12292
  1.2 22.2 %copy-start = (bf16[256,1024]{1,0:T(8,128)(2,1)S(1)}, bf16[256,1024]{1,0:T(8,128)(2,1)}, u32[]{:S(2)}) copy-start(bf16[256,1024]{1,0:T(8,128)(2,1)} %param.9) | copy-start | bytes 1572868
  1.3 36.6 %collective-permute-start = (bf16[1024,512]{1,0:T(8,128)(2,1)S(1)}, bf16[1024,512]{1,0:T(8,128)(2,1)S(1)}, u32[]{:S(2)}, u32[]{:S(2)}) collective-permute-start(bf16[1024,512]{1,0:T(8,128)(2,1)S(1)} %constant_dynamic-update-slice_fusion), channel_id=1, source_target_pairs={{0,2},{2,0},{1,3},{3,1},{4,6},{6,4},{5,7},{7,5},{8,10},{10,8},{9,1... | collective-permute-start | bytes 3145736 | tf_op jit(solution)/shard_map/ppermute | solution.py:25
  5.5 31.3 %all-to-all-start = ((bf16[48,2,1024]{2,1,0:T(2,128)(2,1)}), bf16[48,2,1024]{2,1,0:T(2,128)(2,1)S(1)}, u32[]{:S(2)}, u32[]{:S(2)}) async-start(bf16[48,2,1024]{2,1,0:T(2,128)(2,1)} %broadcast_in_dim.8), calls=%async_computation | async-start | bytes 393216 | tf_op jit(solution)/shard_map/all_to_all | solution.py:30
  23.5 36.9 %collective-permute-start.1 = (bf16[256,1024]{1,0:T(8,128)(2,1)S(1)}, bf16[256,1024]{1,0:T(8,128)(2,1)S(1)}, u32[]{:S(2)}, u32[]{:S(2)}) collective-permute-start(bf16[256,1024]{1,0:T(8,128)(2,1)S(1)} %copy-done), channel_id=1, source_target_pairs={{0,2},{2,0},{1,3},{3,1},{4,6},{6,4},{5,7},{7,5},{8,10},{10,8},{9,1... | collective-permute-start | bytes 1572872 | tf_op jit(solution)/shard_map/ppermute | solution.py:26
  36.9 0.7 copy-start.2

commit v7 on v4

--- a/solution.py
+++ b/solution.py
@@ -20,9 +20,16 @@
     total = rows * ring
     half = total // CORE
     core = lax.axis_index("core")
-    paired = jnp.concatenate([w_gate, w_up], axis=1)
-    far = lax.ppermute(paired, "lo", PAIR)
-    down_far = lax.ppermute(w_down, "lo", PAIR)
+    deep = w_down.shape[0]
+    block = jnp.zeros((feats, width + deep), w_gate.dtype)
+    block = lax.dynamic_update_slice(block, w_gate, (0, 0))
+    block = lax.dynamic_update_slice(block, w_up, (0, deep))
+    for stripe in range(feats // deep):
+        part = w_down[:, stripe * deep : (stripe + 1) * deep]
+        block = lax.dynamic_update_slice(block, part, (stripe * deep, width))
+    swapped = lax.ppermute(block, "lo", PAIR)
+    paired, far = block[:, :width], swapped[:, :width]
+    down_far = jnp.split(swapped[:, width:], feats // deep, axis=0)
     mixed = tokens
     for step in range(ITERS):
         spread = jnp.broadcast_to(mixed[None], (ring, rows, feats))
@@ -51,7 +58,9 @@
             up = share[:, base + near : base + width] * scale
             sides.append((jax.nn.silu(gate) * up).astype(jnp.bfloat16))
         hidden = lax.all_gather(jnp.concatenate(sides, axis=1), "core", axis=0, tiled=True)
-        delta = matmul(hidden[:, :near], w_down) + matmul(hidden[:, near:], down_far)
+        delta = matmul(hidden[:, :near], w_down) + jnp.concatenate(
+            [matmul(hidden[:, near:], stripe) for stripe in down_far], axis=1
+        )
         deltas = lax.all_to_all(delta.astype(jnp.bfloat16).reshape(ring, rows, feats), "ring", 0, 0)
         mixed = (
             mixed.astype(jnp.float32) + jnp.sum(deltas.astype(jnp.float32), axis=0)

time: 154 us -> 163 us (1.058)
  blocking collectives: 109 us -> 115 us
  waiting for transfers between devices: 11.1 us -> 14.8 us
  starting transfers between devices: 24.4 us -> 21.9 us
    all_to_all x2, blocking collectives: 48 us -> 53.2 us  [on_device(): lax.all_to_all(delta.astype(jnp.bfloat16).reshape(ring, rows, feats), 'ri...]
    ppermute x2 -> x1, starting transfers between devices: 5.97 us -> 3.48 us  [on_device(): swapped = lax.ppermute(block, 'lo', PAIR)]
    all_to_all x1, waiting for transfers between devices: 11.1 us -> 13.4 us  [on_device(): everyone = lax.all_to_all(spread, 'ring', 0, 0)]
    unnamed x9 -> x12, local copies, waits for them, and re-layouts: 1.75 us -> 0.09 us
  transfers between devices with their start and end apart: 3 -> 2, of which waited for: 1 -> 2; matrix products, arithmetic and copies ran while one was open for 1% -> 1% of each run, Pallas kernels for 0% -> 0%
where the time goes in v7:
time: 163 us; the launch traced here: 160 us
  blocking collectives  115 us (71%)
  starting transfers between devices  21.9 us (13%)
  waiting for transfers between devices  14.8 us (9%)
  matrix products  2.92 us (2%)
  local copies, waits for them, and re-layouts  2.76 us (2%)
  other arithmetic  1.93 us (1%)
    all_to_all x2, blocking collectives, on_device(): lax.all_to_all(delta.astype(jnp.bfloat16).reshape(ring, rows, feats), 'ri...  53.2 us
    all_gather x2, blocking collectives, on_device(): lax.all_gather(chip, 'hi', axis=0).astype(jnp.float32)  34.5 us
    all_to_all x1, blocking collectives, on_device(): everyone = lax.all_to_all(spread, 'ring', 0, 0)  19.7 us
    all_to_all x1, starting transfers between devices, on_device(): everyone = lax.all_to_all(spread, 'ring', 0, 0)  18.4 us
    all_to_all x1, waiting for transfers between devices, on_device(): everyone = lax.all_to_all(spread, 'ring', 0, 0)  13.4 us
    all_gather x2, blocking collectives, on_device(): both = lax.all_gather(packed, 'core', axis=0)  4.25 us
    all_gather x2, blocking collectives, on_device(): lax.all_gather(jnp.concatenate(sides, axis=1), 'core', axis=0, tiled=True)  3.75 us
    ppermute x1, starting transfers between devices, on_device(): swapped = lax.ppermute(block, 'lo', PAIR)  3.48 us
  transfers between devices with their start and end apart: 2, of which 2 were waited for; matrix products, arithmetic and copies ran while one was open for 1% of the time, Pallas kernels for 0%

profile of v7, /device:TPU:6, one launch (start us, length us, event | category | flops | bytes accessed | tf_op | source)
XLA Modules:
  0.0 160.0 jit_solution(8016268364935184772)
XLA Ops:
  0.0 1.2 dynamic_update_slice.18
  1.3 0.0 copy-done.1
  1.5 3.5 %collective-permute-start = (bf16[1024,768]{1,0:T(8,128)(2,1)S(1)}, bf16[1024,768]{1,0:T(8,128)(2,1)S(1)}, u32[]{:S(2)}, u32[]{:S(2)}) collective-permute-start(bf16[1024,768]{1,0:T(8,128)(2,1)S(1)} %slice_dynamic-update-slice_fusion), channel_id=1, source_target_pairs={{0,48},{48,0},{1,49},{49,1},{2,50},{50,2},{3,51},{51,3},{4,52},{52... | collective-permute-start | bytes 4718600 | tf_op jit(solution)/shard_map/ppermute | solution.py:30
  5.0 0.8 broadcast_in_dim.8
  5.7 18.4 %all-to-all-start = ((bf16[48,2,1024]{2,1,0:T(2,128)(2,1)}), bf16[48,2,1024]{2,1,0:T(2,128)(2,1)S(1)}, u32[]{:S(2)}, u32[]{:S(2)}) async-start(bf16[48,2,1024]{2,1,0:T(2,128)(2,1)} %broadcast_in_dim.8), calls=%async_computation | async-start | bytes 393216 | tf_op jit(solution)/shard_map/all_to_all | solution.py:36
  24.2 13.4 %all-to-all-done = bf16[48,2,1024]{2,1,0:T(2,128)(2,1)S(1)} async-done(((bf16[48,2,1024]{2,1,0:T(2,128)(2,1)}), bf16[48,2,1024]{2,1,0:T(2,128)(2,1)S(1)}, u32[]{:S(2)}, u32[]{:S(2)}) %all-to-all-start) | async-done | bytes 196640 | tf_op jit(solution)/shard_map/all_to_all | solution.py:36
  37.6 0.1 reshape.17
  37.7 0.1 fusion.5
  37.8 0.3 convolution_convert_fusion.3
  38.1 1.4 collective-permute-done
  39.5 0.3 convolution_convert_fusion.2
  39.8 0.1 broadcast_in_dim.9
  39.9 2.1 %all-gather = bf16[192,1152]{1,0:T(8,128)(2,1)S(1)} all-gather(bf16[96,1152]{1,0:T(8,128)(2,1)S(1)} %pad_maximum_fusion), channel_id=2, replica_groups=mesh['hi'=4,'core'=2,'lo'=2,'ring'=48] {'core'}, dimensions={0}, use_global_device_ids=true | all-gather | bytes 663552 | tf_op jit(solution)/shard_map/all_gather | solution.py:49
  42.1 19.1 %all-gather.1 = bf16[192,1152]{1,0:T(8,128)(2,1)S(1)} all-gather(bf16[48,1152]{1,0:T(8,128)(2,1)S(1)} %dynamic-slice_reduce_fusion.1), channel_id=3, replica_groups=mesh['hi'=4,'core'=2,'lo'=2,'ring'=48] {'hi'}, dimensions={0}, use_global_device_ids=true | all-gather | bytes 552960 | tf_op jit(solution)/shard_map/all_gather | solution.py:52
  61.1 0.1 convert_reduce_fusion.1
  61.2 0.1 fusion.59
  61.3 0.1 fusion.45
  61.5 1.9 %all_gather.34 = bf16[96,512]{1,0:T(8,128)(2,1)S(1)} all-gather(bf16[48,512]{1,0:T(8,128)(2,1)S(1)} %pad_maximum_fusion.2), channel_id=1, replica_groups=mesh['hi'=4,'core'=2,'lo'=2,'ring'=48] {'core'}, dimensions={0}, use_global_device_ids=true | all-gather | bytes 147456 | tf_op jit(solution)/shard_map/all_gather | solution.py:60
  63.3 0.1 fusion.24
  63.5 0.2 fusion.20
  63.6 0.2 fusion.16
  63.8 0.2 fusion.28
  64.0 0.2 fusion.8
  64.2 0.1 reshape.18
  64.3 32.4 %all_to_all.20 = bf16[48,2,1024]{2,1,0:T(2,128)(2,1)S(1)} all-to-all(bf16[48,2,1024]{2,1,0:T(2,128)(2,1)S(1)} %reshape.18), channel_id=1, replica_groups=mesh['hi'=4,'core'=2,'lo'=2,'ring'=48] {'ring'}, dimensions={0} | all-to-all | bytes 393216 | tf_op jit(solution)/shard_map/all_to_all | solution.py:64
  96.7 0.2 convert_reduce_fusion.3
  96.9 0.1 broadcast_in_dim.10
  97.0 19.7 %all_to_all.21 = bf16[48,2,1024]{2,1,0:T(2,128)(2,1)S(1)} all-to-all(bf16[48,2,1024]{2,1,0:T(2,128)(2,1)S(1)} %broadcast_in_dim.10), channel_id=1, replica_groups=mesh['hi'=4,'core'=2,'lo'=2,'ring'=48] {'ring'}, dimensions={0} | all-to-all | bytes 393216 | tf_op jit(solution)/shard_map/all_to_all | solution.py:36
  116.7 0.1 reshape.19
  116.8 0.3 convolution_convert_fusion.1
  117.1 0.1 fusion.7
  117.2 0.3 convolution_convert_fusion
  117.5 0.1 broadcast_in_dim.11
  117.6 2.1 %all-gather.2 = bf16[192,1152]{1,0:T(8,128)(2,1)S(1)} all-gather(bf16[96,1152]{1,0:T(8,128)(2,1)S(1)} %pad_maximum_fusion.1), channel_id=4, replica_groups=mesh['hi'=4,'core'=2,'lo'=2,'ring'=48] {'core'}, dimensions={0}, use_global_device_ids=true | all-gather | bytes 663552 | tf_op jit(solution)/shard_map/all_gather | solution.py:49
  119.8 15.4 %all-gather.3 = bf16[192,1152]{1,0:T(8,128)(2,1)S(1)} all-gather(bf16[48,1152]{1,0:T(8,128)(2,1)S(1)} %dynamic-slice_reduce_fusion), channel_id=5, replica_groups=mesh['hi'=4,'core'=2,'lo'=2,'ring'=48] {'hi'}, dimensions={0}, use_global_device_ids=true | all-gather | bytes 552960 | tf_op jit(solution)/shard_map/all_gather | solution.py:52
  135.3 0.1 convert_reduce_fusion
  135.3 0.1 fusion.56
  135.4 0.1 fusion.37
  135.6 1.9 %all_gather.39 = bf16[96,512]{1,0:T(8,128)(2,1)S(1)} all-gather(bf16[48,512]{1,0:T(8,128)(2,1)S(1)} %pad_maximum_fusion.3), channel_id=1, replica_groups=mesh['hi'=4,'core'=2,'lo'=2,'ring'=48] {'core'}, dimensions={0}, use_global_device_ids=true | all-gather | bytes 147456 | tf_op jit(solution)/shard_map/all_gather | solution.py:60
  137.5 0.1 fusion.22
  137.6 0.2 fusion.18
  137.8 0.2 fusion.14
  137.9 0.2 fusion.26
  138.1 0.2 fusion.9
  138.3 0.1 reshape.20
  138.4 20.8 %all_to_all.22 = bf16[48,2,1024]{2,1,0:T(2,128)(2,1)S(1)} all-to-all(bf16[48,2,1024]{2,1,0:T(2,128)(2,1)S(1)} %reshape.20), channel_id=1, replica_groups=mesh['hi'=4,'core'=2,'lo'=2,'ring'=48] {'ring'}, dimensions={0} | all-to-all | bytes 393216 | tf_op jit(solution)/shard_map/all_to_all | solution.py:64
  159.2 0.2 convert_reduce_fusion.2
  159.4 0.6 add_convert_fusion
  (23 shorter events, 0.3 us)
Async XLA Ops:
  0.0 1.2 copy-start
  0.0 1.4 copy-start.1
  1.2 3.7 %copy-start.4 = (bf16[2,1024]{1,0:T(2,128)(2,1)S(1)}, bf16[2,1024]{1,0:T(2,128)(2,1)}, u32[]{:S(2)}) copy-start(bf16[2,1024]{1,0:T(2,128)(2,1)} %param.5) | copy-start | bytes 12292
  1.3 36.6 %copy-start.5 = (f32[1024]{0:T(1024)S(1)}, f32[1024]{0:T(1024)}, u32[]{:S(2)}) copy-start(f32[1024]{0:T(1024)} %param.6) | copy-start | bytes 12292
  1.5 38.0 %collective-permute-start = (bf16[1024,768]{1,0:T(8,128)(2,1)S(1)}, bf16[1024,768]{1,0:T(8,128)(2,1)S(1)}, u32[]{:S(2)}, u32[]{:S(2)}) collective-permute-start(bf16[1024,768]{1,0:T(8,128)(2,1)S(1)} %slice_dynamic-update-slice_fusion), channel_id=1, source_target_pairs={{0,48},{48,0},{1,49},{49,1},{2,50},{50,2},{3,51},{51,3},{4,52},{52... | collective-permute-start | bytes 4718600 | tf_op jit(solution)/shard_map/ppermute | solution.py:30
  5.7 31.9 %all-to-all-start = ((bf16[48,2,1024]{2,1,0:T(2,128)(2,1)}), bf16[48,2,1024]{2,1,0:T(2,128)(2,1)S(1)}, u32[]{:S(2)}, u32[]{:S(2)}) async-start(bf16[48,2,1024]{2,1,0:T(2,128)(2,1)} %broadcast_in_dim.8), calls=%async_computation | async-start | bytes 393216 | tf_op jit(solution)/shard_map/all_to_all | solution.py:36
  42.0 21.9 %copy-start.2 = (bf16[256,1024]{1,0:T(8,128)(2,1)S(1)}, bf16[256,1024]{1,0:T(8,128)(2,1)}, u32[]{:S(2)}) copy-start(bf16[256,1024]{1,0:T(8,128)(2,1)} %param.9) | copy-start | bytes 1572868
  119.8 18.3 %copy-start.3 = (bf16[256,1024]{1,0:T(8,128)(2,1)S(1)}, bf16[256,1024]{1,0:T(8,128)(2,1)}, u32[]{:S(2)}) copy-start(bf16[256,1024]{1,0:T(8,128)(2,1)} %param.9) | copy-start | bytes 1572868

commit v8 on v6

--- a/solution.py
+++ b/solution.py
@@ -23,12 +23,16 @@
     core = lax.axis_index("core")
     paired = jnp.concatenate([w_gate, w_up], axis=1)
     far = lax.ppermute(paired, "far", PAIR)
-    down_far = lax.ppermute(w_down, "far", PAIR)
+    down_far = None
     mixed = tokens
     for step in range(ITERS):
         spread = jnp.broadcast_to(mixed[None], (ring, rows, feats))
         everyone = lax.all_to_all(spread, RING, 0, 0)
-        everyone = lax.optimization_barrier(everyone.reshape(total, feats))
+        if step == 0:
+            everyone, later = lax.optimization_barrier((everyone.reshape(total, feats), w_down))
+            down_far = lax.ppermute(later, "far", PAIR)
+        else:
+            everyone = lax.optimization_barrier(everyone.reshape(total, feats))
         wide = everyone.astype(jnp.float32)
         squares = jnp.sum(wide * wide, axis=1, keepdims=True)
         gained = (wide * norm_gain).astype(jnp.bfloat16)

time: 151 us -> 153 us (1.013)
  waiting for transfers between devices: 9.3 us -> 13.4 us
    all_to_all x1, waiting for transfers between devices: 9.3 us -> 13.3 us  [on_device(): everyone = lax.all_to_all(spread, RING, 0, 0)]
where the time goes in v8:
time: 153 us; the launch traced here: 152 us
  blocking collectives  107 us (70%)
  starting transfers between devices  25.4 us (17%)
  waiting for transfers between devices  13.4 us (9%)
  local copies, waits for them, and re-layouts  2.58 us (2%)
  matrix products  2.12 us (1%)
  other arithmetic  1.93 us (1%)
    all_to_all x2, blocking collectives, on_device(): lax.all_to_all(delta.astype(jnp.bfloat16).reshape(ring, rows, feats), RIN...  46.9 us
    all_gather x2, blocking collectives, on_device(): lax.all_gather(chip, 'hi', axis=0).astype(jnp.float32)  33.4 us
    all_to_all x1, blocking collectives, on_device(): everyone = lax.all_to_all(spread, RING, 0, 0)  18.4 us
    all_to_all x1, starting transfers between devices, on_device(): everyone = lax.all_to_all(spread, RING, 0, 0)  18 us
    all_to_all x1, waiting for transfers between devices, on_device(): everyone = lax.all_to_all(spread, RING, 0, 0)  13.3 us
    all_gather x2, blocking collectives, on_device(): both = lax.all_gather(packed, 'core', axis=0)  4.25 us
    ppermute x1, starting transfers between devices, on_device(): down_far = lax.ppermute(later, 'far', PAIR)  4.03 us
    all_gather x2, blocking collectives, on_device(): lax.all_gather(jnp.concatenate(sides, axis=1), 'core', axis=0, tiled=True)  3.75 us
  transfers between devices with their start and end apart: 3, of which 1 were waited for; matrix products, arithmetic and copies ran while one was open for 1% of the time, Pallas kernels for 0%

profile of v8, /device:TPU:6, one launch (start us, length us, event | category | flops | bytes accessed | tf_op | source)
XLA Modules:
  0.0 152.3 jit_solution(10449025103639733822)
XLA Ops:
  0.0 1.1 constant_dynamic-update-slice_fusion.1
  1.1 0.1 copy-done.1
  1.2 0.0 copy-start
  1.3 3.4 %collective-permute-start = (bf16[1024,512]{1,0:T(8,128)(2,1)S(1)}, bf16[1024,512]{1,0:T(8,128)(2,1)S(1)}, u32[]{:S(2)}, u32[]{:S(2)}) collective-permute-start(bf16[1024,512]{1,0:T(8,128)(2,1)S(1)} %constant_dynamic-update-slice_fusion), channel_id=1, source_target_pairs={{0,2},{2,0},{1,3},{3,1},{4,6},{6,4},{5,7},{7,5},{8,10},{10,8},{9,1... | collective-permute-start | bytes 3145736 | tf_op jit(solution)/shard_map/ppermute | solution.py:25
  4.7 0.0 copy-done.3
  4.7 0.8 broadcast_in_dim.8
  5.5 18.0 %all-to-all-start = ((bf16[48,2,1024]{2,1,0:T(2,128)(2,1)}), bf16[48,2,1024]{2,1,0:T(2,128)(2,1)S(1)}, u32[]{:S(2)}, u32[]{:S(2)}) async-start(bf16[48,2,1024]{2,1,0:T(2,128)(2,1)} %broadcast_in_dim.8), calls=%async_computation | async-start | bytes 393216 | tf_op jit(solution)/shard_map/all_to_all | solution.py:30
  23.5 13.3 %all-to-all-done = bf16[48,2,1024]{2,1,0:T(2,128)(2,1)S(1)} async-done(((bf16[48,2,1024]{2,1,0:T(2,128)(2,1)}), bf16[48,2,1024]{2,1,0:T(2,128)(2,1)S(1)}, u32[]{:S(2)}, u32[]{:S(2)}) %all-to-all-start) | async-done | bytes 196640 | tf_op jit(solution)/shard_map/all_to_all | solution.py:30
  36.8 0.1 reshape.17
  36.9 0.0 copy-done
  36.9 0.0 copy-start.2
  36.9 4.0 %collective-permute-start.1 = (bf16[256,1024]{1,0:T(8,128)(2,1)S(1)}, bf16[256,1024]{1,0:T(8,128)(2,1)S(1)}, u32[]{:S(2)}, u32[]{:S(2)}) collective-permute-start(bf16[256,1024]{1,0:T(8,128)(2,1)S(1)} %copy-done), channel_id=1, source_target_pairs={{0,2},{2,0},{1,3},{3,1},{4,6},{6,4},{5,7},{7,5},{8,10},{10,8},{9,1... | collective-permute-start | bytes 1572872 | tf_op jit(solution)/shard_map/ppermute | solution.py:33
  41.0 0.1 fusion.3
  41.1 0.3 convolution_convert_fusion.3
  41.4 0.0 collective-permute-done
  41.4 0.3 convolution_convert_fusion.2
  41.7 0.1 broadcast_in_dim.9
  41.8 2.1 %all-gather = bf16[192,1152]{1,0:T(8,128)(2,1)S(1)} all-gather(bf16[96,1152]{1,0:T(8,128)(2,1)S(1)} %pad_maximum_fusion), channel_id=2, replica_groups=mesh['hi'=4,'core'=2,'yz'=24,'far'=2,'near'=2] {'core'}, dimensions={0}, use_global_device_ids=true | all-gather | bytes 663552 | tf_op jit(solution)/shard_map/all_gather | solution.py:47
  44.0 17.2 %all-gather.1 = bf16[192,1152]{1,0:T(8,128)(2,1)S(1)} all-gather(bf16[48,1152]{1,0:T(8,128)(2,1)S(1)} %dynamic-slice_reduce_fusion.1), channel_id=3, replica_groups=mesh['hi'=4,'core'=2,'yz'=24,'far'=2,'near'=2] {'hi'}, dimensions={0}, use_global_device_ids=true | all-gather | bytes 552960 | tf_op jit(solution)/shard_map/all_gather | solution.py:50
  61.2 0.1 convert_reduce_fusion.1
  61.3 0.1 fusion.29
  61.4 0.1 fusion.23
  61.5 1.9 %all_gather.34 = bf16[96,512]{1,0:T(8,128)(2,1)S(1)} all-gather(bf16[48,512]{1,0:T(8,128)(2,1)S(1)} %pad_maximum_fusion.2), channel_id=1, replica_groups=mesh['hi'=4,'core'=2,'yz'=24,'far'=2,'near'=2] {'core'}, dimensions={0}, use_global_device_ids=true | all-gather | bytes 147456 | tf_op jit(solution)/shard_map/all_gather | solution.py:58
  63.4 0.2 fusion.18
  63.6 0.0 collective-permute-done.1
  63.6 0.2 fusion
  63.8 0.1 reshape.18
  63.9 27.0 %all_to_all.20 = bf16[48,2,1024]{2,1,0:T(2,128)(2,1)S(1)} all-to-all(bf16[48,2,1024]{2,1,0:T(2,128)(2,1)S(1)} %reshape.18), channel_id=1, replica_groups=mesh['hi'=4,'core'=2,'yz'=24,'far'=2,'near'=2] {'yz','near'}, dimensions={0} | all-to-all | bytes 393216 | tf_op jit(solution)/shard_map/all_to_all | solution.py:60
  91.0 0.2 convert_reduce_fusion.3
  91.2 0.1 broadcast_in_dim.10
  91.3 18.4 %all_to_all.21 = bf16[48,2,1024]{2,1,0:T(2,128)(2,1)S(1)} all-to-all(bf16[48,2,1024]{2,1,0:T(2,128)(2,1)S(1)} %broadcast_in_dim.10), channel_id=1, replica_groups=mesh['hi'=4,'core'=2,'yz'=24,'far'=2,'near'=2] {'yz','near'}, dimensions={0} | all-to-all | bytes 393216 | tf_op jit(solution)/shard_map/all_to_all | solution.py:30
  109.7 0.1 reshape.19
  109.8 0.3 convolution_convert_fusion.1
  110.1 0.1 fusion.5
  110.2 0.3 convolution_convert_fusion
  110.5 0.1 broadcast_in_dim.11
  110.6 2.1 %all-gather.2 = bf16[192,1152]{1,0:T(8,128)(2,1)S(1)} all-gather(bf16[96,1152]{1,0:T(8,128)(2,1)S(1)} %pad_maximum_fusion.1), channel_id=4, replica_groups=mesh['hi'=4,'core'=2,'yz'=24,'far'=2,'near'=2] {'core'}, dimensions={0}, use_global_device_ids=true | all-gather | bytes 663552 | tf_op jit(solution)/shard_map/all_gather | solution.py:47
  112.8 16.2 %all-gather.3 = bf16[192,1152]{1,0:T(8,128)(2,1)S(1)} all-gather(bf16[48,1152]{1,0:T(8,128)(2,1)S(1)} %dynamic-slice_reduce_fusion), channel_id=5, replica_groups=mesh['hi'=4,'core'=2,'yz'=24,'far'=2,'near'=2] {'hi'}, dimensions={0}, use_global_device_ids=true | all-gather | bytes 552960 | tf_op jit(solution)/shard_map/all_gather | solution.py:50
  128.9 0.1 convert_reduce_fusion
  129.0 0.1 fusion.26
  129.1 0.1 fusion.16
  129.3 1.9 %all_gather.39 = bf16[96,512]{1,0:T(8,128)(2,1)S(1)} all-gather(bf16[48,512]{1,0:T(8,128)(2,1)S(1)} %pad_maximum_fusion.3), channel_id=1, replica_groups=mesh['hi'=4,'core'=2,'yz'=24,'far'=2,'near'=2] {'core'}, dimensions={0}, use_global_device_ids=true | all-gather | bytes 147456 | tf_op jit(solution)/shard_map/all_gather | solution.py:58
  131.1 0.2 fusion.11
  131.4 0.2 fusion.1
  131.6 0.1 reshape.20
  131.7 19.8 %all_to_all.22 = bf16[48,2,1024]{2,1,0:T(2,128)(2,1)S(1)} all-to-all(bf16[48,2,1024]{2,1,0:T(2,128)(2,1)S(1)} %reshape.20), channel_id=1, replica_groups=mesh['hi'=4,'core'=2,'yz'=24,'far'=2,'near'=2] {'yz','near'}, dimensions={0} | all-to-all | bytes 393216 | tf_op jit(solution)/shard_map/all_to_all | solution.py:60
  151.5 0.2 convert_reduce_fusion.2
  151.7 0.6 add_convert_fusion
  (11 shorter events, 0.2 us)
Async XLA Ops:
  0.0 1.2 copy-start.1
  1.2 3.5 %copy-start.3 = (bf16[2,1024]{1,0:T(2,128)(2,1)S(1)}, bf16[2,1024]{1,0:T(2,128)(2,1)}, u32[]{:S(2)}) copy-start(bf16[2,1024]{1,0:T(2,128)(2,1)} %param.5) | copy-start | bytes 12292
  1.2 35.6 %copy-start = (bf16[256,1024]{1,0:T(8,128)(2,1)S(1)}, bf16[256,1024]{1,0:T(8,128)(2,1)}, u32[]{:S(2)}) copy-start(bf16[256,1024]{1,0:T(8,128)(2,1)} %param.9) | copy-start | bytes 1572868
  1.3 40.1 %collective-permute-start = (bf16[1024,512]{1,0:T(8,128)(2,1)S(1)}, bf16[1024,512]{1,0:T(8,128)(2,1)S(1)}, u32[]{:S(2)}, u32[]{:S(2)}) collective-permute-start(bf16[1024,512]{1,0:T(8,128)(2,1)S(1)} %constant_dynamic-update-slice_fusion), channel_id=1, source_target_pairs={{0,2},{2,0},{1,3},{3,1},{4,6},{6,4},{5,7},{7,5},{8,10},{10,8},{9,1... | collective-permute-start | bytes 3145736 | tf_op jit(solution)/shard_map/ppermute | solution.py:25
  5.5 31.3 %all-to-all-start = ((bf16[48,2,1024]{2,1,0:T(2,128)(2,1)}), bf16[48,2,1024]{2,1,0:T(2,128)(2,1)S(1)}, u32[]{:S(2)}, u32[]{:S(2)}) async-start(bf16[48,2,1024]{2,1,0:T(2,128)(2,1)} %broadcast_in_dim.8), calls=%async_computation | async-start | bytes 393216 | tf_op jit(solution)/shard_map/all_to_all | solution.py:30
  36.9 4.2 %copy-start.2 = (f32[1024]{0:T(1024)S(1)}, f32[1024]{0:T(1024)}, u32[]{:S(2)}) copy-start(f32[1024]{0:T(1024)} %param.6) | copy-start | bytes 12292
  36.9 26.7 %collective-permute-start.1 = (bf16[256,1024]{1,0:T(8,128)(2,1)S(1)}, bf16[256,1024]{1,0:T(8,128)(2,1)S(1)}, u32[]{:S(2)}, u32[]{:S(2)}) collective-permute-start(bf16[256,1024]{1,0:T(8,128)(2,1)S(1)} %copy-done), channel_id=1, source_target_pairs={{0,2},{2,0},{1,3},{3,1},{4,6},{6,4},{5,7},{7,5},{8,10},{10,8},{9,1... | collective-permute-start | bytes 1572872 | tf_op jit(solution)/shard_map/ppermute | solution.py:33

commit v9 on v4

--- a/solution.py
+++ b/solution.py
@@ -5,7 +5,8 @@
 
 D = 8192
 ITERS = 2
-HI, CORE, LO = 4, 2, 2
+HI, CORE, LO, FAR, NEAR = 4, 2, 2, 2, 2
+RING = ("near", "z", "far")
 PAIR = ((0, 1), (1, 0))
 
 
@@ -16,7 +17,7 @@
 def on_device(tokens, norm_gain, w_gate, w_up, w_down):
     width = 2 * w_gate.shape[1]
     rows, feats = tokens.shape
-    ring = lax.axis_size("ring")
+    ring = lax.axis_size(RING)
     total = rows * ring
     half = total // CORE
     core = lax.axis_index("core")
@@ -26,7 +27,7 @@
     mixed = tokens
     for step in range(ITERS):
         spread = jnp.broadcast_to(mixed[None], (ring, rows, feats))
-        everyone = lax.all_to_all(spread, "ring", 0, 0)
+        everyone = lax.all_to_all(spread, RING, 0, 0)
         everyone = lax.optimization_barrier(everyone.reshape(total, feats))
         wide = everyone.astype(jnp.float32)
         squares = jnp.sum(wide * wide, axis=1, keepdims=True)
@@ -52,7 +53,7 @@
             sides.append((jax.nn.silu(gate) * up).astype(jnp.bfloat16))
         hidden = lax.all_gather(jnp.concatenate(sides, axis=1), "core", axis=0, tiled=True)
         delta = matmul(hidden[:, :near], w_down) + matmul(hidden[:, near:], down_far)
-        deltas = lax.all_to_all(delta.astype(jnp.bfloat16).reshape(ring, rows, feats), "ring", 0, 0)
+        deltas = lax.all_to_all(delta.astype(jnp.bfloat16).reshape(ring, rows, feats), RING, 0, 0)
         mixed = (
             mixed.astype(jnp.float32) + jnp.sum(deltas.astype(jnp.float32), axis=0)
         ).astype(jnp.bfloat16)
@@ -60,9 +61,9 @@
 
 
 def solution(mesh):
-    ring = mesh.shape["col"] // LO
-    fine = Mesh(mesh.devices.reshape(HI, CORE, LO, ring), ("hi", "core", "lo", "ring"))
-    row, col = ("hi", "core"), ("lo", "ring")
+    depth = mesh.shape["col"] // (LO * FAR * NEAR)
+    fine = Mesh(mesh.devices.reshape(HI, CORE, LO, depth, FAR, NEAR), ("hi", "core", "lo", "z", "far", "near"))
+    row, col = ("hi", "core"), ("lo", "z", "far", "near")
     return jax.shard_map(
         on_device,
         mesh=fine,

time: 154 us -> 152 us (0.987); the launches traced: 152 us -> 151 us
  no operation moved by 1% of the time
where the time goes in v9:
time: 152 us; the launch traced here: 151 us
  blocking collectives  109 us (72%)
  starting transfers between devices  24.4 us (16%)
  waiting for transfers between devices  11 us (7%)
  local copies, waits for them, and re-layouts  3.12 us (2%)
  matrix products  2.11 us (1%)
  other arithmetic  1.93 us (1%)
    all_to_all x2, blocking collectives, on_device(): lax.all_to_all(delta.astype(jnp.bfloat16).reshape(ring, rows, feats), RIN...  47.9 us
    all_gather x2, blocking collectives, on_device(): lax.all_gather(chip, 'hi', axis=0).astype(jnp.float32)  33.4 us
    all_to_all x1, blocking collectives, on_device(): everyone = lax.all_to_all(spread, RING, 0, 0)  19.2 us
    all_to_all x1, starting transfers between devices, on_device(): everyone = lax.all_to_all(spread, RING, 0, 0)  18.5 us
    all_to_all x1, waiting for transfers between devices, on_device(): everyone = lax.all_to_all(spread, RING, 0, 0)  11 us
    all_gather x2, blocking collectives, on_device(): both = lax.all_gather(packed, 'core', axis=0)  4.25 us
    all_gather x2, blocking collectives, on_device(): lax.all_gather(jnp.concatenate(sides, axis=1), 'core', axis=0, tiled=True)  3.75 us
    ppermute x1, starting transfers between devices, on_device(): far = lax.ppermute(paired, 'lo', PAIR)  3.62 us
  transfers between devices with their start and end apart: 3, of which 1 were waited for; matrix products, arithmetic and copies ran while one was open for 1% of the time, Pallas kernels for 0%

profile of v9, /device:TPU:6, one launch (start us, length us, event | category | flops | bytes accessed | tf_op | source)
XLA Modules:
  0.0 151.5 jit_solution(4839337572038515569)
XLA Ops:
  0.0 1.1 constant_dynamic-update-slice_fusion.1
  1.1 0.1 copy-done.1
  1.2 0.0 copy-start
  1.3 3.6 %collective-permute-start = (bf16[1024,512]{1,0:T(8,128)(2,1)S(1)}, bf16[1024,512]{1,0:T(8,128)(2,1)S(1)}, u32[]{:S(2)}, u32[]{:S(2)}) collective-permute-start(bf16[1024,512]{1,0:T(8,128)(2,1)S(1)} %constant_dynamic-update-slice_fusion), channel_id=1, source_target_pairs={{0,48},{48,0},{1,49},{49,1},{2,50},{50,2},{3,51},{51,3},{4,52},{52... | collective-permute-start | bytes 3145736 | tf_op jit(solution)/shard_map/ppermute | solution.py:25
  4.9 0.0 copy-done.3
  4.9 0.8 broadcast_in_dim.8
  5.7 18.5 %all-to-all-start = ((bf16[48,2,1024]{2,1,0:T(2,128)(2,1)}), bf16[48,2,1024]{2,1,0:T(2,128)(2,1)S(1)}, u32[]{:S(2)}, u32[]{:S(2)}) async-start(bf16[48,2,1024]{2,1,0:T(2,128)(2,1)} %broadcast_in_dim.8), calls=%async_computation | async-start | bytes 393216 | tf_op jit(solution)/shard_map/all_to_all | solution.py:30
  24.2 2.4 %collective-permute-start.1 = (bf16[256,1024]{1,0:T(8,128)(2,1)S(1)}, bf16[256,1024]{1,0:T(8,128)(2,1)S(1)}, u32[]{:S(2)}, u32[]{:S(2)}) collective-permute-start(bf16[256,1024]{1,0:T(8,128)(2,1)S(1)} %copy-done), channel_id=1, source_target_pairs={{0,48},{48,0},{1,49},{49,1},{2,50},{50,2},{3,51},{51,3},{4,52},{52... | collective-permute-start | bytes 1572872 | tf_op jit(solution)/shard_map/ppermute | solution.py:26
  26.5 11.0 %all-to-all-done = bf16[48,2,1024]{2,1,0:T(2,128)(2,1)S(1)} async-done(((bf16[48,2,1024]{2,1,0:T(2,128)(2,1)}), bf16[48,2,1024]{2,1,0:T(2,128)(2,1)S(1)}, u32[]{:S(2)}, u32[]{:S(2)}) %all-to-all-start) | async-done | bytes 196640 | tf_op jit(solution)/shard_map/all_to_all | solution.py:30
  37.5 0.1 reshape.17
  37.6 0.0 copy-start.2
  37.6 0.1 fusion.3
  37.8 0.5 copy-done.2
  38.3 0.3 convolution_convert_fusion.3
  38.6 0.0 collective-permute-done
  38.6 0.3 convolution_convert_fusion.2
  38.9 0.1 broadcast_in_dim.9
  39.0 2.1 %all-gather = bf16[192,1152]{1,0:T(8,128)(2,1)S(1)} all-gather(bf16[96,1152]{1,0:T(8,128)(2,1)S(1)} %pad_maximum_fusion), channel_id=2, replica_groups=mesh['hi'=4,'core'=2,'lo'=2,'z'=12,'far'=2,'near'=2] {'core'}, dimensions={0}, use_global_device_ids=true | all-gather | bytes 663552 | tf_op jit(solution)/shard_map/all_gather | solution.py:43
  41.2 17.3 %all-gather.1 = bf16[192,1152]{1,0:T(8,128)(2,1)S(1)} all-gather(bf16[48,1152]{1,0:T(8,128)(2,1)S(1)} %dynamic-slice_reduce_fusion.1), channel_id=3, replica_groups=mesh['hi'=4,'core'=2,'lo'=2,'z'=12,'far'=2,'near'=2] {'hi'}, dimensions={0}, use_global_device_ids=true | all-gather | bytes 552960 | tf_op jit(solution)/shard_map/all_gather | solution.py:46
  58.5 0.1 convert_reduce_fusion.1
  58.5 0.1 fusion.29
  58.6 0.1 fusion.23
  58.8 1.9 %all_gather.34 = bf16[96,512]{1,0:T(8,128)(2,1)S(1)} all-gather(bf16[48,512]{1,0:T(8,128)(2,1)S(1)} %pad_maximum_fusion.2), channel_id=1, replica_groups=mesh['hi'=4,'core'=2,'lo'=2,'z'=12,'far'=2,'near'=2] {'core'}, dimensions={0}, use_global_device_ids=true | all-gather | bytes 147456 | tf_op jit(solution)/shard_map/all_gather | solution.py:54
  60.6 0.2 fusion.18
  60.9 0.0 collective-permute-done.1
  60.9 0.2 fusion
  61.1 0.1 reshape.18
  61.2 27.0 %all_to_all.20 = bf16[48,2,1024]{2,1,0:T(2,128)(2,1)S(1)} all-to-all(bf16[48,2,1024]{2,1,0:T(2,128)(2,1)S(1)} %reshape.18), channel_id=1, replica_groups=mesh['hi'=4,'core'=2,'lo'=2,'z'=12,'far'=2,'near'=2] {'near','z','far'}, dimensions={0} | all-to-all | bytes 393216 | tf_op jit(solution)/shard_map/all_to_all | solution.py:56
  88.2 0.2 convert_reduce_fusion.3
  88.4 0.1 broadcast_in_dim.10
  88.5 19.2 %all_to_all.21 = bf16[48,2,1024]{2,1,0:T(2,128)(2,1)S(1)} all-to-all(bf16[48,2,1024]{2,1,0:T(2,128)(2,1)S(1)} %broadcast_in_dim.10), channel_id=1, replica_groups=mesh['hi'=4,'core'=2,'lo'=2,'z'=12,'far'=2,'near'=2] {'near','z','far'}, dimensions={0} | all-to-all | bytes 393216 | tf_op jit(solution)/shard_map/all_to_all | solution.py:30
  107.8 0.1 reshape.19
  107.8 0.3 convolution_convert_fusion.1
  108.1 0.1 fusion.5
  108.3 0.3 convolution_convert_fusion
  108.6 0.1 broadcast_in_dim.11
  108.7 2.1 %all-gather.2 = bf16[192,1152]{1,0:T(8,128)(2,1)S(1)} all-gather(bf16[96,1152]{1,0:T(8,128)(2,1)S(1)} %pad_maximum_fusion.1), channel_id=4, replica_groups=mesh['hi'=4,'core'=2,'lo'=2,'z'=12,'far'=2,'near'=2] {'core'}, dimensions={0}, use_global_device_ids=true | all-gather | bytes 663552 | tf_op jit(solution)/shard_map/all_gather | solution.py:43
  110.8 16.2 %all-gather.3 = bf16[192,1152]{1,0:T(8,128)(2,1)S(1)} all-gather(bf16[48,1152]{1,0:T(8,128)(2,1)S(1)} %dynamic-slice_reduce_fusion), channel_id=5, replica_groups=mesh['hi'=4,'core'=2,'lo'=2,'z'=12,'far'=2,'near'=2] {'hi'}, dimensions={0}, use_global_device_ids=true | all-gather | bytes 552960 | tf_op jit(solution)/shard_map/all_gather | solution.py:46
  127.0 0.1 convert_reduce_fusion
  127.1 0.1 fusion.26
  127.2 0.1 fusion.16
  127.3 1.9 %all_gather.39 = bf16[96,512]{1,0:T(8,128)(2,1)S(1)} all-gather(bf16[48,512]{1,0:T(8,128)(2,1)S(1)} %pad_maximum_fusion.3), channel_id=1, replica_groups=mesh['hi'=4,'core'=2,'lo'=2,'z'=12,'far'=2,'near'=2] {'core'}, dimensions={0}, use_global_device_ids=true | all-gather | bytes 147456 | tf_op jit(solution)/shard_map/all_gather | solution.py:54
  129.2 0.2 fusion.11
  129.4 0.2 fusion.1
  129.7 0.1 reshape.20
  129.7 20.9 %all_to_all.22 = bf16[48,2,1024]{2,1,0:T(2,128)(2,1)S(1)} all-to-all(bf16[48,2,1024]{2,1,0:T(2,128)(2,1)S(1)} %reshape.20), channel_id=1, replica_groups=mesh['hi'=4,'core'=2,'lo'=2,'z'=12,'far'=2,'near'=2] {'near','z','far'}, dimensions={0} | all-to-all | bytes 393216 | tf_op jit(solution)/shard_map/all_to_all | solution.py:56
  150.7 0.2 convert_reduce_fusion.2
  150.9 0.6 add_convert_fusion
  (11 shorter events, 0.2 us)
Async XLA Ops:
  0.0 1.2 copy-start.1
  1.2 3.7 %copy-start.3 = (bf16[2,1024]{1,0:T(2,128)(2,1)S(1)}, bf16[2,1024]{1,0:T(2,128)(2,1)}, u32[]{:S(2)}) copy-start(bf16[2,1024]{1,0:T(2,128)(2,1)} %param.5) | copy-start | bytes 12292
  1.2 22.9 %copy-start = (bf16[256,1024]{1,0:T(8,128)(2,1)S(1)}, bf16[256,1024]{1,0:T(8,128)(2,1)}, u32[]{:S(2)}) copy-start(bf16[256,1024]{1,0:T(8,128)(2,1)} %param.9) | copy-start | bytes 1572868
  1.3 37.4 %collective-permute-start = (bf16[1024,512]{1,0:T(8,128)(2,1)S(1)}, bf16[1024,512]{1,0:T(8,128)(2,1)S(1)}, u32[]{:S(2)}, u32[]{:S(2)}) collective-permute-start(bf16[1024,512]{1,0:T(8,128)(2,1)S(1)} %constant_dynamic-update-slice_fusion), channel_id=1, source_target_pairs={{0,48},{48,0},{1,49},{49,1},{2,50},{50,2},{3,51},{51,3},{4,52},{52... | collective-permute-start | bytes 3145736 | tf_op jit(solution)/shard_map/ppermute | solution.py:25
  5.7 31.9 %all-to-all-start = ((bf16[48,2,1024]{2,1,0:T(2,128)(2,1)}), bf16[48,2,1024]{2,1,0:T(2,128)(2,1)S(1)}, u32[]{:S(2)}, u32[]{:S(2)}) async-start(bf16[48,2,1024]{2,1,0:T(2,128)(2,1)} %broadcast_in_dim.8), calls=%async_computation | async-start | bytes 393216 | tf_op jit(solution)/shard_map/all_to_all | solution.py:30
  24.2 36.7 %collective-permute-start.1 = (bf16[256,1024]{1,0:T(8,128)(2,1)S(1)}, bf16[256,1024]{1,0:T(8,128)(2,1)S(1)}, u32[]{:S(2)}, u32[]{:S(2)}) collective-permute-start(bf16[256,1024]{1,0:T(8,128)(2,1)S(1)} %copy-done), channel_id=1, source_target_pairs={{0,48},{48,0},{1,49},{49,1},{2,50},{50,2},{3,51},{51,3},{4,52},{52... | collective-permute-start | bytes 1572872 | tf_op jit(solution)/shard_map/ppermute | solution.py:26
  37.6 0.7 copy-start.2

commit v10 on v9

v10 whole, which is shorter than its diff:
```python
import jax
import jax.numpy as jnp
from jax import lax
from jax.sharding import Mesh, PartitionSpec as P

D = 8192
ITERS = 2
HI, CORE, LO, FAR, NEAR = 4, 2, 2, 2, 2
RING = ("near", "z", "far")
PAIR = ((0, 1), (1, 0))


def matmul(left, right):
    return jnp.dot(left, right, preferred_element_type=jnp.float32)


def partial_sums(rows_in, norm_gain, blocks):
    wide = rows_in.astype(jnp.float32)
    squares = jnp.sum(wide * wide, axis=1, keepdims=True)
    gained = (wide * norm_gain).astype(jnp.bfloat16)
    parts = [matmul(gained, block).astype(jnp.bfloat16) for block in blocks]
    parts.append(jnp.broadcast_to(squares, (rows_in.shape[0], 128)).astype(jnp.bfloat16))
    return jnp.concatenate(parts, axis=1)


def hidden_units(packed, side):
    half = packed.shape[0] // CORE
    both = lax.all_gather(packed, "core", axis=0)
    mine = lax.dynamic_slice_in_dim(both, lax.axis_index("core") * half, half, axis=1)
    chip = jnp.sum(mine.astype(jnp.float32), axis=0).astype(jnp.bfloat16)
    share = jnp.sum(lax.all_gather(chip, "hi", axis=0).astype(jnp.float32), axis=0)
    last = share.shape[1] - 128
    scale = lax.rsqrt(share[:, last : last + 1] / D + 1e-05)
    units = []
    for base in range(0, last, 2 * side):
        gate = share[:, base : base + side] * scale
        up = share[:, base + side : base + 2 * side] * scale
        units.append((jax.nn.silu(gate) * up).astype(jnp.bfloat16))
    return jnp.concatenate(units, axis=1)


def on_device(tokens, norm_gain, w_gate, w_up, w_down):
    side = w_gate.shape[1]
    rows, feats = tokens.shape
    ring = lax.axis_size(RING)
    total = rows * ring
    lo = lax.axis_index("lo")
    paired = jnp.concatenate([w_gate, w_up], axis=1)
    down_far = lax.ppermute(w_down, "lo", PAIR)
    far = None
    mixed = tokens
    for step in range(ITERS):
        spread = jnp.broadcast_to(mixed[None], (ring, rows, feats))
        everyone = lax.all_to_all(spread, RING, 0, 0).reshape(total, feats)
        if step == 0:
            everyone = lax.optimization_barrier(lax.all_gather(everyone, "lo", axis=0, tiled=True))
            units = hidden_units(partial_sums(everyone, norm_gain, [paired]), side)
            blocks = lax.all_gather(units, ("core", "lo"), axis=0)
            near = lax.dynamic_index_in_dim(blocks, lo * LO + lo, 0, keepdims=False)
            other = lax.dynamic_index_in_dim(blocks, lo * LO + 1 - lo, 0, keepdims=False)
        else:
            everyone = lax.optimization_barrier(everyone)
            units = hidden_units(partial_sums(everyone, norm_gain, [paired, far]), side)
            hidden = lax.all_gather(units, "core", axis=0, tiled=True)
            near, other = hidden[:, :side], hidden[:, side:]
        delta = (matmul(near, w_down) + matmul(other, down_far)).astype(jnp.bfloat16)
        if step == 0:
            delta, later = lax.optimization_barrier((delta, paired))
            far = lax.ppermute(later, "lo", PAIR)
        deltas = lax.all_to_all(delta.reshape(ring, rows, feats), RING, 0, 0)
        mixed = (
            mixed.astype(jnp.float32) + jnp.sum(deltas.astype(jnp.float32), axis=0)
        ).astype(jnp.bfloat16)
    return mixed


def solution(mesh):
    depth = mesh.shape["col"] // (LO * FAR * NEAR)
    fine = Mesh(mesh.devices.reshape(HI, CORE, LO, depth, FAR, NEAR), ("hi", "core", "lo", "z", "far", "near"))
    row, col = ("hi", "core"), ("lo", "z", "far", "near")
    return jax.shard_map(
        on_device,
        mesh=fine,
        in_specs=(P(col, row), P(row), P(row, col), P(row, col), P(col, row)),
        out_specs=P(col, row),
        check_vma=False,
    )
```

time: 152 us -> 164 us (1.079)
  blocking collectives: 109 us -> 78.4 us
  waiting for transfers between devices: 11 us -> 33.8 us
  starting transfers between devices: 24.4 us -> 42.2 us
  local copies, waits for them, and re-layouts: 3.12 us -> 5.2 us
    all_to_all x3 -> x1, blocking collectives: 67.2 us -> 21.7 us  [on_device(): deltas = lax.all_to_all(delta.reshape(ring, rows, feats), RING, 0, 0)]
    all_to_all x1 -> x3, waiting for transfers between devices: 11 us -> 33.8 us  [the longest x2 21.7 us: on_device(): everyone = lax.all_to_all(spread, RING, 0, 0).reshape(total, feats)]
    all_to_all x1 -> x3, starting transfers between devices: 18.5 us -> 36.8 us  [the longest x2 25 us: on_device(): everyone = lax.all_to_all(spread, RING, 0, 0).reshape(total, feats)]
    all_gather x6 -> x7, blocking collectives: 41.4 us -> 56.8 us  [the longest x2 34.2 us: hidden_units(): lax.all_gather(chip, 'hi', axis=0).astype(jnp.float32)]
    ppermute x1, starting transfers between devices: 3.62 us -> 1.92 us  [on_device(): far = lax.ppermute(later, 'lo', PAIR)]
  transfers between devices with their start and end apart: 3 -> 5, of which waited for: 1 -> 3; matrix products, arithmetic and copies ran while one was open for 1% -> 2% of each run, Pallas kernels for 0% -> 0%
where the time goes in v10:
time: 164 us
  blocking collectives  78.4 us (48%)
  starting transfers between devices  42.2 us (26%)
  waiting for transfers between devices  33.8 us (21%)
  local copies, waits for them, and re-layouts  5.2 us (3%)
  other arithmetic  1.96 us (1%)
  matrix products  1.9 us (1%)
    all_gather x2, blocking collectives, hidden_units(): lax.all_gather(chip, 'hi', axis=0).astype(jnp.float32)  34.2 us
    all_to_all x2, starting transfers between devices, on_device(): everyone = lax.all_to_all(spread, RING, 0, 0).reshape(total, feats)  25 us
    all_to_all x2, waiting for transfers between devices, on_device(): everyone = lax.all_to_all(spread, RING, 0, 0).reshape(total, feats)  21.7 us
    all_to_all x1, blocking collectives, on_device(): deltas = lax.all_to_all(delta.reshape(ring, rows, feats), RING, 0, 0)  21.7 us
    all_to_all x1, waiting for transfers between devices, on_device(): deltas = lax.all_to_all(delta.reshape(ring, rows, feats), RING, 0, 0)  12.1 us
    all_to_all x1, starting transfers between devices, on_device(): deltas = lax.all_to_all(delta.reshape(ring, rows, feats), RING, 0, 0)  11.8 us
    all_gather x1, blocking collectives, on_device(): blocks = lax.all_gather(units, ('core', 'lo'), axis=0)  10 us
    all_gather x1, blocking collectives, on_device(): lax.all_gather(everyone, 'lo', axis=0, tiled=True)  6.35 us
  transfers between devices with their start and end apart: 5, of which 3 were waited for; matrix products, arithmetic and copies ran while one was open for 2% of the time, Pallas kernels for 0%

profile of v10, /device:TPU:6, one launch (start us, length us, event | category | flops | bytes accessed | tf_op | source)
XLA Modules:
  0.0 163.8 jit_solution(7126101523612212983)
XLA Ops:
  0.0 1.5 broadcast_in_dim.8
  1.5 18.5 %all-to-all-start = ((bf16[48,2,1024]{2,1,0:T(2,128)(2,1)}), bf16[48,2,1024]{2,1,0:T(2,128)(2,1)S(1)}, u32[]{:S(2)}, u32[]{:S(2)}) async-start(bf16[48,2,1024]{2,1,0:T(2,128)(2,1)} %broadcast_in_dim.8), calls=%async_computation | async-start | bytes 393216 | tf_op jit(solution)/shard_map/all_to_all | solution.py:54
  20.0 3.5 %collective-permute-start = (bf16[256,1024]{1,0:T(8,128)(2,1)S(1)}, bf16[256,1024]{1,0:T(8,128)(2,1)S(1)}, u32[]{:S(2)}, u32[]{:S(2)}) collective-permute-start(bf16[256,1024]{1,0:T(8,128)(2,1)S(1)} %copy-done), channel_id=1, source_target_pairs={{0,48},{48,0},{1,49},{49,1},{2,50},{50,2},{3,51},{51,3},{4,52},{52... | collective-permute-start | bytes 1572872 | tf_op jit(solution)/shard_map/ppermute | solution.py:49
  23.5 0.0 copy-start.1
  23.5 1.1 constant_dynamic-update-slice_fusion.1
  24.7 0.0 copy-done.1
  24.8 9.0 %all-to-all-done = bf16[48,2,1024]{2,1,0:T(2,128)(2,1)S(1)} async-done(((bf16[48,2,1024]{2,1,0:T(2,128)(2,1)}), bf16[48,2,1024]{2,1,0:T(2,128)(2,1)S(1)}, u32[]{:S(2)}, u32[]{:S(2)}) %all-to-all-start) | async-done | bytes 196640 | tf_op jit(solution)/shard_map/all_to_all | solution.py:54
  33.8 0.1 reshape.17
  33.9 6.3 %all_gather.36 = bf16[192,1024]{1,0:T(8,128)(2,1)S(1)} all-gather(bf16[96,1024]{1,0:T(8,128)(2,1)S(1)} %reshape.17), channel_id=1, replica_groups=mesh['hi'=4,'core'=2,'lo'=2,'z'=12,'far'=2,'near'=2] {'lo'}, dimensions={0}, use_global_device_ids=true | all-gather | bytes 589824 | tf_op jit(solution)/shard_map/all_gather | solution.py:56
  40.2 0.2 fusion.3
  40.4 0.5 copy-done.2
  40.9 0.4 convolution_convert_fusion
  41.3 0.1 broadcast_in_dim.9
  41.4 2.2 %all-gather = bf16[384,640]{1,0:T(8,128)(2,1)S(1)} all-gather(bf16[192,640]{1,0:T(8,128)(2,1)S(1)} %pad_maximum_fusion), channel_id=2, replica_groups=mesh['hi'=4,'core'=2,'lo'=2,'z'=12,'far'=2,'near'=2] {'core'}, dimensions={0}, use_global_device_ids=true | all-gather | bytes 737280 | tf_op jit(solution)/shard_map/all_gather | solution.py:28
  43.6 19.3 %all-gather.1 = bf16[384,640]{1,0:T(8,128)(2,1)S(1)} all-gather(bf16[96,640]{1,0:T(8,128)(2,1)S(1)} %dynamic-slice_reduce_fusion), channel_id=3, replica_groups=mesh['hi'=4,'core'=2,'lo'=2,'z'=12,'far'=2,'near'=2] {'hi'}, dimensions={0}, use_global_device_ids=true | all-gather | bytes 614400 | tf_op jit(solution)/shard_map/all_gather | solution.py:31
  62.9 0.1 convert_reduce_fusion
  63.0 0.1 fusion.21
  63.1 0.1 fusion.11
  63.2 10.0 %all-gather.2 = bf16[384,256]{1,0:T(8,128)(2,1)S(1)} all-gather(bf16[96,256]{1,0:T(8,128)(2,1)S(1)} %fusion.11), channel_id=4, replica_groups=mesh['hi'=4,'core'=2,'lo'=2,'z'=12,'far'=2,'near'=2] {'core','lo'}, dimensions={0}, use_global_device_ids=true | all-gather | bytes 245760 | tf_op jit(solution)/shard_map/all_gather | solution.py:58
  73.3 0.2 fusion.23
  73.5 0.0 collective-permute-done
  73.5 0.2 fusion
  73.7 0.8 reshape.18
  74.5 11.8 %all-to-all-start.1 = ((bf16[48,2,1024]{2,1,0:T(2,128)(2,1)}), bf16[48,2,1024]{2,1,0:T(2,128)(2,1)S(1)}, u32[]{:S(2)}, u32[]{:S(2)}) async-start(bf16[48,2,1024]{2,1,0:T(2,128)(2,1)} %reshape.18), calls=%async_computation.1 | async-start | bytes 393216 | tf_op jit(solution)/shard_map/all_to_all | solution.py:70
  86.3 0.0 copy-start.3
  86.3 1.9 %collective-permute-start.1 = (bf16[1024,512]{1,0:T(8,128)(2,1)S(1)}, bf16[1024,512]{1,0:T(8,128)(2,1)S(1)}, u32[]{:S(2)}, u32[]{:S(2)}) collective-permute-start(bf16[1024,512]{1,0:T(8,128)(2,1)S(1)} %constant_dynamic-update-slice_fusion), channel_id=1, source_target_pairs={{0,48},{48,0},{1,49},{49,1},{2,50},{50,2},{3,51},{51,3},{4,52},{52... | collective-permute-start | bytes 3145736 | tf_op jit(solution)/shard_map/ppermute | solution.py:69
  88.2 12.1 %all-to-all-done.1 = bf16[48,2,1024]{2,1,0:T(2,128)(2,1)S(1)} async-done(((bf16[48,2,1024]{2,1,0:T(2,128)(2,1)}), bf16[48,2,1024]{2,1,0:T(2,128)(2,1)S(1)}, u32[]{:S(2)}, u32[]{:S(2)}) %all-to-all-start.1) | async-done | bytes 196640 | tf_op jit(solution)/shard_map/all_to_all | solution.py:70
  100.4 0.2 convert_reduce_fusion.3
  100.6 0.8 broadcast_in_dim.10
  101.3 6.5 %all-to-all-start.2 = ((bf16[48,2,1024]{2,1,0:T(2,128)(2,1)}), bf16[48,2,1024]{2,1,0:T(2,128)(2,1)S(1)}, u32[]{:S(2)}, u32[]{:S(2)}) async-start(bf16[48,2,1024]{2,1,0:T(2,128)(2,1)} %broadcast_in_dim.10), calls=%async_computation.2 | async-start | bytes 393216 | tf_op jit(solution)/shard_map/all_to_all | solution.py:54
  107.9 12.7 %all-to-all-done.2 = bf16[48,2,1024]{2,1,0:T(2,128)(2,1)S(1)} async-done(((bf16[48,2,1024]{2,1,0:T(2,128)(2,1)}), bf16[48,2,1024]{2,1,0:T(2,128)(2,1)S(1)}, u32[]{:S(2)}, u32[]{:S(2)}) %all-to-all-start.2) | async-done | bytes 196640 | tf_op jit(solution)/shard_map/all_to_all | solution.py:54
  120.6 0.1 reshape.19
  120.6 0.1 fusion.5
  120.8 0.3 convolution_convert_fusion.2
  121.1 0.3 convolution_convert_fusion.1
  121.4 0.1 broadcast_in_dim.11
  121.5 2.1 %all-gather.3 = bf16[192,1152]{1,0:T(8,128)(2,1)S(1)} all-gather(bf16[96,1152]{1,0:T(8,128)(2,1)S(1)} %pad_maximum_fusion.1), channel_id=5, replica_groups=mesh['hi'=4,'core'=2,'lo'=2,'z'=12,'far'=2,'near'=2] {'core'}, dimensions={0}, use_global_device_ids=true | all-gather | bytes 663552 | tf_op jit(solution)/shard_map/all_gather | solution.py:28
  123.7 14.9 %all-gather.4 = bf16[192,1152]{1,0:T(8,128)(2,1)S(1)} all-gather(bf16[48,1152]{1,0:T(8,128)(2,1)S(1)} %dynamic-slice_reduce_fusion.1), channel_id=6, replica_groups=mesh['hi'=4,'core'=2,'lo'=2,'z'=12,'far'=2,'near'=2] {'hi'}, dimensions={0}, use_global_device_ids=true | all-gather | bytes 552960 | tf_op jit(solution)/shard_map/all_gather | solution.py:31
  138.6 0.1 convert_reduce_fusion.1
  138.7 0.1 fusion.29
  138.8 0.1 fusion.18
  138.9 1.9 %all_gather.47 = bf16[96,512]{1,0:T(8,128)(2,1)S(1)} all-gather(bf16[48,512]{1,0:T(8,128)(2,1)S(1)} %pad_maximum_fusion.2), channel_id=1, replica_groups=mesh['hi'=4,'core'=2,'lo'=2,'z'=12,'far'=2,'near'=2] {'core'}, dimensions={0}, use_global_device_ids=true | all-gather | bytes 147456 | tf_op jit(solution)/shard_map/all_gather | solution.py:64
  140.8 0.2 fusion.13
  141.0 0.2 fusion.1
  141.2 0.1 reshape.20
  141.3 21.7 %all_to_all.20 = bf16[48,2,1024]{2,1,0:T(2,128)(2,1)S(1)} all-to-all(bf16[48,2,1024]{2,1,0:T(2,128)(2,1)S(1)} %reshape.20), channel_id=1, replica_groups=mesh['hi'=4,'core'=2,'lo'=2,'z'=12,'far'=2,'near'=2] {'near','z','far'}, dimensions={0} | all-to-all | bytes 393216 | tf_op jit(solution)/shard_map/all_to_all | solution.py:70
  163.0 0.2 convert_reduce_fusion.2
  163.2 0.6 add_convert_fusion
  (12 shorter events, 0.2 us)
Async XLA Ops:
  0.0 20.0 %copy-start = (bf16[256,1024]{1,0:T(8,128)(2,1)S(1)}, bf16[256,1024]{1,0:T(8,128)(2,1)}, u32[]{:S(2)}) copy-start(bf16[256,1024]{1,0:T(8,128)(2,1)} %param.9) | copy-start | bytes 1572868
  1.5 32.3 %all-to-all-start = ((bf16[48,2,1024]{2,1,0:T(2,128)(2,1)}), bf16[48,2,1024]{2,1,0:T(2,128)(2,1)S(1)}, u32[]{:S(2)}, u32[]{:S(2)}) async-start(bf16[48,2,1024]{2,1,0:T(2,128)(2,1)} %broadcast_in_dim.8), calls=%async_computation | async-start | bytes 393216 | tf_op jit(solution)/shard_map/all_to_all | solution.py:54
  20.0 53.5 %collective-permute-start = (bf16[256,1024]{1,0:T(8,128)(2,1)S(1)}, bf16[256,1024]{1,0:T(8,128)(2,1)S(1)}, u32[]{:S(2)}, u32[]{:S(2)}) collective-permute-start(bf16[256,1024]{1,0:T(8,128)(2,1)S(1)} %copy-done), channel_id=1, source_target_pairs={{0,48},{48,0},{1,49},{49,1},{2,50},{50,2},{3,51},{51,3},{4,52},{52... | collective-permute-start | bytes 1572872 | tf_op jit(solution)/shard_map/ppermute | solution.py:49
  23.5 1.2 copy-start.1
  40.2 0.7 copy-start.2
  74.5 25.9 %all-to-all-start.1 = ((bf16[48,2,1024]{2,1,0:T(2,128)(2,1)}), bf16[48,2,1024]{2,1,0:T(2,128)(2,1)S(1)}, u32[]{:S(2)}, u32[]{:S(2)}) async-start(bf16[48,2,1024]{2,1,0:T(2,128)(2,1)} %reshape.18), calls=%async_computation.1 | async-start | bytes 393216 | tf_op jit(solution)/shard_map/all_to_all | solution.py:70
  86.3 14.2 %copy-start.3 = (bf16[2,1024]{1,0:T(2,128)(2,1)S(1)}, bf16[2,1024]{1,0:T(2,128)(2,1)}, u32[]{:S(2)}) copy-start(bf16[2,1024]{1,0:T(2,128)(2,1)} %param.5) | copy-start | bytes 12292
  86.3 34.8 %collective-permute-start.1 = (bf16[1024,512]{1,0:T(8,128)(2,1)S(1)}, bf16[1024,512]{1,0:T(8,128)(2,1)S(1)}, u32[]{:S(2)}, u32[]{:S(2)}) collective-permute-start(bf16[1024,512]{1,0:T(8,128)(2,1)S(1)} %constant_dynamic-update-slice_fusion), channel_id=1, source_target_pairs={{0,48},{48,0},{1,49},{49,1},{2,50},{50,2},{3,51},{51,3},{4,52},{52... | collective-permute-start | bytes 3145736 | tf_op jit(solution)/shard_map/ppermute | solution.py:69
  101.3 19.2 %all-to-all-start.2 = ((bf16[48,2,1024]{2,1,0:T(2,128)(2,1)}), bf16[48,2,1024]{2,1,0:T(2,128)(2,1)S(1)}, u32[]{:S(2)}, u32[]{:S(2)}) async-start(bf16[48,2,1024]{2,1,0:T(2,128)(2,1)} %broadcast_in_dim.10), calls=%async_computation.2 | async-start | bytes 393216 | tf_op jit(solution)/shard_map/all_to_all | solution.py:54

commit v11 on v9

--- a/solution.py
+++ b/solution.py
@@ -23,12 +23,16 @@
     core = lax.axis_index("core")
     paired = jnp.concatenate([w_gate, w_up], axis=1)
     far = lax.ppermute(paired, "lo", PAIR)
-    down_far = lax.ppermute(w_down, "lo", PAIR)
+    down_far = None
     mixed = tokens
     for step in range(ITERS):
         spread = jnp.broadcast_to(mixed[None], (ring, rows, feats))
         everyone = lax.all_to_all(spread, RING, 0, 0)
-        everyone = lax.optimization_barrier(everyone.reshape(total, feats))
+        if step == 0:
+            everyone, later = lax.optimization_barrier((everyone.reshape(total, feats), w_down))
+            down_far = lax.ppermute(later, "lo", PAIR)
+        else:
+            everyone = lax.optimization_barrier(everyone.reshape(total, feats))
         wide = everyone.astype(jnp.float32)
         squares = jnp.sum(wide * wide, axis=1, keepdims=True)
         gained = (wide * norm_gain).astype(jnp.bfloat16)

time: 152 us -> 152 us (level)
  waiting for transfers between devices: 11 us -> 13.4 us
  blocking collectives: 109 us -> 107 us
    all_to_all x2, blocking collectives: 47.9 us -> 44.1 us  [on_device(): lax.all_to_all(delta.astype(jnp.bfloat16).reshape(ring, rows, feats), RIN...]
    all_gather x2, blocking collectives: 33.4 us -> 35.9 us  [on_device(): lax.all_gather(chip, 'hi', axis=0).astype(jnp.float32)]
    all_to_all x1, waiting for transfers between devices: 11 us -> 13.4 us  [on_device(): everyone = lax.all_to_all(spread, RING, 0, 0)]
where the time goes in v11:
time: 152 us
  blocking collectives  107 us (70%)
  starting transfers between devices  24.4 us (16%)
  waiting for transfers between devices  13.4 us (9%)
  local copies, waits for them, and re-layouts  2.58 us (2%)
  matrix products  2.12 us (1%)
  other arithmetic  1.93 us (1%)
    all_to_all x2, blocking collectives, on_device(): lax.all_to_all(delta.astype(jnp.bfloat16).reshape(ring, rows, feats), RIN...  44.1 us
    all_gather x2, blocking collectives, on_device(): lax.all_gather(chip, 'hi', axis=0).astype(jnp.float32)  35.9 us
    all_to_all x1, blocking collectives, on_device(): everyone = lax.all_to_all(spread, RING, 0, 0)  19.3 us
    all_to_all x1, starting transfers between devices, on_device(): everyone = lax.all_to_all(spread, RING, 0, 0)  18.5 us
    all_to_all x1, waiting for transfers between devices, on_device(): everyone = lax.all_to_all(spread, RING, 0, 0)  13.4 us
    all_gather x2, blocking collectives, on_device(): both = lax.all_gather(packed, 'core', axis=0)  4.25 us
    all_gather x2, blocking collectives, on_device(): lax.all_gather(jnp.concatenate(sides, axis=1), 'core', axis=0, tiled=True)  3.75 us
    ppermute x1, starting transfers between devices, on_device(): far = lax.ppermute(paired, 'lo', PAIR)  3.62 us
  transfers between devices with their start and end apart: 3, of which 1 were waited for; matrix products, arithmetic and copies ran while one was open for 1% of the time, Pallas kernels for 0%

profile of v11, /device:TPU:6, one launch (start us, length us, event | category | flops | bytes accessed | tf_op | source)
XLA Modules:
  0.0 151.9 jit_solution(12366479737768182786)
XLA Ops:
  0.0 1.1 constant_dynamic-update-slice_fusion.1
  1.1 0.1 copy-done.1
  1.2 0.0 copy-start
  1.3 3.6 %collective-permute-start = (bf16[1024,512]{1,0:T(8,128)(2,1)S(1)}, bf16[1024,512]{1,0:T(8,128)(2,1)S(1)}, u32[]{:S(2)}, u32[]{:S(2)}) collective-permute-start(bf16[1024,512]{1,0:T(8,128)(2,1)S(1)} %constant_dynamic-update-slice_fusion), channel_id=1, source_target_pairs={{0,48},{48,0},{1,49},{49,1},{2,50},{50,2},{3,51},{51,3},{4,52},{52... | collective-permute-start | bytes 3145736 | tf_op jit(solution)/shard_map/ppermute | solution.py:25
  4.9 0.0 copy-done.3
  4.9 0.8 broadcast_in_dim.8
  5.7 18.5 %all-to-all-start = ((bf16[48,2,1024]{2,1,0:T(2,128)(2,1)}), bf16[48,2,1024]{2,1,0:T(2,128)(2,1)S(1)}, u32[]{:S(2)}, u32[]{:S(2)}) async-start(bf16[48,2,1024]{2,1,0:T(2,128)(2,1)} %broadcast_in_dim.8), calls=%async_computation | async-start | bytes 393216 | tf_op jit(solution)/shard_map/all_to_all | solution.py:30
  24.2 13.4 %all-to-all-done = bf16[48,2,1024]{2,1,0:T(2,128)(2,1)S(1)} async-done(((bf16[48,2,1024]{2,1,0:T(2,128)(2,1)}), bf16[48,2,1024]{2,1,0:T(2,128)(2,1)S(1)}, u32[]{:S(2)}, u32[]{:S(2)}) %all-to-all-start) | async-done | bytes 196640 | tf_op jit(solution)/shard_map/all_to_all | solution.py:30
  37.5 0.1 reshape.17
  37.6 0.0 copy-done
  37.6 0.0 copy-start.2
  37.6 2.4 %collective-permute-start.1 = (bf16[256,1024]{1,0:T(8,128)(2,1)S(1)}, bf16[256,1024]{1,0:T(8,128)(2,1)S(1)}, u32[]{:S(2)}, u32[]{:S(2)}) collective-permute-start(bf16[256,1024]{1,0:T(8,128)(2,1)S(1)} %copy-done), channel_id=1, source_target_pairs={{0,48},{48,0},{1,49},{49,1},{2,50},{50,2},{3,51},{51,3},{4,52},{52... | collective-permute-start | bytes 1572872 | tf_op jit(solution)/shard_map/ppermute | solution.py:33
  40.0 0.1 fusion.3
  40.1 0.3 convolution_convert_fusion.3
  40.4 0.0 collective-permute-done
  40.5 0.3 convolution_convert_fusion.2
  40.8 0.1 broadcast_in_dim.9
  40.9 2.1 %all-gather = bf16[192,1152]{1,0:T(8,128)(2,1)S(1)} all-gather(bf16[96,1152]{1,0:T(8,128)(2,1)S(1)} %pad_maximum_fusion), channel_id=2, replica_groups=mesh['hi'=4,'core'=2,'lo'=2,'z'=12,'far'=2,'near'=2] {'core'}, dimensions={0}, use_global_device_ids=true | all-gather | bytes 663552 | tf_op jit(solution)/shard_map/all_gather | solution.py:47
  43.0 20.2 %all-gather.1 = bf16[192,1152]{1,0:T(8,128)(2,1)S(1)} all-gather(bf16[48,1152]{1,0:T(8,128)(2,1)S(1)} %dynamic-slice_reduce_fusion.1), channel_id=3, replica_groups=mesh['hi'=4,'core'=2,'lo'=2,'z'=12,'far'=2,'near'=2] {'hi'}, dimensions={0}, use_global_device_ids=true | all-gather | bytes 552960 | tf_op jit(solution)/shard_map/all_gather | solution.py:50
  63.3 0.1 convert_reduce_fusion.1
  63.3 0.1 fusion.29
  63.5 0.1 fusion.23
  63.6 1.9 %all_gather.34 = bf16[96,512]{1,0:T(8,128)(2,1)S(1)} all-gather(bf16[48,512]{1,0:T(8,128)(2,1)S(1)} %pad_maximum_fusion.2), channel_id=1, replica_groups=mesh['hi'=4,'core'=2,'lo'=2,'z'=12,'far'=2,'near'=2] {'core'}, dimensions={0}, use_global_device_ids=true | all-gather | bytes 147456 | tf_op jit(solution)/shard_map/all_gather | solution.py:58
  65.5 0.2 fusion.18
  65.7 0.0 collective-permute-done.1
  65.7 0.2 fusion
  65.9 0.1 reshape.18
  66.0 23.2 %all_to_all.20 = bf16[48,2,1024]{2,1,0:T(2,128)(2,1)S(1)} all-to-all(bf16[48,2,1024]{2,1,0:T(2,128)(2,1)S(1)} %reshape.18), channel_id=1, replica_groups=mesh['hi'=4,'core'=2,'lo'=2,'z'=12,'far'=2,'near'=2] {'near','z','far'}, dimensions={0} | all-to-all | bytes 393216 | tf_op jit(solution)/shard_map/all_to_all | solution.py:60
  89.2 0.2 convert_reduce_fusion.3
  89.4 0.1 broadcast_in_dim.10
  89.5 19.3 %all_to_all.21 = bf16[48,2,1024]{2,1,0:T(2,128)(2,1)S(1)} all-to-all(bf16[48,2,1024]{2,1,0:T(2,128)(2,1)S(1)} %broadcast_in_dim.10), channel_id=1, replica_groups=mesh['hi'=4,'core'=2,'lo'=2,'z'=12,'far'=2,'near'=2] {'near','z','far'}, dimensions={0} | all-to-all | bytes 393216 | tf_op jit(solution)/shard_map/all_to_all | solution.py:30
  108.7 0.1 reshape.19
  108.8 0.3 convolution_convert_fusion.1
  109.1 0.1 fusion.5
  109.3 0.3 convolution_convert_fusion
  109.6 0.1 broadcast_in_dim.11
  109.7 2.1 %all-gather.2 = bf16[192,1152]{1,0:T(8,128)(2,1)S(1)} all-gather(bf16[96,1152]{1,0:T(8,128)(2,1)S(1)} %pad_maximum_fusion.1), channel_id=4, replica_groups=mesh['hi'=4,'core'=2,'lo'=2,'z'=12,'far'=2,'near'=2] {'core'}, dimensions={0}, use_global_device_ids=true | all-gather | bytes 663552 | tf_op jit(solution)/shard_map/all_gather | solution.py:47
  111.8 15.6 %all-gather.3 = bf16[192,1152]{1,0:T(8,128)(2,1)S(1)} all-gather(bf16[48,1152]{1,0:T(8,128)(2,1)S(1)} %dynamic-slice_reduce_fusion), channel_id=5, replica_groups=mesh['hi'=4,'core'=2,'lo'=2,'z'=12,'far'=2,'near'=2] {'hi'}, dimensions={0}, use_global_device_ids=true | all-gather | bytes 552960 | tf_op jit(solution)/shard_map/all_gather | solution.py:50
  127.4 0.1 convert_reduce_fusion
  127.5 0.1 fusion.26
  127.6 0.1 fusion.16
  127.8 1.9 %all_gather.39 = bf16[96,512]{1,0:T(8,128)(2,1)S(1)} all-gather(bf16[48,512]{1,0:T(8,128)(2,1)S(1)} %pad_maximum_fusion.3), channel_id=1, replica_groups=mesh['hi'=4,'core'=2,'lo'=2,'z'=12,'far'=2,'near'=2] {'core'}, dimensions={0}, use_global_device_ids=true | all-gather | bytes 147456 | tf_op jit(solution)/shard_map/all_gather | solution.py:58
  129.6 0.2 fusion.11
  129.9 0.2 fusion.1
  130.1 0.1 reshape.20
  130.2 20.9 %all_to_all.22 = bf16[48,2,1024]{2,1,0:T(2,128)(2,1)S(1)} all-to-all(bf16[48,2,1024]{2,1,0:T(2,128)(2,1)S(1)} %reshape.20), channel_id=1, replica_groups=mesh['hi'=4,'core'=2,'lo'=2,'z'=12,'far'=2,'near'=2] {'near','z','far'}, dimensions={0} | all-to-all | bytes 393216 | tf_op jit(solution)/shard_map/all_to_all | solution.py:60
  151.1 0.2 convert_reduce_fusion.2
  151.3 0.6 add_convert_fusion
  (11 shorter events, 0.2 us)
Async XLA Ops:
  0.0 1.2 copy-start.1
  1.2 3.7 %copy-start.3 = (bf16[2,1024]{1,0:T(2,128)(2,1)S(1)}, bf16[2,1024]{1,0:T(2,128)(2,1)}, u32[]{:S(2)}) copy-start(bf16[2,1024]{1,0:T(2,128)(2,1)} %param.5) | copy-start | bytes 12292
  1.2 36.4 %copy-start = (bf16[256,1024]{1,0:T(8,128)(2,1)S(1)}, bf16[256,1024]{1,0:T(8,128)(2,1)}, u32[]{:S(2)}) copy-start(bf16[256,1024]{1,0:T(8,128)(2,1)} %param.9) | copy-start | bytes 1572868
  1.3 39.2 %collective-permute-start = (bf16[1024,512]{1,0:T(8,128)(2,1)S(1)}, bf16[1024,512]{1,0:T(8,128)(2,1)S(1)}, u32[]{:S(2)}, u32[]{:S(2)}) collective-permute-start(bf16[1024,512]{1,0:T(8,128)(2,1)S(1)} %constant_dynamic-update-slice_fusion), channel_id=1, source_target_pairs={{0,48},{48,0},{1,49},{49,1},{2,50},{50,2},{3,51},{51,3},{4,52},{52... | collective-permute-start | bytes 3145736 | tf_op jit(solution)/shard_map/ppermute | solution.py:25
  5.7 31.9 %all-to-all-start = ((bf16[48,2,1024]{2,1,0:T(2,128)(2,1)}), bf16[48,2,1024]{2,1,0:T(2,128)(2,1)S(1)}, u32[]{:S(2)}, u32[]{:S(2)}) async-start(bf16[48,2,1024]{2,1,0:T(2,128)(2,1)} %broadcast_in_dim.8), calls=%async_computation | async-start | bytes 393216 | tf_op jit(solution)/shard_map/all_to_all | solution.py:30
  37.6 2.5 %copy-start.2 = (f32[1024]{0:T(1024)S(1)}, f32[1024]{0:T(1024)}, u32[]{:S(2)}) copy-start(f32[1024]{0:T(1024)} %param.6) | copy-start | bytes 12292
  37.6 28.1 %collective-permute-start.1 = (bf16[256,1024]{1,0:T(8,128)(2,1)S(1)}, bf16[256,1024]{1,0:T(8,128)(2,1)S(1)}, u32[]{:S(2)}, u32[]{:S(2)}) collective-permute-start(bf16[256,1024]{1,0:T(8,128)(2,1)S(1)} %copy-done), channel_id=1, source_target_pairs={{0,48},{48,0},{1,49},{49,1},{2,50},{50,2},{3,51},{51,3},{4,52},{52... | collective-permute-start | bytes 1572872 | tf_op jit(solution)/shard_map/ppermute | solution.py:33

commit v12 on v6

--- a/solution.py
+++ b/solution.py
@@ -30,27 +30,28 @@
         everyone = lax.all_to_all(spread, RING, 0, 0)
         everyone = lax.optimization_barrier(everyone.reshape(total, feats))
         wide = everyone.astype(jnp.float32)
-        squares = jnp.sum(wide * wide, axis=1, keepdims=True)
+        squares = jnp.sum(wide * wide, axis=1)
         gained = (wide * norm_gain).astype(jnp.bfloat16)
-        packed = jnp.concatenate(
-            [
-                matmul(gained, paired).astype(jnp.bfloat16),
-                matmul(gained, far).astype(jnp.bfloat16),
-                jnp.broadcast_to(squares, (total, 128)).astype(jnp.bfloat16),
-            ],
-            axis=1,
-        )
+        line = jnp.broadcast_to(jnp.pad(squares, (0, feats - total))[None], (8, feats))
+        parts = jnp.concatenate([matmul(gained, paired), matmul(gained, far)], axis=1)
+        packed = jnp.concatenate([parts.astype(jnp.bfloat16), line.astype(jnp.bfloat16)], axis=0)
         both = lax.all_gather(packed, "core", axis=0)
         mine = lax.dynamic_slice_in_dim(both, core * half, half, axis=1)
         chip = jnp.sum(mine.astype(jnp.float32), axis=0).astype(jnp.bfloat16)
-        share = jnp.sum(lax.all_gather(chip, "hi", axis=0).astype(jnp.float32), axis=0)
-        scale = lax.rsqrt(share[:, 2 * width : 2 * width + 1] / D + 1e-05)
+        chip_line = jnp.sum(both[:, total:, :128].astype(jnp.float32), axis=0).astype(jnp.bfloat16)
+        stacked = jnp.concatenate(jnp.split(chip, 2 * width // 128, axis=1) + [chip_line], axis=0)
+        share = jnp.sum(lax.all_gather(stacked, "hi", axis=0).astype(jnp.float32), axis=0)
+        all_squares = share[share.shape[0] - 1, :total]
+        scale = lax.rsqrt(jnp.where(core == 0, all_squares[:half], all_squares[half:]) / D + 1e-05)[:, None]
         side = width // FAR
+        pieces = side // 128
         sides = []
-        for base in (0, width):
-            gate = share[:, base : base + side] * scale
-            up = share[:, base + side : base + width] * scale
-            sides.append((jax.nn.silu(gate) * up).astype(jnp.bfloat16))
+        for block in range(FAR):
+            for piece in range(pieces):
+                at = (2 * pieces * block + piece) * half
+                gate = share[at : at + half] * scale
+                up = share[at + pieces * half : at + (pieces + 1) * half] * scale
+                sides.append((jax.nn.silu(gate) * up).astype(jnp.bfloat16))
         hidden = lax.all_gather(jnp.concatenate(sides, axis=1), "core", axis=0, tiled=True)
         delta = matmul(hidden[:, :side], w_down) + matmul(hidden[:, side:], down_far)
         deltas = lax.all_to_all(delta.astype(jnp.bfloat16).reshape(ring, rows, feats), RING, 0, 0)

time: 151 us -> 150 us (level)
  no operation moved by 1% of the time
where the time goes in v12:
time: 150 us; the launch traced here: 149 us
  blocking collectives  106 us (71%)
  starting transfers between devices  25.4 us (17%)
  waiting for transfers between devices  9.3 us (6%)
  local copies, waits for them, and re-layouts  3.2 us (2%)
  matrix products  2.12 us (1%)
  other arithmetic  1.83 us (1%)
    all_to_all x2, blocking collectives, on_device(): lax.all_to_all(delta.astype(jnp.bfloat16).reshape(ring, rows, feats), RIN...  46.8 us
    all_gather x2, blocking collectives, on_device(): lax.all_gather(stacked, 'hi', axis=0).astype(jnp.float32)  33.2 us
    all_to_all x1, blocking collectives, on_device(): everyone = lax.all_to_all(spread, RING, 0, 0)  18.4 us
    all_to_all x1, starting transfers between devices, on_device(): everyone = lax.all_to_all(spread, RING, 0, 0)  18 us
    all_to_all x1, waiting for transfers between devices, on_device(): everyone = lax.all_to_all(spread, RING, 0, 0)  9.3 us
    all_gather x2, blocking collectives, on_device(): both = lax.all_gather(packed, 'core', axis=0)  4.22 us
    ppermute x1, starting transfers between devices, on_device(): down_far = lax.ppermute(w_down, 'far', PAIR)  4.03 us
    all_gather x2, blocking collectives, on_device(): lax.all_gather(jnp.concatenate(sides, axis=1), 'core', axis=0, tiled=True)  3.75 us
  transfers between devices with their start and end apart: 3, of which 1 were waited for; matrix products, arithmetic and copies ran while one was open for 1% of the time, Pallas kernels for 0%

profile of v12, /device:TPU:6, one launch (start us, length us, event | category | flops | bytes accessed | tf_op | source)
XLA Modules:
  0.0 148.5 jit_solution(17101099958531077544)
XLA Ops:
  0.0 0.0 copy-start.1
  0.0 1.1 constant_dynamic-update-slice_fusion.1
  1.1 0.1 copy-done.1
  1.2 0.0 copy-start.3
  1.2 0.0 copy-start
  1.3 3.4 %collective-permute-start = (bf16[1024,512]{1,0:T(8,128)(2,1)S(1)}, bf16[1024,512]{1,0:T(8,128)(2,1)S(1)}, u32[]{:S(2)}, u32[]{:S(2)}) collective-permute-start(bf16[1024,512]{1,0:T(8,128)(2,1)S(1)} %constant_dynamic-update-slice_fusion), channel_id=1, source_target_pairs={{0,2},{2,0},{1,3},{3,1},{4,6},{6,4},{5,7},{7,5},{8,10},{10,8},{9,1... | collective-permute-start | bytes 3145736 | tf_op jit(solution)/shard_map/ppermute | solution.py:25
  4.7 0.0 copy-done.3
  4.7 0.8 broadcast_in_dim.8
  5.5 18.0 %all-to-all-start = ((bf16[48,2,1024]{2,1,0:T(2,128)(2,1)}), bf16[48,2,1024]{2,1,0:T(2,128)(2,1)S(1)}, u32[]{:S(2)}, u32[]{:S(2)}) async-start(bf16[48,2,1024]{2,1,0:T(2,128)(2,1)} %broadcast_in_dim.8), calls=%async_computation | async-start | bytes 393216 | tf_op jit(solution)/shard_map/all_to_all | solution.py:30
  23.5 0.0 copy-done
  23.5 4.0 %collective-permute-start.1 = (bf16[256,1024]{1,0:T(8,128)(2,1)S(1)}, bf16[256,1024]{1,0:T(8,128)(2,1)S(1)}, u32[]{:S(2)}, u32[]{:S(2)}) collective-permute-start(bf16[256,1024]{1,0:T(8,128)(2,1)S(1)} %copy-done), channel_id=1, source_target_pairs={{0,2},{2,0},{1,3},{3,1},{4,6},{6,4},{5,7},{7,5},{8,10},{10,8},{9,1... | collective-permute-start | bytes 1572872 | tf_op jit(solution)/shard_map/ppermute | solution.py:26
  27.5 9.3 %all-to-all-done = bf16[48,2,1024]{2,1,0:T(2,128)(2,1)S(1)} async-done(((bf16[48,2,1024]{2,1,0:T(2,128)(2,1)}), bf16[48,2,1024]{2,1,0:T(2,128)(2,1)S(1)}, u32[]{:S(2)}, u32[]{:S(2)}) %all-to-all-start) | async-done | bytes 196640 | tf_op jit(solution)/shard_map/all_to_all | solution.py:30
  36.8 0.1 reshape.59
  36.9 0.0 copy-start.2
  36.9 0.1 fusion.3
  37.0 0.5 copy-done.2
  37.6 0.3 convolution_convert_fusion.3
  37.9 0.0 collective-permute-done
  37.9 0.3 convolution_convert_fusion.2
  38.2 2.1 %all-gather = bf16[208,1024]{1,0:T(8,128)(2,1)S(1)} all-gather(bf16[104,1024]{1,0:T(8,128)(2,1)S(1)} %pad_maximum_fusion), channel_id=2, replica_groups=mesh['hi'=4,'core'=2,'yz'=24,'far'=2,'near'=2] {'core'}, dimensions={0}, use_global_device_ids=true | all-gather | bytes 638976 | tf_op jit(solution)/shard_map/all_gather | solution.py:38
  40.5 16.8 %all-gather.1 = bf16[1568,128]{1,0:T(8,128)(2,1)S(1)} all-gather(bf16[392,128]{1,0:T(8,128)(2,1)S(1)} %constant_dynamic-update-slice_fusion.2), channel_id=3, replica_groups=mesh['hi'=4,'core'=2,'yz'=24,'far'=2,'near'=2] {'hi'}, dimensions={0}, use_global_device_ids=true | all-gather | bytes 501760 | tf_op jit(solution)/shard_map/all_gather | solution.py:43
  57.4 0.1 rsqrt_bitcast_fusion.1
  57.5 0.1 fusion.31
  57.6 1.9 %all_gather.34 = bf16[96,512]{1,0:T(8,128)(2,1)S(1)} all-gather(bf16[48,512]{1,0:T(8,128)(2,1)S(1)} %pad_maximum_fusion.2), channel_id=1, replica_groups=mesh['hi'=4,'core'=2,'yz'=24,'far'=2,'near'=2] {'core'}, dimensions={0}, use_global_device_ids=true | all-gather | bytes 147456 | tf_op jit(solution)/shard_map/all_gather | solution.py:55
  59.5 0.2 fusion.14
  59.7 0.0 collective-permute-done.1
  59.7 0.2 fusion
  60.0 0.1 reshape.60
  60.1 27.1 %all_to_all.20 = bf16[48,2,1024]{2,1,0:T(2,128)(2,1)S(1)} all-to-all(bf16[48,2,1024]{2,1,0:T(2,128)(2,1)S(1)} %reshape.60), channel_id=1, replica_groups=mesh['hi'=4,'core'=2,'yz'=24,'far'=2,'near'=2] {'yz','near'}, dimensions={0} | all-to-all | bytes 393216 | tf_op jit(solution)/shard_map/all_to_all | solution.py:57
  87.1 0.2 convert_reduce_fusion.3
  87.3 0.1 broadcast_in_dim.10
  87.4 18.4 %all_to_all.21 = bf16[48,2,1024]{2,1,0:T(2,128)(2,1)S(1)} all-to-all(bf16[48,2,1024]{2,1,0:T(2,128)(2,1)S(1)} %broadcast_in_dim.10), channel_id=1, replica_groups=mesh['hi'=4,'core'=2,'yz'=24,'far'=2,'near'=2] {'yz','near'}, dimensions={0} | all-to-all | bytes 393216 | tf_op jit(solution)/shard_map/all_to_all | solution.py:30
  105.8 0.1 reshape.61
  105.9 0.3 convolution_convert_fusion.1
  106.2 0.1 fusion.5
  106.4 0.3 convolution_convert_fusion
  106.7 2.1 %all-gather.2 = bf16[208,1024]{1,0:T(8,128)(2,1)S(1)} all-gather(bf16[104,1024]{1,0:T(8,128)(2,1)S(1)} %pad_maximum_fusion.1), channel_id=4, replica_groups=mesh['hi'=4,'core'=2,'yz'=24,'far'=2,'near'=2] {'core'}, dimensions={0}, use_global_device_ids=true | all-gather | bytes 638976 | tf_op jit(solution)/shard_map/all_gather | solution.py:38
  109.0 16.3 %all-gather.3 = bf16[1568,128]{1,0:T(8,128)(2,1)S(1)} all-gather(bf16[392,128]{1,0:T(8,128)(2,1)S(1)} %constant_dynamic-update-slice_fusion.11), channel_id=5, replica_groups=mesh['hi'=4,'core'=2,'yz'=24,'far'=2,'near'=2] {'hi'}, dimensions={0}, use_global_device_ids=true | all-gather | bytes 501760 | tf_op jit(solution)/shard_map/all_gather | solution.py:43
  125.4 0.1 rsqrt_bitcast_fusion
  125.5 0.1 fusion.23
  125.6 1.9 %all_gather.39 = bf16[96,512]{1,0:T(8,128)(2,1)S(1)} all-gather(bf16[48,512]{1,0:T(8,128)(2,1)S(1)} %pad_maximum_fusion.3), channel_id=1, replica_groups=mesh['hi'=4,'core'=2,'yz'=24,'far'=2,'near'=2] {'core'}, dimensions={0}, use_global_device_ids=true | all-gather | bytes 147456 | tf_op jit(solution)/shard_map/all_gather | solution.py:55
  127.5 0.2 fusion.11
  127.7 0.2 fusion.1
  127.9 0.1 reshape.62
  128.0 19.7 %all_to_all.22 = bf16[48,2,1024]{2,1,0:T(2,128)(2,1)S(1)} all-to-all(bf16[48,2,1024]{2,1,0:T(2,128)(2,1)S(1)} %reshape.62), channel_id=1, replica_groups=mesh['hi'=4,'core'=2,'yz'=24,'far'=2,'near'=2] {'yz','near'}, dimensions={0} | all-to-all | bytes 393216 | tf_op jit(solution)/shard_map/all_to_all | solution.py:57
  147.7 0.2 convert_reduce_fusion.2
  147.9 0.6 add_convert_fusion
  (34 shorter events, 0.5 us)
Async XLA Ops:
  0.0 1.2 copy-start.1
  1.2 3.5 %copy-start.3 = (bf16[2,1024]{1,0:T(2,128)(2,1)S(1)}, bf16[2,1024]{1,0:T(2,128)(2,1)}, u32[]{:S(2)}) copy-start(bf16[2,1024]{1,0:T(2,128)(2,1)} %param.5) | copy-start | bytes 12292
  1.2 22.2 %copy-start = (bf16[256,1024]{1,0:T(8,128)(2,1)S(1)}, bf16[256,1024]{1,0:T(8,128)(2,1)}, u32[]{:S(2)}) copy-start(bf16[256,1024]{1,0:T(8,128)(2,1)} %param.9) | copy-start | bytes 1572868
  1.3 36.6 %collective-permute-start = (bf16[1024,512]{1,0:T(8,128)(2,1)S(1)}, bf16[1024,512]{1,0:T(8,128)(2,1)S(1)}, u32[]{:S(2)}, u32[]{:S(2)}) collective-permute-start(bf16[1024,512]{1,0:T(8,128)(2,1)S(1)} %constant_dynamic-update-slice_fusion), channel_id=1, source_target_pairs={{0,2},{2,0},{1,3},{3,1},{4,6},{6,4},{5,7},{7,5},{8,10},{10,8},{9,1... | collective-permute-start | bytes 3145736 | tf_op jit(solution)/shard_map/ppermute | solution.py:25
  5.5 31.3 %all-to-all-start = ((bf16[48,2,1024]{2,1,0:T(2,128)(2,1)}), bf16[48,2,1024]{2,1,0:T(2,128)(2,1)S(1)}, u32[]{:S(2)}, u32[]{:S(2)}) async-start(bf16[48,2,1024]{2,1,0:T(2,128)(2,1)} %broadcast_in_dim.8), calls=%async_computation | async-start | bytes 393216 | tf_op jit(solution)/shard_map/all_to_all | solution.py:30
  23.5 36.3 %collective-permute-start.1 = (bf16[256,1024]{1,0:T(8,128)(2,1)S(1)}, bf16[256,1024]{1,0:T(8,128)(2,1)S(1)}, u32[]{:S(2)}, u32[]{:S(2)}) collective-permute-start(bf16[256,1024]{1,0:T(8,128)(2,1)S(1)} %copy-done), channel_id=1, source_target_pairs={{0,2},{2,0},{1,3},{3,1},{4,6},{6,4},{5,7},{7,5},{8,10},{10,8},{9,1... | collective-permute-start | bytes 1572872 | tf_op jit(solution)/shard_map/ppermute | solution.py:26
  36.9 0.7 copy-start.2

commit v13 on v12

--- a/solution.py
+++ b/solution.py
@@ -24,6 +24,7 @@
     paired = jnp.concatenate([w_gate, w_up], axis=1)
     far = lax.ppermute(paired, "far", PAIR)
     down_far = lax.ppermute(w_down, "far", PAIR)
+    gain = lax.optimization_barrier(jnp.broadcast_to(norm_gain[None], (8, feats)))
     mixed = tokens
     for step in range(ITERS):
         spread = jnp.broadcast_to(mixed[None], (ring, rows, feats))
@@ -31,7 +32,7 @@
         everyone = lax.optimization_barrier(everyone.reshape(total, feats))
         wide = everyone.astype(jnp.float32)
         squares = jnp.sum(wide * wide, axis=1)
-        gained = (wide * norm_gain).astype(jnp.bfloat16)
+        gained = (wide * gain[:1]).astype(jnp.bfloat16)
         line = jnp.broadcast_to(jnp.pad(squares, (0, feats - total))[None], (8, feats))
         parts = jnp.concatenate([matmul(gained, paired), matmul(gained, far)], axis=1)
         packed = jnp.concatenate([parts.astype(jnp.bfloat16), line.astype(jnp.bfloat16)], axis=0)

time: 150 us -> 149 us (level)
  transfers between devices with their start and end apart: 3 -> 3, of which waited for: 1 -> 1; matrix products, arithmetic and copies ran while one was open for 1% -> 2% of each run, Pallas kernels for 0% -> 0%
where the time goes in v13:
time: 149 us
  blocking collectives  107 us (72%)
  starting transfers between devices  25.4 us (17%)
  waiting for transfers between devices  8.6 us (6%)
  local copies, waits for them, and re-layouts  3.35 us (2%)
  matrix products  2.12 us (1%)
  other arithmetic  1.83 us (1%)
    all_to_all x2, blocking collectives, on_device(): lax.all_to_all(delta.astype(jnp.bfloat16).reshape(ring, rows, feats), RIN...  47.3 us
    all_gather x2, blocking collectives, on_device(): lax.all_gather(stacked, 'hi', axis=0).astype(jnp.float32)  33.2 us
    all_to_all x1, blocking collectives, on_device(): everyone = lax.all_to_all(spread, RING, 0, 0)  18.4 us
    all_to_all x1, starting transfers between devices, on_device(): everyone = lax.all_to_all(spread, RING, 0, 0)  18 us
    all_to_all x1, waiting for transfers between devices, on_device(): everyone = lax.all_to_all(spread, RING, 0, 0)  8.6 us
    all_gather x2, blocking collectives, on_device(): both = lax.all_gather(packed, 'core', axis=0)  4.22 us
    ppermute x1, starting transfers between devices, on_device(): down_far = lax.ppermute(w_down, 'far', PAIR)  4.03 us
    all_gather x2, blocking collectives, on_device(): lax.all_gather(jnp.concatenate(sides, axis=1), 'core', axis=0, tiled=True)  3.75 us
  transfers between devices with their start and end apart: 3, of which 1 were waited for; matrix products, arithmetic and copies ran while one was open for 2% of the time, Pallas kernels for 0%

profile of v13, /device:TPU:6, one launch (start us, length us, event | category | flops | bytes accessed | tf_op | source)
XLA Modules:
  0.0 148.5 jit_solution(12700578075614826194)
XLA Ops:
  0.0 0.0 copy-start.1
  0.0 1.1 constant_dynamic-update-slice_fusion.1
  1.1 0.1 copy-done.1
  1.2 0.0 copy-start.2
  1.2 0.0 copy-start
  1.3 3.4 %collective-permute-start = (bf16[1024,512]{1,0:T(8,128)(2,1)S(1)}, bf16[1024,512]{1,0:T(8,128)(2,1)S(1)}, u32[]{:S(2)}, u32[]{:S(2)}) collective-permute-start(bf16[1024,512]{1,0:T(8,128)(2,1)S(1)} %constant_dynamic-update-slice_fusion), channel_id=1, source_target_pairs={{0,2},{2,0},{1,3},{3,1},{4,6},{6,4},{5,7},{7,5},{8,10},{10,8},{9,1... | collective-permute-start | bytes 3145736 | tf_op jit(solution)/shard_map/ppermute | solution.py:25
  4.7 0.0 copy-done.2
  4.7 0.8 broadcast_in_dim.10
  5.5 18.0 %all-to-all-start = ((bf16[48,2,1024]{2,1,0:T(2,128)(2,1)}), bf16[48,2,1024]{2,1,0:T(2,128)(2,1)S(1)}, u32[]{:S(2)}, u32[]{:S(2)}) async-start(bf16[48,2,1024]{2,1,0:T(2,128)(2,1)} %broadcast_in_dim.10), calls=%async_computation | async-start | bytes 393216 | tf_op jit(solution)/shard_map/all_to_all | solution.py:31
  23.5 0.0 copy-done
  23.5 4.0 %collective-permute-start.1 = (bf16[256,1024]{1,0:T(8,128)(2,1)S(1)}, bf16[256,1024]{1,0:T(8,128)(2,1)S(1)}, u32[]{:S(2)}, u32[]{:S(2)}) collective-permute-start(bf16[256,1024]{1,0:T(8,128)(2,1)S(1)} %copy-done), channel_id=1, source_target_pairs={{0,2},{2,0},{1,3},{3,1},{4,6},{6,4},{5,7},{7,5},{8,10},{10,8},{9,1... | collective-permute-start | bytes 1572872 | tf_op jit(solution)/shard_map/ppermute | solution.py:26
  27.5 0.0 copy-start.3
  27.5 0.7 copy-done.3
  28.2 8.6 %all-to-all-done = bf16[48,2,1024]{2,1,0:T(2,128)(2,1)S(1)} async-done(((bf16[48,2,1024]{2,1,0:T(2,128)(2,1)}), bf16[48,2,1024]{2,1,0:T(2,128)(2,1)S(1)}, u32[]{:S(2)}, u32[]{:S(2)}) %all-to-all-start) | async-done | bytes 196640 | tf_op jit(solution)/shard_map/all_to_all | solution.py:31
  36.8 0.1 reshape.59
  36.9 0.1 fusion.3
  37.0 0.3 convolution_convert_fusion.3
  37.3 0.0 collective-permute-done
  37.4 0.3 convolution_convert_fusion.2
  37.7 2.1 %all-gather = bf16[208,1024]{1,0:T(8,128)(2,1)S(1)} all-gather(bf16[104,1024]{1,0:T(8,128)(2,1)S(1)} %pad_maximum_fusion), channel_id=2, replica_groups=mesh['hi'=4,'core'=2,'yz'=24,'far'=2,'near'=2] {'core'}, dimensions={0}, use_global_device_ids=true | all-gather | bytes 638976 | tf_op jit(solution)/shard_map/all_gather | solution.py:39
  40.0 16.8 %all-gather.1 = bf16[1568,128]{1,0:T(8,128)(2,1)S(1)} all-gather(bf16[392,128]{1,0:T(8,128)(2,1)S(1)} %constant_dynamic-update-slice_fusion.2), channel_id=3, replica_groups=mesh['hi'=4,'core'=2,'yz'=24,'far'=2,'near'=2] {'hi'}, dimensions={0}, use_global_device_ids=true | all-gather | bytes 501760 | tf_op jit(solution)/shard_map/all_gather | solution.py:44
  56.9 0.1 rsqrt_bitcast_fusion.1
  57.0 0.1 fusion.31
  57.1 1.9 %all_gather.34 = bf16[96,512]{1,0:T(8,128)(2,1)S(1)} all-gather(bf16[48,512]{1,0:T(8,128)(2,1)S(1)} %pad_maximum_fusion.2), channel_id=1, replica_groups=mesh['hi'=4,'core'=2,'yz'=24,'far'=2,'near'=2] {'core'}, dimensions={0}, use_global_device_ids=true | all-gather | bytes 147456 | tf_op jit(solution)/shard_map/all_gather | solution.py:56
  59.0 0.2 fusion.14
  59.2 0.0 collective-permute-done.1
  59.2 0.2 fusion
  59.4 0.1 reshape.60
  59.5 27.6 %all_to_all.20 = bf16[48,2,1024]{2,1,0:T(2,128)(2,1)S(1)} all-to-all(bf16[48,2,1024]{2,1,0:T(2,128)(2,1)S(1)} %reshape.60), channel_id=1, replica_groups=mesh['hi'=4,'core'=2,'yz'=24,'far'=2,'near'=2] {'yz','near'}, dimensions={0} | all-to-all | bytes 393216 | tf_op jit(solution)/shard_map/all_to_all | solution.py:58
  87.1 0.2 convert_reduce_fusion.3
  87.3 0.1 broadcast_in_dim.13
  87.4 18.4 %all_to_all.21 = bf16[48,2,1024]{2,1,0:T(2,128)(2,1)S(1)} all-to-all(bf16[48,2,1024]{2,1,0:T(2,128)(2,1)S(1)} %broadcast_in_dim.13), channel_id=1, replica_groups=mesh['hi'=4,'core'=2,'yz'=24,'far'=2,'near'=2] {'yz','near'}, dimensions={0} | all-to-all | bytes 393216 | tf_op jit(solution)/shard_map/all_to_all | solution.py:31
  105.8 0.1 reshape.61
  105.9 0.3 convolution_convert_fusion.1
  106.2 0.1 fusion.5
  106.4 0.3 convolution_convert_fusion
  106.7 2.1 %all-gather.2 = bf16[208,1024]{1,0:T(8,128)(2,1)S(1)} all-gather(bf16[104,1024]{1,0:T(8,128)(2,1)S(1)} %pad_maximum_fusion.1), channel_id=4, replica_groups=mesh['hi'=4,'core'=2,'yz'=24,'far'=2,'near'=2] {'core'}, dimensions={0}, use_global_device_ids=true | all-gather | bytes 638976 | tf_op jit(solution)/shard_map/all_gather | solution.py:39
  109.0 16.3 %all-gather.3 = bf16[1568,128]{1,0:T(8,128)(2,1)S(1)} all-gather(bf16[392,128]{1,0:T(8,128)(2,1)S(1)} %constant_dynamic-update-slice_fusion.11), channel_id=5, replica_groups=mesh['hi'=4,'core'=2,'yz'=24,'far'=2,'near'=2] {'hi'}, dimensions={0}, use_global_device_ids=true | all-gather | bytes 501760 | tf_op jit(solution)/shard_map/all_gather | solution.py:44
  125.4 0.1 rsqrt_bitcast_fusion
  125.5 0.1 fusion.23
  125.6 1.9 %all_gather.39 = bf16[96,512]{1,0:T(8,128)(2,1)S(1)} all-gather(bf16[48,512]{1,0:T(8,128)(2,1)S(1)} %pad_maximum_fusion.3), channel_id=1, replica_groups=mesh['hi'=4,'core'=2,'yz'=24,'far'=2,'near'=2] {'core'}, dimensions={0}, use_global_device_ids=true | all-gather | bytes 147456 | tf_op jit(solution)/shard_map/all_gather | solution.py:56
  127.5 0.2 fusion.11
  127.7 0.2 fusion.1
  127.9 0.1 reshape.62
  128.0 19.7 %all_to_all.22 = bf16[48,2,1024]{2,1,0:T(2,128)(2,1)S(1)} all-to-all(bf16[48,2,1024]{2,1,0:T(2,128)(2,1)S(1)} %reshape.62), channel_id=1, replica_groups=mesh['hi'=4,'core'=2,'yz'=24,'far'=2,'near'=2] {'yz','near'}, dimensions={0} | all-to-all | bytes 393216 | tf_op jit(solution)/shard_map/all_to_all | solution.py:58
  147.7 0.2 convert_reduce_fusion.2
  147.9 0.6 add_convert_fusion
  (36 shorter events, 0.5 us)
Async XLA Ops:
  0.0 1.2 copy-start.1
  1.2 3.5 %copy-start.2 = (bf16[2,1024]{1,0:T(2,128)(2,1)S(1)}, bf16[2,1024]{1,0:T(2,128)(2,1)}, u32[]{:S(2)}) copy-start(bf16[2,1024]{1,0:T(2,128)(2,1)} %param.5) | copy-start | bytes 12292
  1.2 22.2 %copy-start = (bf16[256,1024]{1,0:T(8,128)(2,1)S(1)}, bf16[256,1024]{1,0:T(8,128)(2,1)}, u32[]{:S(2)}) copy-start(bf16[256,1024]{1,0:T(8,128)(2,1)} %param.9) | copy-start | bytes 1572868
  1.3 36.1 %collective-permute-start = (bf16[1024,512]{1,0:T(8,128)(2,1)S(1)}, bf16[1024,512]{1,0:T(8,128)(2,1)S(1)}, u32[]{:S(2)}, u32[]{:S(2)}) collective-permute-start(bf16[1024,512]{1,0:T(8,128)(2,1)S(1)} %constant_dynamic-update-slice_fusion), channel_id=1, source_target_pairs={{0,2},{2,0},{1,3},{3,1},{4,6},{6,4},{5,7},{7,5},{8,10},{10,8},{9,1... | collective-permute-start | bytes 3145736 | tf_op jit(solution)/shard_map/ppermute | solution.py:25
  5.5 31.3 %all-to-all-start = ((bf16[48,2,1024]{2,1,0:T(2,128)(2,1)}), bf16[48,2,1024]{2,1,0:T(2,128)(2,1)S(1)}, u32[]{:S(2)}, u32[]{:S(2)}) async-start(bf16[48,2,1024]{2,1,0:T(2,128)(2,1)} %broadcast_in_dim.10), calls=%async_computation | async-start | bytes 393216 | tf_op jit(solution)/shard_map/all_to_all | solution.py:31
  23.5 35.7 %collective-permute-start.1 = (bf16[256,1024]{1,0:T(8,128)(2,1)S(1)}, bf16[256,1024]{1,0:T(8,128)(2,1)S(1)}, u32[]{:S(2)}, u32[]{:S(2)}) collective-permute-start(bf16[256,1024]{1,0:T(8,128)(2,1)S(1)} %copy-done), channel_id=1, source_target_pairs={{0,2},{2,0},{1,3},{3,1},{4,6},{6,4},{5,7},{7,5},{8,10},{10,8},{9,1... | collective-permute-start | bytes 1572872 | tf_op jit(solution)/shard_map/ppermute | solution.py:26
  27.5 0.7 copy-start.3

commit v14 on v13

--- a/solution.py
+++ b/solution.py
@@ -5,8 +5,8 @@
 
 D = 8192
 ITERS = 2
-HI, CORE, FAR, NEAR = 4, 2, 2, 2
-RING = ("yz", "near")
+HI, CORE, LO, FAR, NEAR = 4, 2, 2, 2, 2
+RING = ("near", "z", "far")
 PAIR = ((0, 1), (1, 0))
 
 
@@ -22,8 +22,8 @@
     half = total // CORE
     core = lax.axis_index("core")
     paired = jnp.concatenate([w_gate, w_up], axis=1)
-    far = lax.ppermute(paired, "far", PAIR)
-    down_far = lax.ppermute(w_down, "far", PAIR)
+    far = lax.ppermute(paired, "lo", PAIR)
+    down_far = lax.ppermute(w_down, "lo", PAIR)
     gain = lax.optimization_barrier(jnp.broadcast_to(norm_gain[None], (8, feats)))
     mixed = tokens
     for step in range(ITERS):
@@ -44,10 +44,10 @@
         share = jnp.sum(lax.all_gather(stacked, "hi", axis=0).astype(jnp.float32), axis=0)
         all_squares = share[share.shape[0] - 1, :total]
         scale = lax.rsqrt(jnp.where(core == 0, all_squares[:half], all_squares[half:]) / D + 1e-05)[:, None]
-        side = width // FAR
+        side = width // LO
         pieces = side // 128
         sides = []
-        for block in range(FAR):
+        for block in range(LO):
             for piece in range(pieces):
                 at = (2 * pieces * block + piece) * half
                 gate = share[at : at + half] * scale
@@ -63,9 +63,9 @@
 
 
 def solution(mesh):
-    planes = mesh.shape["col"] // (FAR * NEAR)
-    fine = Mesh(mesh.devices.reshape(HI, CORE, planes, FAR, NEAR), ("hi", "core", "yz", "far", "near"))
-    row, col = ("hi", "core"), ("yz", "far", "near")
+    depth = mesh.shape["col"] // (LO * FAR * NEAR)
+    fine = Mesh(mesh.devices.reshape(HI, CORE, LO, depth, FAR, NEAR), ("hi", "core", "lo", "z", "far", "near"))
+    row, col = ("hi", "core"), ("lo", "z", "far", "near")
     return jax.shard_map(
         on_device,
         mesh=fine,

time: 149 us -> 152 us (1.020)
  blocking collectives: 107 us -> 109 us
  waiting for transfers between devices: 8.6 us -> 10.3 us
    all_to_all x1, waiting for transfers between devices: 8.6 us -> 10.3 us  [on_device(): everyone = lax.all_to_all(spread, RING, 0, 0)]
    all_to_all x2, blocking collectives: 47.3 us -> 48.9 us  [on_device(): lax.all_to_all(delta.astype(jnp.bfloat16).reshape(ring, rows, feats), RIN...]
  transfers between devices with their start and end apart: 3 -> 3, of which waited for: 1 -> 1; matrix products, arithmetic and copies ran while one was open for 2% -> 1% of each run, Pallas kernels for 0% -> 0%
where the time goes in v14:
time: 152 us; the launch traced here: 151 us
  blocking collectives  109 us (72%)
  starting transfers between devices  24.4 us (16%)
  waiting for transfers between devices  10.3 us (7%)
  local copies, waits for them, and re-layouts  3.35 us (2%)
  matrix products  2.12 us (1%)
  other arithmetic  1.83 us (1%)
    all_to_all x2, blocking collectives, on_device(): lax.all_to_all(delta.astype(jnp.bfloat16).reshape(ring, rows, feats), RIN...  48.9 us
    all_gather x2, blocking collectives, on_device(): lax.all_gather(stacked, 'hi', axis=0).astype(jnp.float32)  32.9 us
    all_to_all x1, blocking collectives, on_device(): everyone = lax.all_to_all(spread, RING, 0, 0)  19.3 us
    all_to_all x1, starting transfers between devices, on_device(): everyone = lax.all_to_all(spread, RING, 0, 0)  18.5 us
    all_to_all x1, waiting for transfers between devices, on_device(): everyone = lax.all_to_all(spread, RING, 0, 0)  10.3 us
    all_gather x2, blocking collectives, on_device(): both = lax.all_gather(packed, 'core', axis=0)  4.22 us
    all_gather x2, blocking collectives, on_device(): lax.all_gather(jnp.concatenate(sides, axis=1), 'core', axis=0, tiled=True)  3.75 us
    ppermute x1, starting transfers between devices, on_device(): far = lax.ppermute(paired, 'lo', PAIR)  3.62 us
  transfers between devices with their start and end apart: 3, of which 1 were waited for; matrix products, arithmetic and copies ran while one was open for 1% of the time, Pallas kernels for 0%

profile of v14, /device:TPU:6, one launch (start us, length us, event | category | flops | bytes accessed | tf_op | source)
XLA Modules:
  0.0 151.4 jit_solution(15125312222323573122)
XLA Ops:
  0.0 0.0 copy-start.1
  0.0 1.1 constant_dynamic-update-slice_fusion.1
  1.1 0.1 copy-done.1
  1.2 0.0 copy-start.2
  1.2 0.0 copy-start
  1.3 3.6 %collective-permute-start = (bf16[1024,512]{1,0:T(8,128)(2,1)S(1)}, bf16[1024,512]{1,0:T(8,128)(2,1)S(1)}, u32[]{:S(2)}, u32[]{:S(2)}) collective-permute-start(bf16[1024,512]{1,0:T(8,128)(2,1)S(1)} %constant_dynamic-update-slice_fusion), channel_id=1, source_target_pairs={{0,48},{48,0},{1,49},{49,1},{2,50},{50,2},{3,51},{51,3},{4,52},{52... | collective-permute-start | bytes 3145736 | tf_op jit(solution)/shard_map/ppermute | solution.py:25
  4.9 0.0 copy-done.2
  4.9 0.8 broadcast_in_dim.10
  5.7 18.5 %all-to-all-start = ((bf16[48,2,1024]{2,1,0:T(2,128)(2,1)}), bf16[48,2,1024]{2,1,0:T(2,128)(2,1)S(1)}, u32[]{:S(2)}, u32[]{:S(2)}) async-start(bf16[48,2,1024]{2,1,0:T(2,128)(2,1)} %broadcast_in_dim.10), calls=%async_computation | async-start | bytes 393216 | tf_op jit(solution)/shard_map/all_to_all | solution.py:31
  24.1 0.0 copy-done
  24.2 2.4 %collective-permute-start.1 = (bf16[256,1024]{1,0:T(8,128)(2,1)S(1)}, bf16[256,1024]{1,0:T(8,128)(2,1)S(1)}, u32[]{:S(2)}, u32[]{:S(2)}) collective-permute-start(bf16[256,1024]{1,0:T(8,128)(2,1)S(1)} %copy-done), channel_id=1, source_target_pairs={{0,48},{48,0},{1,49},{49,1},{2,50},{50,2},{3,51},{51,3},{4,52},{52... | collective-permute-start | bytes 1572872 | tf_op jit(solution)/shard_map/ppermute | solution.py:26
  26.5 0.0 copy-start.3
  26.5 0.7 copy-done.3
  27.2 10.3 %all-to-all-done = bf16[48,2,1024]{2,1,0:T(2,128)(2,1)S(1)} async-done(((bf16[48,2,1024]{2,1,0:T(2,128)(2,1)}), bf16[48,2,1024]{2,1,0:T(2,128)(2,1)S(1)}, u32[]{:S(2)}, u32[]{:S(2)}) %all-to-all-start) | async-done | bytes 196640 | tf_op jit(solution)/shard_map/all_to_all | solution.py:31
  37.5 0.1 reshape.59
  37.6 0.1 fusion.3
  37.8 0.3 convolution_convert_fusion.3
  38.1 0.0 collective-permute-done
  38.1 0.3 convolution_convert_fusion.2
  38.4 2.1 %all-gather = bf16[208,1024]{1,0:T(8,128)(2,1)S(1)} all-gather(bf16[104,1024]{1,0:T(8,128)(2,1)S(1)} %pad_maximum_fusion), channel_id=2, replica_groups=mesh['hi'=4,'core'=2,'lo'=2,'z'=12,'far'=2,'near'=2] {'core'}, dimensions={0}, use_global_device_ids=true | all-gather | bytes 638976 | tf_op jit(solution)/shard_map/all_gather | solution.py:39
  40.7 16.6 %all-gather.1 = bf16[1568,128]{1,0:T(8,128)(2,1)S(1)} all-gather(bf16[392,128]{1,0:T(8,128)(2,1)S(1)} %constant_dynamic-update-slice_fusion.2), channel_id=3, replica_groups=mesh['hi'=4,'core'=2,'lo'=2,'z'=12,'far'=2,'near'=2] {'hi'}, dimensions={0}, use_global_device_ids=true | all-gather | bytes 501760 | tf_op jit(solution)/shard_map/all_gather | solution.py:44
  57.3 0.1 rsqrt_bitcast_fusion.1
  57.4 0.1 fusion.31
  57.6 1.9 %all_gather.34 = bf16[96,512]{1,0:T(8,128)(2,1)S(1)} all-gather(bf16[48,512]{1,0:T(8,128)(2,1)S(1)} %pad_maximum_fusion.2), channel_id=1, replica_groups=mesh['hi'=4,'core'=2,'lo'=2,'z'=12,'far'=2,'near'=2] {'core'}, dimensions={0}, use_global_device_ids=true | all-gather | bytes 147456 | tf_op jit(solution)/shard_map/all_gather | solution.py:56
  59.4 0.2 fusion.14
  59.7 0.0 collective-permute-done.1
  59.7 0.2 fusion
  59.9 0.1 reshape.60
  60.0 27.9 %all_to_all.20 = bf16[48,2,1024]{2,1,0:T(2,128)(2,1)S(1)} all-to-all(bf16[48,2,1024]{2,1,0:T(2,128)(2,1)S(1)} %reshape.60), channel_id=1, replica_groups=mesh['hi'=4,'core'=2,'lo'=2,'z'=12,'far'=2,'near'=2] {'near','z','far'}, dimensions={0} | all-to-all | bytes 393216 | tf_op jit(solution)/shard_map/all_to_all | solution.py:58
  87.9 0.2 convert_reduce_fusion.3
  88.1 0.1 broadcast_in_dim.13
  88.2 19.3 %all_to_all.21 = bf16[48,2,1024]{2,1,0:T(2,128)(2,1)S(1)} all-to-all(bf16[48,2,1024]{2,1,0:T(2,128)(2,1)S(1)} %broadcast_in_dim.13), channel_id=1, replica_groups=mesh['hi'=4,'core'=2,'lo'=2,'z'=12,'far'=2,'near'=2] {'near','z','far'}, dimensions={0} | all-to-all | bytes 393216 | tf_op jit(solution)/shard_map/all_to_all | solution.py:31
  107.5 0.1 reshape.61
  107.6 0.3 convolution_convert_fusion.1
  107.9 0.1 fusion.5
  108.0 0.3 convolution_convert_fusion
  108.4 2.1 %all-gather.2 = bf16[208,1024]{1,0:T(8,128)(2,1)S(1)} all-gather(bf16[104,1024]{1,0:T(8,128)(2,1)S(1)} %pad_maximum_fusion.1), channel_id=4, replica_groups=mesh['hi'=4,'core'=2,'lo'=2,'z'=12,'far'=2,'near'=2] {'core'}, dimensions={0}, use_global_device_ids=true | all-gather | bytes 638976 | tf_op jit(solution)/shard_map/all_gather | solution.py:39
  110.7 16.3 %all-gather.3 = bf16[1568,128]{1,0:T(8,128)(2,1)S(1)} all-gather(bf16[392,128]{1,0:T(8,128)(2,1)S(1)} %constant_dynamic-update-slice_fusion.11), channel_id=5, replica_groups=mesh['hi'=4,'core'=2,'lo'=2,'z'=12,'far'=2,'near'=2] {'hi'}, dimensions={0}, use_global_device_ids=true | all-gather | bytes 501760 | tf_op jit(solution)/shard_map/all_gather | solution.py:44
  127.0 0.1 rsqrt_bitcast_fusion
  127.1 0.1 fusion.23
  127.3 1.9 %all_gather.39 = bf16[96,512]{1,0:T(8,128)(2,1)S(1)} all-gather(bf16[48,512]{1,0:T(8,128)(2,1)S(1)} %pad_maximum_fusion.3), channel_id=1, replica_groups=mesh['hi'=4,'core'=2,'lo'=2,'z'=12,'far'=2,'near'=2] {'core'}, dimensions={0}, use_global_device_ids=true | all-gather | bytes 147456 | tf_op jit(solution)/shard_map/all_gather | solution.py:56
  129.1 0.2 fusion.11
  129.4 0.2 fusion.1
  129.6 0.1 reshape.62
  129.7 20.9 %all_to_all.22 = bf16[48,2,1024]{2,1,0:T(2,128)(2,1)S(1)} all-to-all(bf16[48,2,1024]{2,1,0:T(2,128)(2,1)S(1)} %reshape.62), channel_id=1, replica_groups=mesh['hi'=4,'core'=2,'lo'=2,'z'=12,'far'=2,'near'=2] {'near','z','far'}, dimensions={0} | all-to-all | bytes 393216 | tf_op jit(solution)/shard_map/all_to_all | solution.py:58
  150.6 0.2 convert_reduce_fusion.2
  150.8 0.6 add_convert_fusion
  (36 shorter events, 0.5 us)
Async XLA Ops:
  0.0 1.2 copy-start.1
  1.2 3.7 %copy-start.2 = (bf16[2,1024]{1,0:T(2,128)(2,1)S(1)}, bf16[2,1024]{1,0:T(2,128)(2,1)}, u32[]{:S(2)}) copy-start(bf16[2,1024]{1,0:T(2,128)(2,1)} %param.5) | copy-start | bytes 12292
  1.2 22.9 %copy-start = (bf16[256,1024]{1,0:T(8,128)(2,1)S(1)}, bf16[256,1024]{1,0:T(8,128)(2,1)}, u32[]{:S(2)}) copy-start(bf16[256,1024]{1,0:T(8,128)(2,1)} %param.9) | copy-start | bytes 1572868
  1.3 36.8 %collective-permute-start = (bf16[1024,512]{1,0:T(8,128)(2,1)S(1)}, bf16[1024,512]{1,0:T(8,128)(2,1)S(1)}, u32[]{:S(2)}, u32[]{:S(2)}) collective-permute-start(bf16[1024,512]{1,0:T(8,128)(2,1)S(1)} %constant_dynamic-update-slice_fusion), channel_id=1, source_target_pairs={{0,48},{48,0},{1,49},{49,1},{2,50},{50,2},{3,51},{51,3},{4,52},{52... | collective-permute-start | bytes 3145736 | tf_op jit(solution)/shard_map/ppermute | solution.py:25
  5.7 31.9 %all-to-all-start = ((bf16[48,2,1024]{2,1,0:T(2,128)(2,1)}), bf16[48,2,1024]{2,1,0:T(2,128)(2,1)S(1)}, u32[]{:S(2)}, u32[]{:S(2)}) async-start(bf16[48,2,1024]{2,1,0:T(2,128)(2,1)} %broadcast_in_dim.10), calls=%async_computation | async-start | bytes 393216 | tf_op jit(solution)/shard_map/all_to_all | solution.py:31
  24.2 35.5 %collective-permute-start.1 = (bf16[256,1024]{1,0:T(8,128)(2,1)S(1)}, bf16[256,1024]{1,0:T(8,128)(2,1)S(1)}, u32[]{:S(2)}, u32[]{:S(2)}) collective-permute-start(bf16[256,1024]{1,0:T(8,128)(2,1)S(1)} %copy-done), channel_id=1, source_target_pairs={{0,48},{48,0},{1,49},{49,1},{2,50},{50,2},{3,51},{51,3},{4,52},{52... | collective-permute-start | bytes 1572872 | tf_op jit(solution)/shard_map/ppermute | solution.py:26
  26.5 0.7 copy-start.3
